TPU v7x, 512 devices: a whole 4x8x8 slice. The times are simulated.
512 devices in a mesh: lon: 32 (over x, y), lat: 4 (over z_lo, core), lev: 4 (over z_hi).
Axes of the slice: x: 4, y: 8, z: 8 (z_hi: 4, z_lo: 2; z = z_hi * 2 + z_lo), core: 2. Of those that a mesh axis runs over, the one named last changes fastest.
Arguments:
- adjoint_field: float32 [12, 12, 128, 4096], P(None, 'lev', 'lat', 'lon'), may hold values from -6 to 6
- east_courant: float32 [12, 128, 4096], P('lev', 'lat', 'lon'), may hold values from -0.2 to 0.2
- north_courant: float32 [12, 128, 4096], P('lev', 'lat', 'lon'), may hold values from -0.2 to 0.2
- pole_courant: float32 [12, 4096], P('lev', 'lon'), may hold values from -0.2 to 0.2
- mix_fraction: float32 [12, 128, 4096], P('lev', 'lat', 'lon'), may hold values from 0.05 to 0.6
- detrain_share: float32 [12, 128, 4096], P('lev', 'lat', 'lon'), may hold values from 0.1 to 3
- sounding_owner: int32 [2, 32768, 1], P(None, ('lon', 'lat')), may hold values from 0 to 127; in each aligned block of 256 rows (0 to 255, 256 to 511, ..., all dimensions but the last counted through in order) at most 4 rows name the same one
- sounding_cell: int32 [2, 32768], P(None, ('lon', 'lat')), may hold values from 0 to 4095
- sounding_count: int32 [2, 128], P(None, ('lon', 'lat')), may hold values from 1 to 256, 20480 in all within a row
- sounding_forcing: float32 [2, 12, 32768], P(None, 'lev', ('lon', 'lat')), may hold values from -6 to 6
Outputs:
- earlier_adjoint: float32 [12, 12, 128, 4096], P(None, 'lev', 'lat', 'lon')
Inputs may be any that keep to these rules, and one draw needn't show every extreme that they name: `sounding_owner`: in each aligned block of 256 slots of one step (the slots of one device) no owner is named more than 4 times, a bound that some block reaches. `sounding_count`: each step's counts sum to 20480; at each step some device has exactly 256.
All inputs are finite; a program needn't handle non-finite values.
Results may differ from a plain program's by a relative error of at most 0.0001.
Values sent between devices are 32-bit elements; how exact they have to be, the bound alone decides.
A program may use at most 128 MiB of HBM per device.

v0:
```python
import jax
import jax.numpy as jnp
from jax import lax
from jax.sharding import PartitionSpec as P


def from_behind(value, axis, steps):
    count = lax.axis_size(axis)
    pairs = [(source, (source + steps) % count) for source in range(count)]
    return lax.ppermute(value, axis, pairs)


def from_behind_2(block, axis, distance):
    devices = range(lax.axis_size(axis))
    route = [(i - distance, i) for i in devices if i - distance in devices]
    return lax.ppermute(block, axis, route)


def extended(x, sides, width, wrap):
    for axis, dim in sides:
        size, length = (lax.axis_size(axis), x.shape[dim])
        up = [(i, (i + 1) % size) for i in range(size if wrap else size - 1)]
        down = [(j, i) for i, j in up]
        last = lax.slice_in_dim(x, length - width, length, axis=dim)
        initial = lax.slice_in_dim(x, 0, width, axis=dim)
        before = lax.ppermute(last, axis, up)
        after = lax.ppermute(initial, axis, down)
        x = jnp.concatenate([before, x, after], axis=dim)
    return x


def mix_sum(partial_sum):
    return lax.psum(partial_sum, "lev")


def on_device(
    adjoint_field,
    east_courant,
    north_courant,
    pole_courant,
    mix_fraction,
    detrain_share,
    sounding_owner,
    sounding_cell,
    sounding_count,
    sounding_forcing,
):
    lon_count = lax.axis_size("lon")
    lat_count = lax.axis_size("lat")
    lat_place = lax.axis_index("lat")
    owner_self = lax.axis_index("lon") * lat_count + lat_place
    tracers, lev_dev, lat_rows, lon_cols = adjoint_field.shape
    step_count = sounding_forcing.shape[0]
    slot_count = sounding_forcing.shape[2]
    grid_cells = lat_rows * lon_cols
    live_slots = jnp.arange(slot_count, dtype=jnp.int32)[None, :] < sounding_count
    values = jnp.where(live_slots[:, None, :], sounding_forcing, 0.0)
    owner_ids = sounding_owner[:, :, 0]
    step_ids = jnp.arange(step_count, dtype=jnp.int32)[:, None]
    index_pair = jnp.stack([owner_ids, sounding_cell], axis=1)
    all_values, all_pairs = (
        lax.all_gather(values, ("lon", "lat"), axis=2, tiled=True),
        lax.all_gather(index_pair, ("lon", "lat"), axis=2, tiled=True),
    )
    kept_values = jnp.where((all_pairs[:, 0, :] == owner_self)[:, None, :], all_values, 0.0)
    target_cells = all_pairs[:, 1, :]
    forcing_grid = (
        jnp.zeros((step_count, lev_dev, grid_cells), jnp.float32)
        .at[step_ids, :, target_cells]
        .add(jnp.swapaxes(kept_values, 1, 2))
    )
    forcing_grid = forcing_grid.reshape(step_count, lev_dev, lat_rows, lon_cols)
    west_column = from_behind(east_courant[:, :, -1:], "lon", 1)
    west_wind = jnp.concatenate([west_column, east_courant[:, :, :-1]], axis=2)
    south_row = from_behind_2(north_courant[:, -1:, :], "lat", 1)
    south_wind = jnp.concatenate([south_row, north_courant[:, :-1, :]], axis=1)
    pole_pair = jnp.stack([north_courant[:, -1, :], pole_courant], axis=0)
    partner_winds = from_behind(pole_pair, "lon", lon_count // 2)
    row_index = jnp.arange(lat_rows, dtype=jnp.int32)[None, :, None]
    at_top = jnp.logical_and(lat_place == lat_count - 1, row_index == lat_rows - 1)
    at_bottom = jnp.logical_and(lat_place == 0, row_index == 0)
    upwind_east = jnp.maximum(east_courant, 0.0)
    upwind_west = -jnp.minimum(west_wind, 0.0)
    upwind_north = jnp.maximum(north_courant, 0.0) + jnp.where(
        at_top, -jnp.minimum(partner_winds[0], 0.0)[:, None, :], 0.0
    )
    upwind_south = jnp.where(
        at_bottom,
        (jnp.maximum(pole_courant, 0.0) - jnp.minimum(partner_winds[1], 0.0))[:, None, :],
        -jnp.minimum(south_wind, 0.0),
    )
    total_detrain = lax.psum(jnp.sum(detrain_share, axis=0), "lev")
    adjoint = adjoint_field
    for position in range(step_count):
        step_now = step_count - 1 - position
        adjoint = adjoint + forcing_grid[step_now][None]
        partial_sum = jnp.sum(detrain_share[None] * adjoint, axis=1)
        column_sum = mix_sum(partial_sum)
        adjoint = (1.0 - mix_fraction)[None] * adjoint + mix_fraction[None] * (
            column_sum / total_detrain
        )[:, None]
        across = extended(adjoint, (("lon", 3),), 1, True)
        east_side = across[:, :, :, 2:]
        west_side = across[:, :, :, :-2]
        upright = extended(adjoint, (("lat", 2),), 1, False)
        north_side = upright[:, :, 2:, :]
        south_side = upright[:, :, :-2, :]
        edge_row = jnp.where(lat_place == 0, adjoint[:, :, :1, :], adjoint[:, :, -1:, :])
        partner_row = from_behind(edge_row, "lon", lon_count // 2)
        north_side = jnp.where(at_top, partner_row, north_side)
        south_side = jnp.where(at_bottom, partner_row, south_side)
        adjoint = (
            adjoint
            + upwind_east * (east_side - adjoint)
            + upwind_west * (west_side - adjoint)
            + upwind_north * (north_side - adjoint)
            + upwind_south * (south_side - adjoint)
        )
    return adjoint


def solution(mesh):
    return jax.shard_map(
        on_device,
        mesh=mesh,
        in_specs=(
            P(None, "lev", "lat", "lon"),
            P("lev", "lat", "lon"),
            P("lev", "lat", "lon"),
            P("lev", "lon"),
            P("lev", "lat", "lon"),
            P("lev", "lat", "lon"),
            P(None, ("lon", "lat"), None),
            P(None, ("lon", "lat")),
            P(None, ("lon", "lat")),
            P(None, "lev", ("lon", "lat")),
        ),
        out_specs=P(None, "lev", "lat", "lon"),
        check_vma=False,
    )
```

profile of v0, /device:TPU:1, one launch (start us, length us, event | category | flops | bytes accessed | tf_op | source)
XLA Modules:
  0.0 865.7 jit_solution(10978872272690706526)
XLA Ops:
  7.9 160.9 %all_gather.6 = s32[2,2,32768]{2,0,1:T(2,128)S(1)} all-gather(s32[2,2,256]{2,0,1:T(2,128)S(1)} %pad_add_fusion.1), channel_id=1, replica_groups=mesh['lon'=32,'lat'=4,'lev'=4] {'lon','lat'}, dimensions={2}, use_global_device_ids=true | all-gather | bytes 528384 | tf_op jit(solution)/shard_map/all_gather | solution.py:63
  169.1 1.1 multiply_reduce_fusion.1
  170.3 1.4 and_reduce_fusion
  172.1 153.2 %all_gather.7 = f32[2,3,32768]{2,0,1:T(2,128)S(1)} all-gather(f32[2,3,256]{2,0,1:T(2,128)S(1)} %broadcast_select_fusion.2), channel_id=1, replica_groups=mesh['lon'=32,'lat'=4,'lev'=4] {'lon','lat'}, dimensions={2}, use_global_device_ids=true | all-gather | bytes 792576 | tf_op jit(solution)/shard_map/all_gather | solution.py:62
  325.8 16.6 %copy.38 = f32[2,32768,3]{2,1,0:T(8,128)} copy(f32[2,32768,3]{1,0,2:T(2,128)S(1)} %select_bitcast_fusion) | data formatting | bytes 1572864 | tf_op jit(solution)/shard_map/transpose | solution.py:70
  342.3 349.8 %scatter_custom_fusion = f32[3,8192]{0,1:T(8,128)} fusion(s32[65536]{0:T(1024)S(1)} %bitcast.41, f32[65536,3]{1,0:T(8,128)} %bitcast.36, f32[]{:T(128)} %constant.12.clone.1), kind=kCustom, calls=%fused_computation.1 | custom fusion | flops 196608 | bytes 98816
  692.1 3.9 fusion.43
  696.0 2.2 copy.24
  698.3 1.1 fusion.34
  699.5 3.4 collective-permute-start.6
  702.9 1.9 collective-permute-start.3
  704.9 1.9 collective-permute-start.1
  706.9 21.0 %psum.22 = f32[32,128]{1,0:T(8,128)S(1)} all-reduce(f32[32,128]{1,0:T(8,128)S(1)} %reduce_sum.28), channel_id=1, replica_groups=mesh['lon'=32,'lat'=4,'lev'=4] {'lev'}, use_global_device_ids=true, to_apply=%region_4.5 | all-reduce | flops 4096 | bytes 32768 | tf_op jit(solution)/shard_map/psum | solution.py:92
  728.7 21.9 %all-reduce.3.cloned.1.call-done = f32[12,32,128]{2,0,1:T(8,128)} async-done(((f32[12,32,128]{2,0,1:T(8,128)}), f32[12,32,128]{2,0,1:T(8,128)}) %all-reduce.3.cloned.1.call-update) | async-done | bytes 196624 | tf_op jit(solution)/shard_map/psum | solution.py:33
  750.6 1.0 broadcast_divide_fusion.1
  752.4 4.6 collective-permute-start.4
  757.0 4.9 collective-permute-start.5
  761.9 2.3 collective-permute-start.7
  764.5 5.2 collective-permute-start
  770.1 1.9 collective-permute-start.2
  772.5 5.4 collective-permute-done.2
  779.6 2.3 multiply_reduce_fusion
  781.9 47.8 %all-reduce.5.cloned.1.call-done = f32[12,32,128]{2,0,1:T(8,128)} async-done(((f32[12,32,128]{2,0,1:T(8,128)}), f32[12,32,128]{2,0,1:T(8,128)}) %all-reduce.5.cloned.1.call-update) | async-done | bytes 196624 | tf_op jit(solution)/shard_map/psum | solution.py:33
  829.8 1.0 broadcast_divide_fusion
  830.9 4.6 collective-permute-start.10
  835.5 4.9 collective-permute-start.11
  840.5 2.3 collective-permute-start.12
  843.4 5.1 collective-permute-start.8
  848.8 1.9 collective-permute-start.9
  851.1 5.5 collective-permute-done.9
  857.0 0.8 fusion.5
  857.8 1.0 copy.37
  (84 shorter events, 9.0 us)
Async XLA Ops:
  6.5 165.5 %copy-start.14 = (s32[2,1]{0,1:T(1,128)S(1)}, s32[2,1]{0,1:T(1,128)}, u32[]{:S(2)}) copy-start(s32[2,1]{0,1:T(1,128)} %param.18) | copy-start | bytes 28
  6.5 165.6 %copy-start.13 = (f32[2,3,256]{2,0,1:T(2,128)S(1)}, f32[2,3,256]{2,0,1:T(2,128)}, u32[]{:S(2)}) copy-start(f32[2,3,256]{2,0,1:T(2,128)} %param.19) | copy-start | bytes 18436
  6.5 744.1 %all-reduce.3.cloned.1.call-start = ((), (), s32[]{:S(2)}) async-start(), calls=%async_computation | async-start | bytes 524288 | tf_op jit(solution)/shard_map/psum | solution.py:33
  692.1 6.1 copy-start
  692.1 6.1 copy-start.1
  692.1 7.3 copy-start.4
  692.1 10.7 %copy-start.12 = (f32[3,128]{1,0:T(4,128)S(1)}, f32[3,128]{1,0:T(4,128)}, u32[]{:S(2)}) copy-start(f32[3,128]{1,0:T(4,128)} %param.13) | copy-start | bytes 4612
  692.1 12.7 %copy-start.2 = (f32[3,32,128]{2,1,0:T(8,128)S(1)}, f32[3,32,128]{2,1,0:T(8,128)}, u32[]{:S(2)}) copy-start(f32[3,32,128]{2,1,0:T(8,128)} %param.11) | copy-start | bytes 147460
  692.1 14.7 %copy-start.3 = (f32[3,32,128]{2,1,0:T(8,128)S(1)}, f32[3,32,128]{2,1,0:T(8,128)}, u32[]{:S(2)}) copy-start(f32[3,32,128]{2,1,0:T(8,128)} %param.14) | copy-start | bytes 147460
  699.4 130.4 %all-reduce.5.cloned.1.call-start = ((), (), s32[]{:S(2)}) async-start(), calls=%async_computation.1 | async-start | bytes 524288 | tf_op jit(solution)/shard_map/psum | solution.py:33
  699.5 29.1 %collective-permute-start.6 = (f32[3,1,128]{2,0,1:T(4,128)S(1)}, f32[3,1,128]{2,0,1:T(4,128)S(1)}, u32[]{:S(2)}, u32[]{:S(2)}) collective-permute-start(f32[3,1,128]{2,0,1:T(4,128)S(1)} %copy.55), channel_id=1, source_target_pairs={{0,4},{4,8},{8,12},{1,5},{5,9},{9,13},{2,6},{6,10},{10,14},{3,7},{... | collective-permute-start | bytes 4616 | tf_op jit(solution)/shard_map/ppermute | solution.py:16
  702.9 25.8 %collective-permute-start.3 = (f32[2,3,128]{2,1,0:T(4,128)S(1)}, f32[2,3,128]{2,1,0:T(4,128)S(1)}, u32[]{:S(2)}, u32[]{:S(2)}) collective-permute-start(f32[2,3,128]{2,1,0:T(4,128)S(1)} %pad_maximum_fusion.8), channel_id=1, source_target_pairs={{0,256},{16,272},{32,288},{48,304},{64,320},{80,336},{96,352},{112... | collective-permute-start | bytes 9224 | tf_op jit(solution)/shard_map/ppermute | solution.py:10
  704.9 23.6 %collective-permute-start.1 = (f32[3,32,1]{2,1,0:T(8,128)S(1)}, f32[3,32,1]{2,1,0:T(8,128)S(1)}, u32[]{:S(2)}, u32[]{:S(2)}) collective-permute-start(f32[3,32,1]{2,1,0:T(8,128)S(1)} %slice.98), channel_id=1, source_target_pairs={{0,16},{16,32},{32,48},{48,64},{64,80},{80,96},{96,112},{112,128},... | collective-permute-start | bytes 1160 | tf_op jit(solution)/shard_map/ppermute | solution.py:10
  706.9 57.7 %copy-start.10 = (pred[32]{0:T(512)(128)(4,1)}, pred[32]{0:T(512)(128)(4,1)S(1)}, u32[]{:S(2)}) copy-start(pred[32]{0:T(512)(128)(4,1)S(1)} %get-tuple-element.22) | copy-start | bytes 100
  706.9 65.1 %copy-start.8 = (pred[32]{0:T(512)(128)(4,1)}, pred[32]{0:T(512)(128)(4,1)S(1)}, u32[]{:S(2)}) copy-start(pred[32]{0:T(512)(128)(4,1)S(1)} %get-tuple-element.21) | copy-start | bytes 100
  752.4 26.0 %collective-permute-start.4 = (f32[12,3,1,128]{3,0,2,1:T(8,128)S(1)}, f32[12,3,1,128]{3,0,2,1:T(8,128)S(1)}, u32[]{:S(2)}, u32[]{:S(2)}) collective-permute-start(f32[12,3,1,128]{3,0,2,1:T(8,128)S(1)} %get-tuple-element.16), channel_id=1, source_target_pairs={{0,256},{16,272},{32,288},{48,304},{64,320},{80,336},{96,352},{112... | collective-permute-start | bytes 55304 | tf_op jit(solution)/shard_map/ppermute | solution.py:10
  757.0 21.4 %collective-permute-start.5 = (f32[12,3,1,128]{3,0,2,1:T(8,128)S(1)}, f32[12,3,1,128]{3,0,2,1:T(8,128)S(1)}, u32[]{:S(2)}, u32[]{:S(2)}) collective-permute-start(f32[12,3,1,128]{3,0,2,1:T(8,128)S(1)} %get-tuple-element.18), channel_id=1, source_target_pairs={{4,0},{8,4},{12,8},{5,1},{9,5},{13,9},{6,2},{10,6},{14,10},{7,3},{... | collective-permute-start | bytes 55304 | tf_op jit(solution)/shard_map/ppermute | solution.py:27
  761.9 16.5 %collective-permute-start.7 = (f32[12,3,1,128]{3,0,2,1:T(8,128)S(1)}, f32[12,3,1,128]{3,0,2,1:T(8,128)S(1)}, u32[]{:S(2)}, u32[]{:S(2)}) collective-permute-start(f32[12,3,1,128]{3,0,2,1:T(8,128)S(1)} %get-tuple-element.17), channel_id=1, source_target_pairs={{0,4},{4,8},{8,12},{1,5},{5,9},{9,13},{2,6},{6,10},{10,14},{3,7},{... | collective-permute-start | bytes 55304 | tf_op jit(solution)/shard_map/ppermute | solution.py:26
  764.5 7.6 collective-permute-start
  770.1 7.8 collective-permute-start.2
  778.4 0.6 copy-start.5
  778.4 0.6 copy-start.6
  779.0 0.6 copy-start.7
  830.8 26.3 %copy-start.9 = (pred[32]{0:T(512)(128)(4,1)S(1)}, pred[32]{0:T(512)(128)(4,1)}, u32[]{:S(2)}) copy-start(pred[32]{0:T(512)(128)(4,1)} %copy-done.8) | copy-start | bytes 100
  830.8 26.3 %copy-start.11 = (pred[32]{0:T(512)(128)(4,1)S(1)}, pred[32]{0:T(512)(128)(4,1)}, u32[]{:S(2)}) copy-start(pred[32]{0:T(512)(128)(4,1)} %copy-done.10) | copy-start | bytes 100
  830.9 26.1 %collective-permute-start.10 = (f32[12,3,1,128]{3,0,2,1:T(8,128)S(1)}, f32[12,3,1,128]{3,0,2,1:T(8,128)S(1)}, u32[]{:S(2)}, u32[]{:S(2)}) collective-permute-start(f32[12,3,1,128]{3,0,2,1:T(8,128)S(1)} %get-tuple-element.9), channel_id=1, source_target_pairs={{0,256},{16,272},{32,288},{48,304},{64,320},{80,336},{96,352},{112... | collective-permute-start | bytes 55304 | tf_op jit(solution)/shard_map/ppermute | solution.py:10
  835.5 21.5 %collective-permute-start.11 = (f32[12,3,1,128]{3,0,2,1:T(8,128)S(1)}, f32[12,3,1,128]{3,0,2,1:T(8,128)S(1)}, u32[]{:S(2)}, u32[]{:S(2)}) collective-permute-start(f32[12,3,1,128]{3,0,2,1:T(8,128)S(1)} %get-tuple-element.11), channel_id=1, source_target_pairs={{4,0},{8,4},{12,8},{5,1},{9,5},{13,9},{6,2},{10,6},{14,10},{7,3},{... | collective-permute-start | bytes 55304 | tf_op jit(solution)/shard_map/ppermute | solution.py:27
  840.5 16.6 %collective-permute-start.12 = (f32[12,3,1,128]{3,0,2,1:T(8,128)S(1)}, f32[12,3,1,128]{3,0,2,1:T(8,128)S(1)}, u32[]{:S(2)}, u32[]{:S(2)}) collective-permute-start(f32[12,3,1,128]{3,0,2,1:T(8,128)S(1)} %get-tuple-element.10), channel_id=1, source_target_pairs={{0,4},{4,8},{8,12},{1,5},{5,9},{9,13},{2,6},{6,10},{10,14},{3,7},{... | collective-permute-start | bytes 55304 | tf_op jit(solution)/shard_map/ppermute | solution.py:26
  843.4 7.3 collective-permute-start.8
  848.8 7.8 collective-permute-start.9
Sparse Core Ops, SparseCore 0:
  699.5 51.0 all-reduce.2
  782.1 47.6 all-reduce.4
where the time goes:
time: 866 us
  other arithmetic  361 us (42%)
  blocking collectives  335 us (39%)
  waiting for transfers between devices  80.7 us (9%)
  starting transfers between devices  44.9 us (5%)
  local copies, waits for them, and re-layouts  30 us (3%)
  between operations  13.9 us (2%)
    unnamed x4, other arithmetic  352 us
    all_gather x1, blocking collectives, on_device(): lax.all_gather(index_pair, ('lon', 'lat'), axis=2, tiled=True)  161 us
    all_gather x1, blocking collectives, on_device(): lax.all_gather(values, ('lon', 'lat'), axis=2, tiled=True)  153 us
    psum x2, waiting for transfers between devices, mix_sum(): return lax.psum(partial_sum, 'lev')  69.7 us
    psum x1, blocking collectives, on_device(): total_detrain = lax.psum(jnp.sum(detrain_share, axis=0), 'lev')  21 us
    ppermute x4, starting transfers between devices, extended(): after = lax.ppermute(initial, axis, down)  20.2 us
  transfers between devices with their start and end apart: 15, of which 4 were waited for; matrix products, arithmetic and copies ran while one was open for 0% of the time, Pallas kernels for 0%

commit v1 on v0

--- a/solution.py
+++ b/solution.py
@@ -53,21 +53,35 @@
     step_count = sounding_forcing.shape[0]
     slot_count = sounding_forcing.shape[2]
     grid_cells = lat_rows * lon_cols
+    owner_count = lon_count * lat_count
+    cap = 4
     live_slots = jnp.arange(slot_count, dtype=jnp.int32)[None, :] < sounding_count
     values = jnp.where(live_slots[:, None, :], sounding_forcing, 0.0)
     owner_ids = sounding_owner[:, :, 0]
-    step_ids = jnp.arange(step_count, dtype=jnp.int32)[:, None]
-    index_pair = jnp.stack([owner_ids, sounding_cell], axis=1)
-    all_values, all_pairs = (
-        lax.all_gather(values, ("lon", "lat"), axis=2, tiled=True),
-        lax.all_gather(index_pair, ("lon", "lat"), axis=2, tiled=True),
+    slot_iota = jnp.arange(slot_count, dtype=jnp.int32)
+    earlier = slot_iota[None, :, None] < slot_iota[None, None, :]
+    same_owner = owner_ids[:, :, None] == owner_ids[:, None, :]
+    rank = jnp.sum(jnp.logical_and(earlier, same_owner), axis=1, dtype=jnp.int32)
+    position = owner_ids * cap + rank
+    bucket_iota = jnp.arange(owner_count * cap, dtype=jnp.int32)
+    chosen = position[:, :, None] == bucket_iota[None, None, :]
+    bucket_values = jnp.sum(
+        jnp.where(chosen[:, None, :, :], values[:, :, :, None], 0.0), axis=2
     )
-    kept_values = jnp.where((all_pairs[:, 0, :] == owner_self)[:, None, :], all_values, 0.0)
-    target_cells = all_pairs[:, 1, :]
-    forcing_grid = (
-        jnp.zeros((step_count, lev_dev, grid_cells), jnp.float32)
-        .at[step_ids, :, target_cells]
-        .add(jnp.swapaxes(kept_values, 1, 2))
+    bucket_cell = jnp.max(
+        jnp.where(chosen, sounding_cell[:, :, None] + 1, 0), axis=1
+    ).astype(jnp.float32) - 1.0
+    packed = jnp.concatenate([bucket_values, bucket_cell[:, None, :]], axis=1)
+    packed = packed.reshape(step_count, lev_dev + 1, owner_count, cap)
+    packed = jnp.transpose(packed, (2, 0, 1, 3))
+    arrived = lax.all_to_all(packed, ("lon", "lat"), 0, 0, tiled=True)
+    arrived = jnp.transpose(arrived, (1, 2, 0, 3)).reshape(
+        step_count, lev_dev + 1, owner_count * cap
+    )
+    cell_iota = jnp.arange(grid_cells, dtype=jnp.int32).astype(jnp.float32)
+    hit = (arrived[:, lev_dev, :, None] == cell_iota[None, None, :]).astype(jnp.float32)
+    forcing_grid = jnp.einsum(
+        "tke,tec->tkc", arrived[:, :lev_dev, :], hit, precision=lax.Precision.HIGHEST
     )
     forcing_grid = forcing_grid.reshape(step_count, lev_dev, lat_rows, lon_cols)
     west_column = from_behind(east_courant[:, :, -1:], "lon", 1)

time: 866 us -> 239 us (0.28)
  other arithmetic: 361 us -> 12.2 us
  blocking collectives: 335 us -> 21.4 us
  waiting for transfers between devices: 80.7 us -> 115 us
  local copies, waits for them, and re-layouts: 30 us -> 9.05 us
  starting transfers between devices: 44.9 us -> 61.3 us
    unnamed x4 -> x0, other arithmetic: 352 us -> none
    all_gather x2 -> x0, blocking collectives: 314 us -> none  [the longest x1 161 us: on_device(): lax.all_gather(index_pair, ('lon', 'lat'), axis=2, tiled=True)]
    psum x2, waiting for transfers between devices: 69.7 us -> 109 us  [mix_sum(): return lax.psum(partial_sum, 'lev')]
    transpose x1 -> x2, local copies, waits for them, and re-layouts: 16.6 us -> 1.3 us  [the longest x1 1.2 us: on_device(): packed = jnp.transpose(packed, (2, 0, 1, 3))]
    all_to_all x0 -> x1, starting transfers between devices: none -> 8.66 us  [on_device(): arrived = lax.all_to_all(packed, ('lon', 'lat'), 0, 0, tiled=True)]
  transfers between devices with their start and end apart: 15 -> 16, of which waited for: 4 -> 4; matrix products, arithmetic and copies ran while one was open for 0% -> 5% of each run, Pallas kernels for 0% -> 0%
where the time goes in v1:
time: 239 us; the launch traced here: 238 us
  waiting for transfers between devices  115 us (48%)
  starting transfers between devices  61.3 us (26%)
  blocking collectives  21.4 us (9%)
  between operations  14 us (6%)
  other arithmetic  12.2 us (5%)
  local copies, waits for them, and re-layouts  9.05 us (4%)
  matrix products  4.78 us (2%)
    psum x2, waiting for transfers between devices, mix_sum(): return lax.psum(partial_sum, 'lev')  109 us
    psum x1, blocking collectives, on_device(): total_detrain = lax.psum(jnp.sum(detrain_share, axis=0), 'lev')  21.4 us
    ppermute x4, starting transfers between devices, from_behind(): return lax.ppermute(value, axis, pairs)  17 us
    ppermute x4, starting transfers between devices, extended(): before = lax.ppermute(last, axis, up)  15.6 us
    ppermute x4, starting transfers between devices, extended(): after = lax.ppermute(initial, axis, down)  14.6 us
    all_to_all x1, starting transfers between devices, on_device(): arrived = lax.all_to_all(packed, ('lon', 'lat'), 0, 0, tiled=True)  8.66 us
    ppermute x4, waiting for transfers between devices, extended(): before = lax.ppermute(last, axis, up)  5.48 us
    ppermute x1, starting transfers between devices, from_behind_2(): return lax.ppermute(block, axis, route)  5.38 us
  transfers between devices with their start and end apart: 16, of which 4 were waited for; matrix products, arithmetic and copies ran while one was open for 5% of the time, Pallas kernels for 0%

profile of v1, /device:TPU:1, one launch (start us, length us, event | category | flops | bytes accessed | tf_op | source)
XLA Modules:
  0.0 237.8 jit_solution(9995370526051326967)
XLA Ops:
  6.5 0.7 slice.102
  7.2 5.4 %collective-permute-start.6 = (f32[3,1,128]{2,0,1:T(4,128)S(1)}, f32[3,1,128]{2,0,1:T(4,128)S(1)}, u32[]{:S(2)}, u32[]{:S(2)}) collective-permute-start(f32[3,1,128]{2,0,1:T(4,128)S(1)} %copy.79), channel_id=1, source_target_pairs={{0,4},{4,8},{8,12},{1,5},{5,9},{9,13},{2,6},{6,10},{10,14},{3,7},{... | collective-permute-start | bytes 4616 | tf_op jit(solution)/shard_map/ppermute | solution.py:16
  13.3 4.6 %collective-permute-start.3 = (f32[2,3,128]{2,1,0:T(4,128)S(1)}, f32[2,3,128]{2,1,0:T(4,128)S(1)}, u32[]{:S(2)}, u32[]{:S(2)}) collective-permute-start(f32[2,3,128]{2,1,0:T(4,128)S(1)} %pad_maximum_fusion.8), channel_id=1, source_target_pairs={{0,256},{16,272},{32,288},{48,304},{64,320},{80,336},{96,352},{112... | collective-permute-start | bytes 9224 | tf_op jit(solution)/shard_map/ppermute | solution.py:10
  18.0 0.9 slice.98
  18.8 3.2 %collective-permute-start.1 = (f32[3,32,1]{2,1,0:T(8,128)S(1)}, f32[3,32,1]{2,1,0:T(8,128)S(1)}, u32[]{:S(2)}, u32[]{:S(2)}) collective-permute-start(f32[3,32,1]{2,1,0:T(8,128)S(1)} %slice.98), channel_id=1, source_target_pairs={{0,16},{16,32},{32,48},{48,64},{64,80},{80,96},{96,112},{112,128},... | collective-permute-start | bytes 1160 | tf_op jit(solution)/shard_map/ppermute | solution.py:10
  22.1 0.7 iota_compare_fusion.2
  24.2 0.7 broadcast_select_fusion.2
  25.0 0.7 fusion.45
  27.2 1.2 copy.40
  28.4 8.7 %all-to-all-start = ((f32[128,2,4,4]{3,1,2,0:T(2,128)}), f32[128,2,4,4]{3,1,2,0:T(2,128)S(1)}, u32[]{:S(2)}, u32[]{:S(2)}) async-start(f32[128,2,4,4]{3,1,2,0:T(2,128)} %copy.40), calls=%async_computation | async-start | bytes 1048576 | tf_op jit(solution)/shard_map/all_to_all | solution.py:77
  37.2 21.4 %psum.22 = f32[32,128]{1,0:T(8,128)S(1)} all-reduce(f32[32,128]{1,0:T(8,128)S(1)} %reduce_sum.51), channel_id=1, replica_groups=mesh['lon'=32,'lat'=4,'lev'=4] {'lev'}, use_global_device_ids=true, to_apply=%region_6.7 | all-reduce | flops 4096 | bytes 32768 | tf_op jit(solution)/shard_map/psum | solution.py:106
  59.3 4.8 %fusion = f32[2,3,4096]{2,1,0:T(4,128)S(1)} fusion(f32[4096]{0:T(1024)S(1)} %iota_convert_fusion, f32[2,512]{1,0:T(2,128)S(1)} %bitcast.56, f32[2,4,512]{2,1,0:T(4,128)S(1)} %reshape.146), kind=kOutput, calls=%fused_computation | convolution fusion | flops 155189248 | bytes 135168 | tf_op jit(solution)/shard_map/tke,tec->tkc/dot_general | solution.py:83
  64.2 1.1 fusion.36
  65.4 56.0 %all-reduce.3.cloned.1.call-done = f32[12,32,128]{2,0,1:T(8,128)} async-done(((f32[12,32,128]{2,0,1:T(8,128)}), f32[12,32,128]{2,0,1:T(8,128)}) %all-reduce.3.cloned.1.call-update) | async-done | bytes 196624 | tf_op jit(solution)/shard_map/psum | solution.py:33
  121.4 1.0 broadcast_divide_fusion.1
  123.8 4.6 %collective-permute-start.4 = (f32[12,3,1,128]{3,0,2,1:T(8,128)}, f32[12,3,1,128]{3,0,2,1:T(8,128)}, u32[]{:S(2)}, u32[]{:S(2)}) collective-permute-start(f32[12,3,1,128]{3,0,2,1:T(8,128)} %get-tuple-element.14), channel_id=1, source_target_pairs={{0,256},{16,272},{32,288},{48,304},{64,320},{80,336},{96,352},{112... | collective-permute-start | bytes 55304 | tf_op jit(solution)/shard_map/ppermute | solution.py:10
  128.3 5.3 %collective-permute-start.7 = (f32[12,3,1,128]{3,0,2,1:T(8,128)}, f32[12,3,1,128]{3,0,2,1:T(8,128)}, u32[]{:S(2)}, u32[]{:S(2)}) collective-permute-start(f32[12,3,1,128]{3,0,2,1:T(8,128)} %get-tuple-element.15), channel_id=1, source_target_pairs={{0,4},{4,8},{8,12},{1,5},{5,9},{9,13},{2,6},{6,10},{10,14},{3,7},{... | collective-permute-start | bytes 55304 | tf_op jit(solution)/shard_map/ppermute | solution.py:26
  133.7 2.1 collective-permute-start.5
  136.4 3.1 %collective-permute-start.2 = (f32[12,3,32,1]{2,3,1,0:T(1,128)S(1)}, f32[12,3,32,1]{2,3,1,0:T(1,128)S(1)}, u32[]{:S(2)}, u32[]{:S(2)}) collective-permute-start(f32[12,3,32,1]{2,3,1,0:T(1,128)S(1)} %copy.45), channel_id=1, source_target_pairs={{0,16},{16,32},{32,48},{48,64},{64,80},{80,96},{96,112},{112,128},... | collective-permute-start | bytes 13832 | tf_op jit(solution)/shard_map/ppermute | solution.py:26
  139.6 5.5 %collective-permute-start = (f32[12,3,32,1]{2,3,1,0:T(1,128)S(1)}, f32[12,3,32,1]{2,3,1,0:T(1,128)S(1)}, u32[]{:S(2)}, u32[]{:S(2)}) collective-permute-start(f32[12,3,32,1]{2,3,1,0:T(1,128)S(1)} %copy.43), channel_id=1, source_target_pairs={{16,0},{32,16},{48,32},{64,48},{80,64},{96,80},{112,96},{128,112},... | collective-permute-start | bytes 13832 | tf_op jit(solution)/shard_map/ppermute | solution.py:27
  145.2 0.8 collective-permute-done
  146.8 2.3 multiply_reduce_fusion
  149.2 52.8 %all-reduce.5.cloned.1.call-done = f32[12,32,128]{2,0,1:T(8,128)} async-done(((f32[12,32,128]{2,0,1:T(8,128)}), f32[12,32,128]{2,0,1:T(8,128)}) %all-reduce.5.cloned.1.call-update) | async-done | bytes 196624 | tf_op jit(solution)/shard_map/psum | solution.py:33
  201.9 1.0 broadcast_divide_fusion
  203.1 4.6 %collective-permute-start.10 = (f32[12,3,1,128]{3,0,2,1:T(8,128)S(1)}, f32[12,3,1,128]{3,0,2,1:T(8,128)S(1)}, u32[]{:S(2)}, u32[]{:S(2)}) collective-permute-start(f32[12,3,1,128]{3,0,2,1:T(8,128)S(1)} %get-tuple-element.7), channel_id=1, source_target_pairs={{0,256},{16,272},{32,288},{48,304},{64,320},{80,336},{96,352},{112... | collective-permute-start | bytes 55304 | tf_op jit(solution)/shard_map/ppermute | solution.py:10
  207.6 5.3 %collective-permute-start.12 = (f32[12,3,1,128]{3,0,2,1:T(8,128)S(1)}, f32[12,3,1,128]{3,0,2,1:T(8,128)S(1)}, u32[]{:S(2)}, u32[]{:S(2)}) collective-permute-start(f32[12,3,1,128]{3,0,2,1:T(8,128)S(1)} %get-tuple-element.8), channel_id=1, source_target_pairs={{0,4},{4,8},{8,12},{1,5},{5,9},{9,13},{2,6},{6,10},{10,14},{3,7},{... | collective-permute-start | bytes 55304 | tf_op jit(solution)/shard_map/ppermute | solution.py:26
  213.0 1.9 collective-permute-start.11
  215.5 5.1 %collective-permute-start.8 = (f32[12,3,32,1]{2,3,1,0:T(1,128)S(1)}, f32[12,3,32,1]{2,3,1,0:T(1,128)S(1)}, u32[]{:S(2)}, u32[]{:S(2)}) collective-permute-start(f32[12,3,32,1]{2,3,1,0:T(1,128)S(1)} %copy.49), channel_id=1, source_target_pairs={{16,0},{32,16},{48,32},{64,48},{80,64},{96,80},{112,96},{128,112},... | collective-permute-start | bytes 13832 | tf_op jit(solution)/shard_map/ppermute | solution.py:27
  220.9 1.9 collective-permute-start.9
  223.3 5.5 %collective-permute-done.9 = f32[12,3,32,1]{2,3,1,0:T(1,128)S(1)} collective-permute-done((f32[12,3,32,1]{2,3,1,0:T(1,128)S(1)}, f32[12,3,32,1]{2,3,1,0:T(1,128)S(1)}, u32[]{:S(2)}, u32[]{:S(2)}) %collective-permute-start.9) | collective-permute-done | bytes 4640 | tf_op jit(solution)/shard_map/ppermute | solution.py:26
  229.2 0.8 fusion.7
  230.0 1.0 copy.53
  (83 shorter events, 9.3 us)
Async XLA Ops:
  7.2 51.5 %collective-permute-start.6 = (f32[3,1,128]{2,0,1:T(4,128)S(1)}, f32[3,1,128]{2,0,1:T(4,128)S(1)}, u32[]{:S(2)}, u32[]{:S(2)}) collective-permute-start(f32[3,1,128]{2,0,1:T(4,128)S(1)} %copy.79), channel_id=1, source_target_pairs={{0,4},{4,8},{8,12},{1,5},{5,9},{9,13},{2,6},{6,10},{10,14},{3,7},{... | collective-permute-start | bytes 4616 | tf_op jit(solution)/shard_map/ppermute | solution.py:16
  13.3 45.5 %collective-permute-start.3 = (f32[2,3,128]{2,1,0:T(4,128)S(1)}, f32[2,3,128]{2,1,0:T(4,128)S(1)}, u32[]{:S(2)}, u32[]{:S(2)}) collective-permute-start(f32[2,3,128]{2,1,0:T(4,128)S(1)} %pad_maximum_fusion.8), channel_id=1, source_target_pairs={{0,256},{16,272},{32,288},{48,304},{64,320},{80,336},{96,352},{112... | collective-permute-start | bytes 9224 | tf_op jit(solution)/shard_map/ppermute | solution.py:10
  18.8 39.8 %collective-permute-start.1 = (f32[3,32,1]{2,1,0:T(8,128)S(1)}, f32[3,32,1]{2,1,0:T(8,128)S(1)}, u32[]{:S(2)}, u32[]{:S(2)}) collective-permute-start(f32[3,32,1]{2,1,0:T(8,128)S(1)} %slice.98), channel_id=1, source_target_pairs={{0,16},{16,32},{32,48},{48,64},{64,80},{80,96},{96,112},{112,128},... | collective-permute-start | bytes 1160 | tf_op jit(solution)/shard_map/ppermute | solution.py:10
  28.4 8.7 %copy-start.2 = (f32[3,32,128]{2,1,0:T(8,128)S(1)}, f32[3,32,128]{2,1,0:T(8,128)}, u32[]{:S(2)}) copy-start(f32[3,32,128]{2,1,0:T(8,128)} %param.11) | copy-start | bytes 147460
  28.4 8.8 %copy-start.3 = (f32[3,32,128]{2,1,0:T(8,128)S(1)}, f32[3,32,128]{2,1,0:T(8,128)}, u32[]{:S(2)}) copy-start(f32[3,32,128]{2,1,0:T(8,128)} %param.14) | copy-start | bytes 147460
  28.4 8.8 %copy-start.1 = (f32[3,32,128]{2,1,0:T(8,128)S(1)}, f32[3,32,128]{2,1,0:T(8,128)}, u32[]{:S(2)}) copy-start(f32[3,32,128]{2,1,0:T(8,128)} %param.15) | copy-start | bytes 147460
  28.4 30.4 %copy-start.4 = (f32[3,32,128]{2,1,0:T(8,128)S(1)}, f32[3,32,128]{2,1,0:T(8,128)}, u32[]{:S(2)}) copy-start(f32[3,32,128]{2,1,0:T(8,128)} %param.12) | copy-start | bytes 147460
  28.4 30.5 %all-to-all-start = ((f32[128,2,4,4]{3,1,2,0:T(2,128)}), f32[128,2,4,4]{3,1,2,0:T(2,128)S(1)}, u32[]{:S(2)}, u32[]{:S(2)}) async-start(f32[128,2,4,4]{3,1,2,0:T(2,128)} %copy.40), calls=%async_computation | async-start | bytes 1048576 | tf_op jit(solution)/shard_map/all_to_all | solution.py:77
  37.1 84.3 %all-reduce.3.cloned.1.call-start = ((), (), s32[]{:S(2)}) async-start(), calls=%async_computation.1 | async-start | bytes 524288 | tf_op jit(solution)/shard_map/psum | solution.py:33
  37.2 26.9 %copy-start.7 = (pred[32]{0:T(512)(128)(4,1)}, pred[32]{0:T(512)(128)(4,1)S(1)}, u32[]{:S(2)}) copy-start(pred[32]{0:T(512)(128)(4,1)S(1)} %get-tuple-element.22) | copy-start | bytes 100
  37.2 107.8 %copy-start.5 = (pred[32]{0:T(512)(128)(4,1)}, pred[32]{0:T(512)(128)(4,1)S(1)}, u32[]{:S(2)}) copy-start(pred[32]{0:T(512)(128)(4,1)S(1)} %get-tuple-element.21) | copy-start | bytes 100
  59.3 4.8 %copy-start = (f32[12,3,32,128]{3,2,1,0:T(8,128)S(1)}, f32[12,3,32,128]{3,2,1,0:T(8,128)}, u32[]{:S(2)}) copy-start(f32[12,3,32,128]{3,2,1,0:T(8,128)} %param.10) | copy-start | bytes 1769476
  64.1 1.2 copy-start.9
  65.3 136.6 %all-reduce.5.cloned.1.call-start = ((), (), s32[]{:S(2)}) async-start(), calls=%async_computation.2 | async-start | bytes 524288 | tf_op jit(solution)/shard_map/psum | solution.py:33
  123.8 23.0 %collective-permute-start.4 = (f32[12,3,1,128]{3,0,2,1:T(8,128)}, f32[12,3,1,128]{3,0,2,1:T(8,128)}, u32[]{:S(2)}, u32[]{:S(2)}) collective-permute-start(f32[12,3,1,128]{3,0,2,1:T(8,128)} %get-tuple-element.14), channel_id=1, source_target_pairs={{0,256},{16,272},{32,288},{48,304},{64,320},{80,336},{96,352},{112... | collective-permute-start | bytes 55304 | tf_op jit(solution)/shard_map/ppermute | solution.py:10
  128.3 18.4 %collective-permute-start.7 = (f32[12,3,1,128]{3,0,2,1:T(8,128)}, f32[12,3,1,128]{3,0,2,1:T(8,128)}, u32[]{:S(2)}, u32[]{:S(2)}) collective-permute-start(f32[12,3,1,128]{3,0,2,1:T(8,128)} %get-tuple-element.15), channel_id=1, source_target_pairs={{0,4},{4,8},{8,12},{1,5},{5,9},{9,13},{2,6},{6,10},{10,14},{3,7},{... | collective-permute-start | bytes 55304 | tf_op jit(solution)/shard_map/ppermute | solution.py:26
  133.7 13.1 %collective-permute-start.5 = (f32[12,3,1,128]{3,0,2,1:T(8,128)}, f32[12,3,1,128]{3,0,2,1:T(8,128)}, u32[]{:S(2)}, u32[]{:S(2)}) collective-permute-start(f32[12,3,1,128]{3,0,2,1:T(8,128)} %get-tuple-element.16), channel_id=1, source_target_pairs={{4,0},{8,4},{12,8},{5,1},{9,5},{13,9},{6,2},{10,6},{14,10},{7,3},{... | collective-permute-start | bytes 55304 | tf_op jit(solution)/shard_map/ppermute | solution.py:27
  136.4 9.9 %collective-permute-start.2 = (f32[12,3,32,1]{2,3,1,0:T(1,128)S(1)}, f32[12,3,32,1]{2,3,1,0:T(1,128)S(1)}, u32[]{:S(2)}, u32[]{:S(2)}) collective-permute-start(f32[12,3,32,1]{2,3,1,0:T(1,128)S(1)} %copy.45), channel_id=1, source_target_pairs={{0,16},{16,32},{32,48},{48,64},{64,80},{80,96},{96,112},{112,128},... | collective-permute-start | bytes 13832 | tf_op jit(solution)/shard_map/ppermute | solution.py:26
  139.6 6.4 %collective-permute-start = (f32[12,3,32,1]{2,3,1,0:T(1,128)S(1)}, f32[12,3,32,1]{2,3,1,0:T(1,128)S(1)}, u32[]{:S(2)}, u32[]{:S(2)}) collective-permute-start(f32[12,3,32,1]{2,3,1,0:T(1,128)S(1)} %copy.43), channel_id=1, source_target_pairs={{16,0},{32,16},{48,32},{64,48},{80,64},{96,80},{112,96},{128,112},... | collective-permute-start | bytes 13832 | tf_op jit(solution)/shard_map/ppermute | solution.py:27
  203.1 26.1 %collective-permute-start.10 = (f32[12,3,1,128]{3,0,2,1:T(8,128)S(1)}, f32[12,3,1,128]{3,0,2,1:T(8,128)S(1)}, u32[]{:S(2)}, u32[]{:S(2)}) collective-permute-start(f32[12,3,1,128]{3,0,2,1:T(8,128)S(1)} %get-tuple-element.7), channel_id=1, source_target_pairs={{0,256},{16,272},{32,288},{48,304},{64,320},{80,336},{96,352},{112... | collective-permute-start | bytes 55304 | tf_op jit(solution)/shard_map/ppermute | solution.py:10
  207.6 21.5 %collective-permute-start.12 = (f32[12,3,1,128]{3,0,2,1:T(8,128)S(1)}, f32[12,3,1,128]{3,0,2,1:T(8,128)S(1)}, u32[]{:S(2)}, u32[]{:S(2)}) collective-permute-start(f32[12,3,1,128]{3,0,2,1:T(8,128)S(1)} %get-tuple-element.8), channel_id=1, source_target_pairs={{0,4},{4,8},{8,12},{1,5},{5,9},{9,13},{2,6},{6,10},{10,14},{3,7},{... | collective-permute-start | bytes 55304 | tf_op jit(solution)/shard_map/ppermute | solution.py:26
  213.0 16.2 %collective-permute-start.11 = (f32[12,3,1,128]{3,0,2,1:T(8,128)S(1)}, f32[12,3,1,128]{3,0,2,1:T(8,128)S(1)}, u32[]{:S(2)}, u32[]{:S(2)}) collective-permute-start(f32[12,3,1,128]{3,0,2,1:T(8,128)S(1)} %get-tuple-element.9), channel_id=1, source_target_pairs={{4,0},{8,4},{12,8},{5,1},{9,5},{13,9},{6,2},{10,6},{14,10},{7,3},{... | collective-permute-start | bytes 55304 | tf_op jit(solution)/shard_map/ppermute | solution.py:27
  215.5 7.3 %collective-permute-start.8 = (f32[12,3,32,1]{2,3,1,0:T(1,128)S(1)}, f32[12,3,32,1]{2,3,1,0:T(1,128)S(1)}, u32[]{:S(2)}, u32[]{:S(2)}) collective-permute-start(f32[12,3,32,1]{2,3,1,0:T(1,128)S(1)} %copy.49), channel_id=1, source_target_pairs={{16,0},{32,16},{48,32},{64,48},{80,64},{96,80},{112,96},{128,112},... | collective-permute-start | bytes 13832 | tf_op jit(solution)/shard_map/ppermute | solution.py:27
  220.9 8.3 %copy-start.6 = (pred[32]{0:T(512)(128)(4,1)S(1)}, pred[32]{0:T(512)(128)(4,1)}, u32[]{:S(2)}) copy-start(pred[32]{0:T(512)(128)(4,1)} %copy-done.5) | copy-start | bytes 100
  220.9 8.3 %copy-start.8 = (pred[32]{0:T(512)(128)(4,1)S(1)}, pred[32]{0:T(512)(128)(4,1)}, u32[]{:S(2)}) copy-start(pred[32]{0:T(512)(128)(4,1)} %copy-done.7) | copy-start | bytes 100
  220.9 7.8 %collective-permute-start.9 = (f32[12,3,32,1]{2,3,1,0:T(1,128)S(1)}, f32[12,3,32,1]{2,3,1,0:T(1,128)S(1)}, u32[]{:S(2)}, u32[]{:S(2)}) collective-permute-start(f32[12,3,32,1]{2,3,1,0:T(1,128)S(1)} %copy.51), channel_id=1, source_target_pairs={{0,16},{16,32},{32,48},{48,64},{64,80},{80,96},{96,112},{112,128},... | collective-permute-start | bytes 13832 | tf_op jit(solution)/shard_map/ppermute | solution.py:26
Sparse Core Ops, SparseCore 0:
  65.4 55.9 all-reduce.2
  149.3 52.6 all-reduce.4

commit v2 on v1

--- a/solution.py
+++ b/solution.py
@@ -1,7 +1,70 @@
+import functools
+
 import jax
 import jax.numpy as jnp
 from jax import lax
+from jax.experimental import pallas as pl
+from jax.experimental.pallas import tpu as pltpu
 from jax.sharding import PartitionSpec as P
+
+MESH = pl.DeviceIdType.MESH
+
+
+def lev_sum_body(n, part_ref, out_ref, slots, send_sem, recv_sem):
+    me = lax.axis_index("lev")
+    barrier = pltpu.get_barrier_semaphore()
+    for d in range(1, n):
+        pl.semaphore_signal(
+            barrier, inc=1, device_id={"lev": lax.rem(me + d, n)}, device_id_type=MESH
+        )
+    pl.semaphore_wait(barrier, n - 1)
+    sends = []
+    for d in range(1, n):
+        copy = pltpu.make_async_remote_copy(
+            src_ref=part_ref,
+            dst_ref=slots.at[me],
+            send_sem=send_sem.at[d - 1],
+            recv_sem=recv_sem.at[me],
+            device_id={"lev": lax.rem(me + d, n)},
+            device_id_type=MESH,
+        )
+        copy.start()
+        sends.append(copy)
+    slots[me] = part_ref[...]
+    for d in range(1, n):
+        sender = lax.rem(me + n - d, n)
+        pltpu.make_async_remote_copy(
+            src_ref=part_ref,
+            dst_ref=slots.at[sender],
+            send_sem=send_sem.at[d - 1],
+            recv_sem=recv_sem.at[sender],
+            device_id={"lev": sender},
+            device_id_type=MESH,
+        ).wait_recv()
+    for copy in sends:
+        copy.wait_send()
+    total = slots[0]
+    for s in range(1, n):
+        total = total + slots[s]
+    out_ref[...] = total
+
+
+def lev_sum(x, collective_id):
+    n = lax.axis_size("lev")
+    return pl.pallas_call(
+        functools.partial(lev_sum_body, n),
+        out_shape=jax.ShapeDtypeStruct(x.shape, x.dtype),
+        in_specs=[pl.BlockSpec(memory_space=pltpu.VMEM)],
+        out_specs=pl.BlockSpec(memory_space=pltpu.VMEM),
+        scratch_shapes=[
+            pltpu.VMEM((n,) + x.shape, x.dtype),
+            pltpu.SemaphoreType.DMA((n - 1,)),
+            pltpu.SemaphoreType.DMA((n,)),
+        ],
+        compiler_params=pltpu.CompilerParams(
+            collective_id=collective_id, has_side_effects=True
+        ),
+    )(x)
 
 
 def from_behind(value, axis, steps):
@@ -103,13 +166,19 @@
         (jnp.maximum(pole_courant, 0.0) - jnp.minimum(partner_winds[1], 0.0))[:, None, :],
         -jnp.minimum(south_wind, 0.0),
     )
-    total_detrain = lax.psum(jnp.sum(detrain_share, axis=0), "lev")
+    detrain_part = jnp.sum(detrain_share, axis=0)
     adjoint = adjoint_field
     for position in range(step_count):
         step_now = step_count - 1 - position
         adjoint = adjoint + forcing_grid[step_now][None]
         partial_sum = jnp.sum(detrain_share[None] * adjoint, axis=1)
-        column_sum = mix_sum(partial_sum)
+        if position == 0:
+            reduced = lev_sum(
+                jnp.concatenate([partial_sum, detrain_part[None]], axis=0), 0
+            )
+            column_sum, total_detrain = reduced[:tracers], reduced[tracers]
+        else:
+            column_sum = lev_sum(partial_sum, 1)
         adjoint = (1.0 - mix_fraction)[None] * adjoint + mix_fraction[None] * (
             column_sum / total_detrain
         )[:, None]

time: 239 us -> 163 us (0.68)
  waiting for transfers between devices: 115 us -> 24.8 us
  Pallas kernels: 0 us -> 53.5 us
  blocking collectives: 21.4 us -> 0 us
  between operations: 14 us -> 0.6 us
  starting transfers between devices: 61.3 us -> 55.7 us
    psum x2 -> x0, waiting for transfers between devices: 109 us -> none  [mix_sum(): return lax.psum(partial_sum, 'lev')]
    pallas_call x0 -> x2, Pallas kernels: none -> 53.5 us  [lev_sum(): pl.pallas_call(functools.partial(lev_sum_body, n), out_shape=jax.ShapeDty...]
    psum x1 -> x0, blocking collectives: 21.4 us -> none  [on_device(): total_detrain = lax.psum(jnp.sum(detrain_share, axis=0), 'lev')]
    all_to_all x1, waiting for transfers between devices: 0.01 us -> 18.6 us  [on_device(): arrived = lax.all_to_all(packed, ('lon', 'lat'), 0, 0, tiled=True)]
    ppermute x4, starting transfers between devices: 15.6 us -> 10.9 us  [extended(): before = lax.ppermute(last, axis, up)]
    ppermute x4, starting transfers between devices: 17 us -> 13.5 us  [from_behind(): return lax.ppermute(value, axis, pairs)]
    ppermute x4, starting transfers between devices: 14.6 us -> 17.3 us  [extended(): after = lax.ppermute(initial, axis, down)]
  transfers between devices with their start and end apart: 16 -> 14, of which waited for: 4 -> 3; matrix products, arithmetic and copies ran while one was open for 5% -> 7% of each run, Pallas kernels for 0% -> 0%
where the time goes in v2:
time: 163 us; the launch traced here: 162 us
  starting transfers between devices  55.7 us (34%)
  Pallas kernels  53.5 us (33%)
  waiting for transfers between devices  24.8 us (15%)
  other arithmetic  11.4 us (7%)
  local copies, waits for them, and re-layouts  10.8 us (7%)
  matrix products  4.78 us (3%)
    pallas_call x2, Pallas kernels, lev_sum(): pl.pallas_call(functools.partial(lev_sum_body, n), out_shape=jax.ShapeDty...  53.5 us
    all_to_all x1, waiting for transfers between devices, on_device(): arrived = lax.all_to_all(packed, ('lon', 'lat'), 0, 0, tiled=True)  18.6 us
    ppermute x4, starting transfers between devices, extended(): after = lax.ppermute(initial, axis, down)  17.3 us
    ppermute x4, starting transfers between devices, from_behind(): return lax.ppermute(value, axis, pairs)  13.5 us
    ppermute x4, starting transfers between devices, extended(): before = lax.ppermute(last, axis, up)  10.9 us
    all_to_all x1, starting transfers between devices, on_device(): arrived = lax.all_to_all(packed, ('lon', 'lat'), 0, 0, tiled=True)  8.66 us
    ppermute x4, waiting for transfers between devices, extended(): before = lax.ppermute(last, axis, up)  5.48 us
    ppermute x1, starting transfers between devices, from_behind_2(): return lax.ppermute(block, axis, route)  5.38 us
  transfers between devices with their start and end apart: 14, of which 3 were waited for; matrix products, arithmetic and copies ran while one was open for 7% of the time, Pallas kernels for 0%

profile of v2, /device:TPU:1, one launch (start us, length us, event | category | flops | bytes accessed | tf_op | source)
XLA Modules:
  0.0 161.7 jit_solution(8559665060213443067)
XLA Ops:
  0.0 0.7 slice.110
  0.7 5.4 %collective-permute-start.6 = (f32[3,1,128]{2,0,1:T(4,128)S(1)}, f32[3,1,128]{2,0,1:T(4,128)S(1)}, u32[]{:S(2)}, u32[]{:S(2)}) collective-permute-start(f32[3,1,128]{2,0,1:T(4,128)S(1)} %copy.89), channel_id=1, source_target_pairs={{0,4},{4,8},{8,12},{1,5},{5,9},{9,13},{2,6},{6,10},{10,14},{3,7},{... | collective-permute-start | bytes 4616 | tf_op jit(solution)/shard_map/ppermute | solution.py:79
  6.8 4.6 %collective-permute-start.3 = (f32[2,3,128]{2,1,0:T(4,128)S(1)}, f32[2,3,128]{2,1,0:T(4,128)S(1)}, u32[]{:S(2)}, u32[]{:S(2)}) collective-permute-start(f32[2,3,128]{2,1,0:T(4,128)S(1)} %pad_maximum_fusion.9), channel_id=1, source_target_pairs={{0,256},{16,272},{32,288},{48,304},{64,320},{80,336},{96,352},{112... | collective-permute-start | bytes 9224 | tf_op jit(solution)/shard_map/ppermute | solution.py:73
  11.5 0.9 slice.106
  12.3 3.2 %collective-permute-start.1 = (f32[3,32,1]{2,1,0:T(8,128)S(1)}, f32[3,32,1]{2,1,0:T(8,128)S(1)}, u32[]{:S(2)}, u32[]{:S(2)}) collective-permute-start(f32[3,32,1]{2,1,0:T(8,128)S(1)} %slice.106), channel_id=1, source_target_pairs={{0,16},{16,32},{32,48},{48,64},{64,80},{80,96},{96,112},{112,128},... | collective-permute-start | bytes 1160 | tf_op jit(solution)/shard_map/ppermute | solution.py:73
  15.6 0.7 iota_compare_fusion.2
  20.7 1.2 copy.46
  21.9 8.7 %all-to-all-start = ((f32[128,2,4,4]{3,1,2,0:T(2,128)}), f32[128,2,4,4]{3,1,2,0:T(2,128)S(1)}, u32[]{:S(2)}, u32[]{:S(2)}) async-start(f32[128,2,4,4]{3,1,2,0:T(2,128)} %copy.46), calls=%async_computation | async-start | bytes 1048576 | tf_op jit(solution)/shard_map/all_to_all | solution.py:140
  30.9 18.6 %all-to-all-done = f32[128,2,4,4]{3,1,2,0:T(2,128)S(1)} async-done(((f32[128,2,4,4]{3,1,2,0:T(2,128)}), f32[128,2,4,4]{3,1,2,0:T(2,128)S(1)}, u32[]{:S(2)}, u32[]{:S(2)}) %all-to-all-start) | async-done | bytes 16416 | tf_op jit(solution)/shard_map/all_to_all | solution.py:140
  49.9 4.8 %fusion = f32[2,3,4096]{2,1,0:T(4,128)S(1)} fusion(f32[4096]{0:T(1024)S(1)} %iota_convert_fusion, f32[2,512]{1,0:T(2,128)S(1)} %bitcast.60, f32[2,4,512]{2,1,0:T(4,128)S(1)} %reshape.145), kind=kOutput, calls=%fused_computation | convolution fusion | flops 155189248 | bytes 135168 | tf_op jit(solution)/shard_map/tke,tec->tkc/dot_general | solution.py:146
  55.3 0.7 pad_maximum_fusion.8.part_ref
  56.0 31.6 %shard_map.100 = f32[13,32,128]{2,1,0:T(8,128)} custom-call(f32[13,32,128]{2,1,0:T(8,128)} %pad_maximum_fusion.8.part_ref), custom_call_target="tpu_custom_call" | custom-call | tf_op jit(solution)/shard_map/pallas_call | solution.py:54
  87.5 0.7 slice_bitcast_fusion.2
  88.3 0.9 slice_divide_fusion
  90.7 3.6 %collective-permute-start.4 = (f32[12,3,1,128]{3,0,2,1:T(8,128)}, f32[12,3,1,128]{3,0,2,1:T(8,128)}, u32[]{:S(2)}, u32[]{:S(2)}) collective-permute-start(f32[12,3,1,128]{3,0,2,1:T(8,128)} %get-tuple-element.14), channel_id=1, source_target_pairs={{0,256},{16,272},{32,288},{48,304},{64,320},{80,336},{96,352},{112... | collective-permute-start | bytes 55304 | tf_op jit(solution)/shard_map/ppermute | solution.py:73
  94.3 1.9 %collective-permute-start.7 = (f32[12,3,1,128]{3,0,2,1:T(8,128)}, f32[12,3,1,128]{3,0,2,1:T(8,128)}, u32[]{:S(2)}, u32[]{:S(2)}) collective-permute-start(f32[12,3,1,128]{3,0,2,1:T(8,128)} %get-tuple-element.15), channel_id=1, source_target_pairs={{0,4},{4,8},{8,12},{1,5},{5,9},{9,13},{2,6},{6,10},{10,14},{3,7},{... | collective-permute-start | bytes 55304 | tf_op jit(solution)/shard_map/ppermute | solution.py:89
  96.2 3.0 %collective-permute-start.5 = (f32[12,3,1,128]{3,0,2,1:T(8,128)}, f32[12,3,1,128]{3,0,2,1:T(8,128)}, u32[]{:S(2)}, u32[]{:S(2)}) collective-permute-start(f32[12,3,1,128]{3,0,2,1:T(8,128)} %get-tuple-element.16), channel_id=1, source_target_pairs={{4,0},{8,4},{12,8},{5,1},{9,5},{13,9},{6,2},{10,6},{14,10},{7,3},{... | collective-permute-start | bytes 55304 | tf_op jit(solution)/shard_map/ppermute | solution.py:90
  99.9 3.2 %collective-permute-start.2 = (f32[12,3,32,1]{2,3,1,0:T(1,128)S(1)}, f32[12,3,32,1]{2,3,1,0:T(1,128)S(1)}, u32[]{:S(2)}, u32[]{:S(2)}) collective-permute-start(f32[12,3,32,1]{2,3,1,0:T(1,128)S(1)} %copy.53), channel_id=1, source_target_pairs={{0,16},{16,32},{32,48},{48,64},{64,80},{80,96},{96,112},{112,128},... | collective-permute-start | bytes 13832 | tf_op jit(solution)/shard_map/ppermute | solution.py:89
  103.1 5.6 %collective-permute-start = (f32[12,3,32,1]{2,3,1,0:T(1,128)S(1)}, f32[12,3,32,1]{2,3,1,0:T(1,128)S(1)}, u32[]{:S(2)}, u32[]{:S(2)}) collective-permute-start(f32[12,3,32,1]{2,3,1,0:T(1,128)S(1)} %copy.51), channel_id=1, source_target_pairs={{16,0},{32,16},{48,32},{64,48},{80,64},{96,80},{112,96},{128,112},... | collective-permute-start | bytes 13832 | tf_op jit(solution)/shard_map/ppermute | solution.py:90
  108.8 0.8 collective-permute-done
  110.4 1.6 %multiply_reduce_fusion = (f32[12,32,128]{2,0,1:T(8,128)S(1)}, f32[12,3,32,128]{3,0,2,1:T(8,128)S(1)}) fusion(f32[3,32,128]{2,1,0:T(8,128)S(1)} %copy-done.1, f32[3,32,128]{2,1,0:T(8,128)S(1)} %bitcast.54, f32[12,3,32,128]{3,0,2,1:T(8,128)S(1)} %fusion.35, f32[12,3,1,128]{3,0,2,1:T(8,128)} %collective-permute-done.7, pred[32]{0:T(512)(128)(4,1)} %copy-done.5, ...), kind=kLoop, calls=%fused_computation.50 | loop fusion | flops 3047424 | bytes 1735744 | tf_op jit(solution)/shard_map/reduce_sum | solution.py:174
  112.1 0.7 copy.57.part_ref
  112.8 21.9 %shard_map.101 = f32[12,32,128]{2,1,0:T(8,128)} custom-call(f32[12,32,128]{2,1,0:T(8,128)} %copy.57.part_ref), custom_call_target="tpu_custom_call" | custom-call | tf_op jit(solution)/shard_map/pallas_call | solution.py:54
  134.8 0.9 broadcast_divide_fusion
  136.0 2.1 %collective-permute-start.10 = (f32[12,3,1,128]{3,0,2,1:T(8,128)S(1)}, f32[12,3,1,128]{3,0,2,1:T(8,128)S(1)}, u32[]{:S(2)}, u32[]{:S(2)}) collective-permute-start(f32[12,3,1,128]{3,0,2,1:T(8,128)S(1)} %get-tuple-element.7), channel_id=1, source_target_pairs={{0,256},{16,272},{32,288},{48,304},{64,320},{80,336},{96,352},{112... | collective-permute-start | bytes 55304 | tf_op jit(solution)/shard_map/ppermute | solution.py:73
  138.1 3.9 %collective-permute-start.12 = (f32[12,3,1,128]{3,0,2,1:T(8,128)S(1)}, f32[12,3,1,128]{3,0,2,1:T(8,128)S(1)}, u32[]{:S(2)}, u32[]{:S(2)}) collective-permute-start(f32[12,3,1,128]{3,0,2,1:T(8,128)S(1)} %get-tuple-element.8), channel_id=1, source_target_pairs={{0,4},{4,8},{8,12},{1,5},{5,9},{9,13},{2,6},{6,10},{10,14},{3,7},{... | collective-permute-start | bytes 55304 | tf_op jit(solution)/shard_map/ppermute | solution.py:89
  142.0 1.9 %collective-permute-start.11 = (f32[12,3,1,128]{3,0,2,1:T(8,128)S(1)}, f32[12,3,1,128]{3,0,2,1:T(8,128)S(1)}, u32[]{:S(2)}, u32[]{:S(2)}) collective-permute-start(f32[12,3,1,128]{3,0,2,1:T(8,128)S(1)} %get-tuple-element.9), channel_id=1, source_target_pairs={{4,0},{8,4},{12,8},{5,1},{9,5},{13,9},{6,2},{10,6},{14,10},{7,3},{... | collective-permute-start | bytes 55304 | tf_op jit(solution)/shard_map/ppermute | solution.py:90
  144.5 6.8 %collective-permute-start.8 = (f32[12,3,32,1]{2,3,1,0:T(1,128)S(1)}, f32[12,3,32,1]{2,3,1,0:T(1,128)S(1)}, u32[]{:S(2)}, u32[]{:S(2)}) collective-permute-start(f32[12,3,32,1]{2,3,1,0:T(1,128)S(1)} %copy.59), channel_id=1, source_target_pairs={{16,0},{32,16},{48,32},{64,48},{80,64},{96,80},{112,96},{128,112},... | collective-permute-start | bytes 13832 | tf_op jit(solution)/shard_map/ppermute | solution.py:90
  151.7 1.9 %collective-permute-start.9 = (f32[12,3,32,1]{2,3,1,0:T(1,128)S(1)}, f32[12,3,32,1]{2,3,1,0:T(1,128)S(1)}, u32[]{:S(2)}, u32[]{:S(2)}) collective-permute-start(f32[12,3,32,1]{2,3,1,0:T(1,128)S(1)} %copy.61), channel_id=1, source_target_pairs={{0,16},{16,32},{32,48},{48,64},{64,80},{80,96},{96,112},{112,128},... | collective-permute-start | bytes 13832 | tf_op jit(solution)/shard_map/ppermute | solution.py:89
  154.0 5.5 %collective-permute-done.9 = f32[12,3,32,1]{2,3,1,0:T(1,128)S(1)} collective-permute-done((f32[12,3,32,1]{2,3,1,0:T(1,128)S(1)}, f32[12,3,32,1]{2,3,1,0:T(1,128)S(1)}, u32[]{:S(2)}, u32[]{:S(2)}) %collective-permute-start.9) | collective-permute-done | bytes 4640 | tf_op jit(solution)/shard_map/ppermute | solution.py:89
  160.0 0.8 fusion.7
  160.7 1.0 copy.63
  (84 shorter events, 11.3 us)
Async XLA Ops:
  0.7 30.1 %collective-permute-start.6 = (f32[3,1,128]{2,0,1:T(4,128)S(1)}, f32[3,1,128]{2,0,1:T(4,128)S(1)}, u32[]{:S(2)}, u32[]{:S(2)}) collective-permute-start(f32[3,1,128]{2,0,1:T(4,128)S(1)} %copy.89), channel_id=1, source_target_pairs={{0,4},{4,8},{8,12},{1,5},{5,9},{9,13},{2,6},{6,10},{10,14},{3,7},{... | collective-permute-start | bytes 4616 | tf_op jit(solution)/shard_map/ppermute | solution.py:79
  6.8 24.0 %collective-permute-start.3 = (f32[2,3,128]{2,1,0:T(4,128)S(1)}, f32[2,3,128]{2,1,0:T(4,128)S(1)}, u32[]{:S(2)}, u32[]{:S(2)}) collective-permute-start(f32[2,3,128]{2,1,0:T(4,128)S(1)} %pad_maximum_fusion.9), channel_id=1, source_target_pairs={{0,256},{16,272},{32,288},{48,304},{64,320},{80,336},{96,352},{112... | collective-permute-start | bytes 9224 | tf_op jit(solution)/shard_map/ppermute | solution.py:73
  12.3 18.4 %collective-permute-start.1 = (f32[3,32,1]{2,1,0:T(8,128)S(1)}, f32[3,32,1]{2,1,0:T(8,128)S(1)}, u32[]{:S(2)}, u32[]{:S(2)}) collective-permute-start(f32[3,32,1]{2,1,0:T(8,128)S(1)} %slice.106), channel_id=1, source_target_pairs={{0,16},{16,32},{32,48},{48,64},{64,80},{80,96},{96,112},{112,128},... | collective-permute-start | bytes 1160 | tf_op jit(solution)/shard_map/ppermute | solution.py:73
  21.9 8.7 %copy-start.2 = (f32[3,32,128]{2,1,0:T(8,128)S(1)}, f32[3,32,128]{2,1,0:T(8,128)}, u32[]{:S(2)}) copy-start(f32[3,32,128]{2,1,0:T(8,128)} %param.11) | copy-start | bytes 147460
  21.9 8.7 %copy-start.3 = (f32[3,32,128]{2,1,0:T(8,128)S(1)}, f32[3,32,128]{2,1,0:T(8,128)}, u32[]{:S(2)}) copy-start(f32[3,32,128]{2,1,0:T(8,128)} %param.14) | copy-start | bytes 147460
  21.9 8.8 %copy-start.1 = (f32[3,32,128]{2,1,0:T(8,128)S(1)}, f32[3,32,128]{2,1,0:T(8,128)}, u32[]{:S(2)}) copy-start(f32[3,32,128]{2,1,0:T(8,128)} %param.15) | copy-start | bytes 147460
  21.9 9.0 %copy-start.4 = (f32[3,32,128]{2,1,0:T(8,128)S(1)}, f32[3,32,128]{2,1,0:T(8,128)}, u32[]{:S(2)}) copy-start(f32[3,32,128]{2,1,0:T(8,128)} %param.12) | copy-start | bytes 147460
  21.9 9.0 %copy-start.9 = (f32[3,128]{1,0:T(4,128)S(1)}, f32[3,128]{1,0:T(4,128)}, u32[]{:S(2)}) copy-start(f32[3,128]{1,0:T(4,128)} %param.13) | copy-start | bytes 4612
  21.9 27.6 %all-to-all-start = ((f32[128,2,4,4]{3,1,2,0:T(2,128)}), f32[128,2,4,4]{3,1,2,0:T(2,128)S(1)}, u32[]{:S(2)}, u32[]{:S(2)}) async-start(f32[128,2,4,4]{3,1,2,0:T(2,128)} %copy.46), calls=%async_computation | async-start | bytes 1048576 | tf_op jit(solution)/shard_map/all_to_all | solution.py:140
  30.7 18.8 %copy-start.7 = (pred[32]{0:T(512)(128)(4,1)}, pred[32]{0:T(512)(128)(4,1)S(1)}, u32[]{:S(2)}) copy-start(pred[32]{0:T(512)(128)(4,1)S(1)} %get-tuple-element.22) | copy-start | bytes 100
  30.7 78.0 %copy-start.5 = (pred[32]{0:T(512)(128)(4,1)}, pred[32]{0:T(512)(128)(4,1)S(1)}, u32[]{:S(2)}) copy-start(pred[32]{0:T(512)(128)(4,1)S(1)} %get-tuple-element.21) | copy-start | bytes 100
  49.9 4.8 %copy-start = (f32[12,3,32,128]{3,2,1,0:T(8,128)S(1)}, f32[12,3,32,128]{3,2,1,0:T(8,128)}, u32[]{:S(2)}) copy-start(f32[12,3,32,128]{3,2,1,0:T(8,128)} %param.10) | copy-start | bytes 1769476
  90.7 19.7 %collective-permute-start.4 = (f32[12,3,1,128]{3,0,2,1:T(8,128)}, f32[12,3,1,128]{3,0,2,1:T(8,128)}, u32[]{:S(2)}, u32[]{:S(2)}) collective-permute-start(f32[12,3,1,128]{3,0,2,1:T(8,128)} %get-tuple-element.14), channel_id=1, source_target_pairs={{0,256},{16,272},{32,288},{48,304},{64,320},{80,336},{96,352},{112... | collective-permute-start | bytes 55304 | tf_op jit(solution)/shard_map/ppermute | solution.py:73
  94.3 16.1 %collective-permute-start.7 = (f32[12,3,1,128]{3,0,2,1:T(8,128)}, f32[12,3,1,128]{3,0,2,1:T(8,128)}, u32[]{:S(2)}, u32[]{:S(2)}) collective-permute-start(f32[12,3,1,128]{3,0,2,1:T(8,128)} %get-tuple-element.15), channel_id=1, source_target_pairs={{0,4},{4,8},{8,12},{1,5},{5,9},{9,13},{2,6},{6,10},{10,14},{3,7},{... | collective-permute-start | bytes 55304 | tf_op jit(solution)/shard_map/ppermute | solution.py:89
  96.2 14.2 %collective-permute-start.5 = (f32[12,3,1,128]{3,0,2,1:T(8,128)}, f32[12,3,1,128]{3,0,2,1:T(8,128)}, u32[]{:S(2)}, u32[]{:S(2)}) collective-permute-start(f32[12,3,1,128]{3,0,2,1:T(8,128)} %get-tuple-element.16), channel_id=1, source_target_pairs={{4,0},{8,4},{12,8},{5,1},{9,5},{13,9},{6,2},{10,6},{14,10},{7,3},{... | collective-permute-start | bytes 55304 | tf_op jit(solution)/shard_map/ppermute | solution.py:90
  99.9 10.1 %collective-permute-start.2 = (f32[12,3,32,1]{2,3,1,0:T(1,128)S(1)}, f32[12,3,32,1]{2,3,1,0:T(1,128)S(1)}, u32[]{:S(2)}, u32[]{:S(2)}) collective-permute-start(f32[12,3,32,1]{2,3,1,0:T(1,128)S(1)} %copy.53), channel_id=1, source_target_pairs={{0,16},{16,32},{32,48},{48,64},{64,80},{80,96},{96,112},{112,128},... | collective-permute-start | bytes 13832 | tf_op jit(solution)/shard_map/ppermute | solution.py:89
  103.1 6.5 %collective-permute-start = (f32[12,3,32,1]{2,3,1,0:T(1,128)S(1)}, f32[12,3,32,1]{2,3,1,0:T(1,128)S(1)}, u32[]{:S(2)}, u32[]{:S(2)}) collective-permute-start(f32[12,3,32,1]{2,3,1,0:T(1,128)S(1)} %copy.51), channel_id=1, source_target_pairs={{16,0},{32,16},{48,32},{64,48},{80,64},{96,80},{112,96},{128,112},... | collective-permute-start | bytes 13832 | tf_op jit(solution)/shard_map/ppermute | solution.py:90
  136.0 23.9 %collective-permute-start.10 = (f32[12,3,1,128]{3,0,2,1:T(8,128)S(1)}, f32[12,3,1,128]{3,0,2,1:T(8,128)S(1)}, u32[]{:S(2)}, u32[]{:S(2)}) collective-permute-start(f32[12,3,1,128]{3,0,2,1:T(8,128)S(1)} %get-tuple-element.7), channel_id=1, source_target_pairs={{0,256},{16,272},{32,288},{48,304},{64,320},{80,336},{96,352},{112... | collective-permute-start | bytes 55304 | tf_op jit(solution)/shard_map/ppermute | solution.py:73
  138.1 21.8 %collective-permute-start.12 = (f32[12,3,1,128]{3,0,2,1:T(8,128)S(1)}, f32[12,3,1,128]{3,0,2,1:T(8,128)S(1)}, u32[]{:S(2)}, u32[]{:S(2)}) collective-permute-start(f32[12,3,1,128]{3,0,2,1:T(8,128)S(1)} %get-tuple-element.8), channel_id=1, source_target_pairs={{0,4},{4,8},{8,12},{1,5},{5,9},{9,13},{2,6},{6,10},{10,14},{3,7},{... | collective-permute-start | bytes 55304 | tf_op jit(solution)/shard_map/ppermute | solution.py:89
  142.0 17.9 %collective-permute-start.11 = (f32[12,3,1,128]{3,0,2,1:T(8,128)S(1)}, f32[12,3,1,128]{3,0,2,1:T(8,128)S(1)}, u32[]{:S(2)}, u32[]{:S(2)}) collective-permute-start(f32[12,3,1,128]{3,0,2,1:T(8,128)S(1)} %get-tuple-element.9), channel_id=1, source_target_pairs={{4,0},{8,4},{12,8},{5,1},{9,5},{13,9},{6,2},{10,6},{14,10},{7,3},{... | collective-permute-start | bytes 55304 | tf_op jit(solution)/shard_map/ppermute | solution.py:90
  144.5 9.1 %collective-permute-start.8 = (f32[12,3,32,1]{2,3,1,0:T(1,128)S(1)}, f32[12,3,32,1]{2,3,1,0:T(1,128)S(1)}, u32[]{:S(2)}, u32[]{:S(2)}) collective-permute-start(f32[12,3,32,1]{2,3,1,0:T(1,128)S(1)} %copy.59), channel_id=1, source_target_pairs={{16,0},{32,16},{48,32},{64,48},{80,64},{96,80},{112,96},{128,112},... | collective-permute-start | bytes 13832 | tf_op jit(solution)/shard_map/ppermute | solution.py:90
  151.7 8.3 %copy-start.6 = (pred[32]{0:T(512)(128)(4,1)S(1)}, pred[32]{0:T(512)(128)(4,1)}, u32[]{:S(2)}) copy-start(pred[32]{0:T(512)(128)(4,1)} %copy-done.5) | copy-start | bytes 100
  151.7 8.3 %copy-start.8 = (pred[32]{0:T(512)(128)(4,1)S(1)}, pred[32]{0:T(512)(128)(4,1)}, u32[]{:S(2)}) copy-start(pred[32]{0:T(512)(128)(4,1)} %copy-done.7) | copy-start | bytes 100
  151.7 7.8 %collective-permute-start.9 = (f32[12,3,32,1]{2,3,1,0:T(1,128)S(1)}, f32[12,3,32,1]{2,3,1,0:T(1,128)S(1)}, u32[]{:S(2)}, u32[]{:S(2)}) collective-permute-start(f32[12,3,32,1]{2,3,1,0:T(1,128)S(1)} %copy.61), channel_id=1, source_target_pairs={{0,16},{16,32},{32,48},{48,64},{64,80},{80,96},{96,112},{112,128},... | collective-permute-start | bytes 13832 | tf_op jit(solution)/shard_map/ppermute | solution.py:89

commit v3 on v2

--- a/solution.py
+++ b/solution.py
@@ -47,6 +47,82 @@
     for s in range(1, n):
         total = total + slots[s]
     out_ref[...] = total
+
+
+def halo_body(lon_n, lat_n, col_last, col_first, row_last, row_first,
+              west_out, east_out, north_out, south_out, cols, rows, send_sem, col_sem, row_sem):
+    lon = lax.axis_index("lon")
+    lat = lax.axis_index("lat")
+    half = lon_n // 2
+    top = lat // (lat_n - 1)
+    inner = (lat + lat_n - 1) // lat_n
+    east = {"lon": lax.rem(lon + 1, lon_n)}
+    west = {"lon": lax.rem(lon + lon_n - 1, lon_n)}
+    up = {"lon": lax.rem(lon + half * top, lon_n), "lat": lat + 1 - top}
+    down = {"lon": lax.rem(lon + half * (1 - inner), lon_n), "lat": lat - inner}
+    up_slot = 1 - top
+    down_slot = 1 - inner
+    barrier = pltpu.get_barrier_semaphore()
+    for peer in (east, west, up, down):
+        pl.semaphore_signal(barrier, inc=1, device_id=peer, device_id_type=MESH)
+    pl.semaphore_wait(barrier, 4)
+    plan = (
+        (col_last, cols.at[0], col_sem.at[0], east),
+        (col_first, cols.at[1], col_sem.at[1], west),
+        (row_last, rows.at[up_slot], row_sem.at[up_slot], up),
+        (row_first, rows.at[down_slot], row_sem.at[down_slot], down),
+    )
+    sends = []
+    for i, (src, dst, sem, peer) in enumerate(plan):
+        copy = pltpu.make_async_remote_copy(
+            src_ref=src, dst_ref=dst, send_sem=send_sem.at[i], recv_sem=sem,
+            device_id=peer, device_id_type=MESH,
+        )
+        copy.start()
+        sends.append(copy)
+    arrivals = (
+        (col_last, cols.at[0], col_sem.at[0]),
+        (col_first, cols.at[1], col_sem.at[1]),
+        (row_last, rows.at[0], row_sem.at[0]),
+        (row_first, rows.at[1], row_sem.at[1]),
+    )
+    for src, dst, sem in arrivals:
+        pltpu.make_async_remote_copy(
+            src_ref=src, dst_ref=dst, send_sem=send_sem.at[0], recv_sem=sem,
+            device_id=east, device_id_type=MESH,
+        ).wait_recv()
+    for copy in sends:
+        copy.wait_send()
+    west_out[...] = cols[0]
+    east_out[...] = cols[1]
+    north_out[...] = rows[0]
+    south_out[...] = rows[1]
+
+
+def halo_swap(col_last, col_first, row_last, row_first, collective_id):
+    lon_n, lat_n = lax.axis_size("lon"), lax.axis_size("lat")
+    vmem = pl.BlockSpec(memory_space=pltpu.VMEM)
+    return pl.pallas_call(
+        functools.partial(halo_body, lon_n, lat_n),
+        out_shape=(
+            jax.ShapeDtypeStruct(col_last.shape, col_last.dtype),
+            jax.ShapeDtypeStruct(col_last.shape, col_last.dtype),
+            jax.ShapeDtypeStruct(row_last.shape, row_last.dtype),
+            jax.ShapeDtypeStruct(row_last.shape, row_last.dtype),
+        ),
+        in_specs=[vmem] * 4,
+        out_specs=(vmem,) * 4,
+        scratch_shapes=[
+            pltpu.VMEM((2,) + col_last.shape, col_last.dtype),
+            pltpu.VMEM((2,) + row_last.shape, row_last.dtype),
+            pltpu.SemaphoreType.DMA((4,)),
+            pltpu.SemaphoreType.DMA((2,)),
+            pltpu.SemaphoreType.DMA((2,)),
+        ],
+        compiler_params=pltpu.CompilerParams(
+            collective_id=collective_id, has_side_effects=True
+        ),
+    )(col_last, col_first, row_last, row_first)
 
 
 def lev_sum(x, collective_id):
@@ -182,16 +258,26 @@
         adjoint = (1.0 - mix_fraction)[None] * adjoint + mix_fraction[None] * (
             column_sum / total_detrain
         )[:, None]
-        across = extended(adjoint, (("lon", 3),), 1, True)
-        east_side = across[:, :, :, 2:]
-        west_side = across[:, :, :, :-2]
-        upright = extended(adjoint, (("lat", 2),), 1, False)
-        north_side = upright[:, :, 2:, :]
-        south_side = upright[:, :, :-2, :]
-        edge_row = jnp.where(lat_place == 0, adjoint[:, :, :1, :], adjoint[:, :, -1:, :])
-        partner_row = from_behind(edge_row, "lon", lon_count // 2)
-        north_side = jnp.where(at_top, partner_row, north_side)
-        south_side = jnp.where(at_bottom, partner_row, south_side)
+        planes = tracers * lev_dev
+        west_halo, east_halo, north_halo, south_halo = halo_swap(
+            adjoint[:, :, :, -1].reshape(planes, lat_rows),
+            adjoint[:, :, :, 0].reshape(planes, lat_rows),
+            adjoint[:, :, -1, :].reshape(planes, lon_cols),
+            adjoint[:, :, 0, :].reshape(planes, lon_cols),
+            2 + position,
+        )
+        east_side = jnp.concatenate(
+            [adjoint[:, :, :, 1:], east_halo.reshape(tracers, lev_dev, lat_rows, 1)], axis=3
+        )
+        west_side = jnp.concatenate(
+            [west_halo.reshape(tracers, lev_dev, lat_rows, 1), adjoint[:, :, :, :-1]], axis=3
+        )
+        north_side = jnp.concatenate(
+            [adjoint[:, :, 1:, :], north_halo.reshape(tracers, lev_dev, 1, lon_cols)], axis=2
+        )
+        south_side = jnp.concatenate(
+            [south_halo.reshape(tracers, lev_dev, 1, lon_cols), adjoint[:, :, :-1, :]], axis=2
+        )
         adjoint = (
             adjoint
             + upwind_east * (east_side - adjoint)

time: 163 us -> 145 us (0.89)
  starting transfers between devices: 55.7 us -> 26.1 us
  waiting for transfers between devices: 24.8 us -> 5.67 us
  Pallas kernels: 53.5 us -> 70 us
  local copies, waits for them, and re-layouts: 10.8 us -> 22.7 us
  other arithmetic: 11.4 us -> 14.2 us
    ppermute x8 -> x0, starting transfers between devices: 28.2 us -> none  [the longest x4 17.3 us: extended(): after = lax.ppermute(initial, axis, down)]
    all_to_all x1, waiting for transfers between devices: 18.6 us -> 0.01 us  [on_device(): arrived = lax.all_to_all(packed, ('lon', 'lat'), 0, 0, tiled=True)]
    pallas_call x0 -> x2, Pallas kernels: none -> 16.2 us  [halo_swap(): pl.pallas_call(functools.partial(halo_body, lon_n, lat_n), out_shape=(jax...]
    reshape x0 -> x8, local copies, waits for them, and re-layouts: none -> 8.51 us  [the longest x2 2.66 us: on_device(): east_halo.reshape(tracers, lev_dev, lat_rows, 1)]
    ppermute x8 -> x0, waiting for transfers between devices: 6.26 us -> none  [the longest x4 5.48 us: extended(): before = lax.ppermute(last, axis, up)]
    all_to_all x1, starting transfers between devices: 8.66 us -> 14.4 us  [on_device(): arrived = lax.all_to_all(packed, ('lon', 'lat'), 0, 0, tiled=True)]
    ppermute x4 -> x2, waiting for transfers between devices: 0.01 us -> 5.67 us  [from_behind(): return lax.ppermute(value, axis, pairs)]
    ppermute x4 -> x2, starting transfers between devices: 13.5 us -> 8.22 us  [from_behind(): return lax.ppermute(value, axis, pairs)]
  transfers between devices with their start and end apart: 14 -> 4, of which waited for: 3 -> 1; matrix products, arithmetic and copies ran while one was open for 7% -> 2% of each run, Pallas kernels for 0% -> 0%
where the time goes in v3:
time: 145 us; the launch traced here: 144 us
  Pallas kernels  70 us (48%)
  starting transfers between devices  26.1 us (18%)
  local copies, waits for them, and re-layouts  22.7 us (16%)
  other arithmetic  14.2 us (10%)
  waiting for transfers between devices  5.67 us (4%)
  matrix products  4.78 us (3%)
    pallas_call x2, Pallas kernels, lev_sum(): pl.pallas_call(functools.partial(lev_sum_body, n), out_shape=jax.ShapeDty...  53.7 us
    pallas_call x2, Pallas kernels, halo_swap(): pl.pallas_call(functools.partial(halo_body, lon_n, lat_n), out_shape=(jax...  16.2 us
    all_to_all x1, starting transfers between devices, on_device(): arrived = lax.all_to_all(packed, ('lon', 'lat'), 0, 0, tiled=True)  14.4 us
    ppermute x2, starting transfers between devices, from_behind(): return lax.ppermute(value, axis, pairs)  8.22 us
    ppermute x2, waiting for transfers between devices, from_behind(): return lax.ppermute(value, axis, pairs)  5.67 us
    dot_general x1, matrix products, on_device(): jnp.einsum('tke,tec->tkc', arrived[:, :lev_dev, :], hit, precision=lax.Pr...  4.78 us
    ppermute x1, starting transfers between devices, from_behind_2(): return lax.ppermute(block, axis, route)  3.54 us
  transfers between devices with their start and end apart: 4, of which 1 were waited for; matrix products, arithmetic and copies ran while one was open for 2% of the time, Pallas kernels for 0%

profile of v3, /device:TPU:1, one launch (start us, length us, event | category | flops | bytes accessed | tf_op | source)
XLA Modules:
  0.0 143.9 jit_solution(16974948001091311228)
XLA Ops:
  0.0 0.7 copy.81
  0.9 0.7 fusion.29
  1.8 0.7 iota_compare_fusion.2
  2.5 0.7 broadcast_select_fusion
  4.5 1.2 copy.52
  5.7 14.4 %all-to-all-start = ((f32[128,2,4,4]{3,1,2,0:T(2,128)}), f32[128,2,4,4]{3,1,2,0:T(2,128)S(1)}, u32[]{:S(2)}, u32[]{:S(2)}) async-start(f32[128,2,4,4]{3,1,2,0:T(2,128)} %copy.52), calls=%async_computation | async-start | bytes 1048576 | tf_op jit(solution)/shard_map/all_to_all | solution.py:216
  20.1 3.5 %collective-permute-start.2 = (f32[3,1,128]{2,0,1:T(4,128)S(1)}, f32[3,1,128]{2,0,1:T(4,128)S(1)}, u32[]{:S(2)}, u32[]{:S(2)}) collective-permute-start(f32[3,1,128]{2,0,1:T(4,128)S(1)} %copy.82), channel_id=1, source_target_pairs={{0,4},{4,8},{8,12},{1,5},{5,9},{9,13},{2,6},{6,10},{10,14},{3,7},{... | collective-permute-start | bytes 4616 | tf_op jit(solution)/shard_map/ppermute | solution.py:155
  23.7 4.9 %collective-permute-start.1 = (f32[2,3,128]{2,1,0:T(4,128)S(1)}, f32[2,3,128]{2,1,0:T(4,128)S(1)}, u32[]{:S(2)}, u32[]{:S(2)}) collective-permute-start(f32[2,3,128]{2,1,0:T(4,128)S(1)} %pad_maximum_fusion.1), channel_id=1, source_target_pairs={{0,256},{16,272},{32,288},{48,304},{64,320},{80,336},{96,352},{112... | collective-permute-start | bytes 9224 | tf_op jit(solution)/shard_map/ppermute | solution.py:149
  28.7 3.3 %collective-permute-start = (f32[3,32,1]{2,1,0:T(8,128)S(1)}, f32[3,32,1]{2,1,0:T(8,128)S(1)}, u32[]{:S(2)}, u32[]{:S(2)}) collective-permute-start(f32[3,32,1]{2,1,0:T(8,128)S(1)} %slice.97), channel_id=1, source_target_pairs={{0,16},{16,32},{32,48},{48,64},{64,80},{80,96},{96,112},{112,128},... | collective-permute-start | bytes 1160 | tf_op jit(solution)/shard_map/ppermute | solution.py:149
  32.7 5.7 %collective-permute-done = f32[3,32,1]{2,1,0:T(8,128)S(1)} collective-permute-done((f32[3,32,1]{2,1,0:T(8,128)S(1)}, f32[3,32,1]{2,1,0:T(8,128)S(1)}, u32[]{:S(2)}, u32[]{:S(2)}) %collective-permute-start) | collective-permute-done | bytes 416 | tf_op jit(solution)/shard_map/ppermute | solution.py:149
  38.4 0.7 fusion.21
  39.1 0.7 select_add_fusion
  39.8 0.7 fusion.23
  40.9 4.8 %fusion = f32[2,3,4096]{2,1,0:T(4,128)S(1)} fusion(f32[4096]{0:T(1024)S(1)} %iota_convert_fusion, f32[2,512]{1,0:T(2,128)S(1)} %bitcast.52, f32[2,4,512]{2,1,0:T(4,128)S(1)} %reshape.165), kind=kOutput, calls=%fused_computation | convolution fusion | flops 155189248 | bytes 135168 | tf_op jit(solution)/shard_map/tke,tec->tkc/dot_general | solution.py:222
  45.7 0.6 copy_bitcast_fusion
  46.4 0.7 pad_maximum_fusion.part_ref
  47.1 31.5 %shard_map.100 = f32[13,32,128]{2,1,0:T(8,128)} custom-call(f32[13,32,128]{2,1,0:T(8,128)} %pad_maximum_fusion.part_ref), custom_call_target="tpu_custom_call" | custom-call | tf_op jit(solution)/shard_map/pallas_call | solution.py:130
  78.6 0.7 slice_bitcast_fusion.2
  79.4 0.9 slice_divide_fusion
  81.9 1.1 fusion.34
  85.5 8.1 %shard_map.101 = (f32[36,32]{1,0:T(8,128)}, f32[36,32]{1,0:T(8,128)}, f32[36,128]{1,0:T(8,128)}, f32[36,128]{1,0:T(8,128)}) custom-call(f32[36,32]{1,0:T(8,128)} %reshape_squeeze.24.col_last, f32[36,32]{1,0:T(8,128)} %reshape_squeeze.25.col_first, f32[36,128]{1,0:T(8,128)} %reshape_squeeze.26.row_last, f32[36,128]{1,0:T(8,128)} %reshape_squeeze.27.row_first), custom_call_target="tpu_custom_call" | custom-call | tf_op jit(solution)/shard_map/pallas_call | solution.py:105
  93.7 1.3 reshape.174
  96.9 2.8 %multiply_reduce_fusion = (f32[12,32,128]{2,1,0:T(8,128)}, f32[12,3,32,128]{3,2,1,0:T(8,128)S(1)}) fusion(f32[3,32,128]{2,1,0:T(8,128)} %param.15, f32[3,32,128]{2,1,0:T(8,128)} %get-tuple-element.43, f32[12,3,31,128]{3,2,1,0:T(8,128)} %get-tuple-element.38, f32[12,3,1,128]{3,2,1,0:T(1,128)} %reshape.177, f32[3,32,128]{2,1,0:T(8,128)} %fusion.23, ...), kind=kLoop, calls=%fused_computation.37 | loop fusion | flops 3342336 | bytes 4374528 | tf_op jit(solution)/shard_map/reduce_sum | solution.py:250
  99.6 22.2 %shard_map.102 = f32[12,32,128]{2,1,0:T(8,128)} custom-call(f32[12,32,128]{2,1,0:T(8,128)} %get-tuple-element.29.part_ref), custom_call_target="tpu_custom_call" | custom-call | tf_op jit(solution)/shard_map/pallas_call | solution.py:130
  121.9 0.9 broadcast_divide_fusion
  123.6 1.0 fusion.32
  127.8 8.1 %shard_map.103 = (f32[36,32]{1,0:T(8,128)}, f32[36,32]{1,0:T(8,128)}, f32[36,128]{1,0:T(8,128)}, f32[36,128]{1,0:T(8,128)}) custom-call(f32[36,32]{1,0:T(8,128)} %reshape_squeeze.28.col_last, f32[36,32]{1,0:T(8,128)} %reshape_squeeze.29.col_first, f32[36,128]{1,0:T(8,128)} %reshape_squeeze.30.row_last, f32[36,128]{1,0:T(8,128)} %reshape_squeeze.31.row_first), custom_call_target="tpu_custom_call" | custom-call | tf_op jit(solution)/shard_map/pallas_call | solution.py:105
  135.9 1.3 reshape.178
  137.3 1.3 reshape.179
  138.6 1.3 reshape.180
  139.9 1.3 reshape.181
  141.3 2.6 %fusion.17 = f32[12,3,32,128]{3,2,1,0:T(8,128)} fusion(f32[12,3,32,1]{3,2,1,0:T(8,128)S(1)} %reshape.178, f32[12,3,32,127]{3,2,1,0:T(8,128)} %get-tuple-element.34, f32[12,3,32,127]{3,2,1,0:T(8,128)S(1)} %get-tuple-element.33, f32[12,3,32,1]{3,2,1,0:T(8,128)S(1)} %reshape.179, f32[12,3,1,128]{3,2,1,0:T(1,128)} %reshape.180, ...), kind=kLoop, calls=%fused_computation.29 | loop fusion | flops 2801664 | bytes 4030464 | tf_op jit(solution)/shard_map/add | solution.py:282
  (85 shorter events, 12.6 us)
Async XLA Ops:
  0.0 4.0 %copy-start.15 = (s32[2,256]{1,0:T(2,128)S(1)}, s32[2,256]{1,0:T(2,128)}, u32[]{:S(2)}) copy-start(s32[2,256]{1,0:T(2,128)} %param.17) | copy-start | bytes 6148
  5.7 14.4 %copy-start.10 = (f32[3,32,128]{2,1,0:T(8,128)S(1)}, f32[3,32,128]{2,1,0:T(8,128)}, u32[]{:S(2)}) copy-start(f32[3,32,128]{2,1,0:T(8,128)} %param.12) | copy-start | bytes 147460
  5.7 18.0 %copy-start.14 = (f32[3,128]{1,0:T(4,128)S(1)}, f32[3,128]{1,0:T(4,128)}, u32[]{:S(2)}) copy-start(f32[3,128]{1,0:T(4,128)} %param.13) | copy-start | bytes 4612
  5.7 22.9 %copy-start.9 = (f32[3,32,128]{2,1,0:T(8,128)S(1)}, f32[3,32,128]{2,1,0:T(8,128)}, u32[]{:S(2)}) copy-start(f32[3,32,128]{2,1,0:T(8,128)} %param.11) | copy-start | bytes 147460
  5.7 26.9 %copy-start.3 = (f32[3,32,128]{2,1,0:T(8,128)S(1)}, f32[3,32,128]{2,1,0:T(8,128)}, u32[]{:S(2)}) copy-start(f32[3,32,128]{2,1,0:T(8,128)} %param.14) | copy-start | bytes 147460
  5.7 27.0 %copy-start.8 = (f32[3,32,128]{2,1,0:T(8,128)S(1)}, f32[3,32,128]{2,1,0:T(8,128)}, u32[]{:S(2)}) copy-start(f32[3,32,128]{2,1,0:T(8,128)} %param.15) | copy-start | bytes 147460
  5.7 34.8 %all-to-all-start = ((f32[128,2,4,4]{3,1,2,0:T(2,128)}), f32[128,2,4,4]{3,1,2,0:T(2,128)S(1)}, u32[]{:S(2)}, u32[]{:S(2)}) async-start(f32[128,2,4,4]{3,1,2,0:T(2,128)} %copy.52), calls=%async_computation | async-start | bytes 1048576 | tf_op jit(solution)/shard_map/all_to_all | solution.py:216
  20.1 19.0 %collective-permute-start.2 = (f32[3,1,128]{2,0,1:T(4,128)S(1)}, f32[3,1,128]{2,0,1:T(4,128)S(1)}, u32[]{:S(2)}, u32[]{:S(2)}) collective-permute-start(f32[3,1,128]{2,0,1:T(4,128)S(1)} %copy.82), channel_id=1, source_target_pairs={{0,4},{4,8},{8,12},{1,5},{5,9},{9,13},{2,6},{6,10},{10,14},{3,7},{... | collective-permute-start | bytes 4616 | tf_op jit(solution)/shard_map/ppermute | solution.py:155
  23.7 15.4 %collective-permute-start.1 = (f32[2,3,128]{2,1,0:T(4,128)S(1)}, f32[2,3,128]{2,1,0:T(4,128)S(1)}, u32[]{:S(2)}, u32[]{:S(2)}) collective-permute-start(f32[2,3,128]{2,1,0:T(4,128)S(1)} %pad_maximum_fusion.1), channel_id=1, source_target_pairs={{0,256},{16,272},{32,288},{48,304},{64,320},{80,336},{96,352},{112... | collective-permute-start | bytes 9224 | tf_op jit(solution)/shard_map/ppermute | solution.py:149
  28.7 9.7 %collective-permute-start = (f32[3,32,1]{2,1,0:T(8,128)S(1)}, f32[3,32,1]{2,1,0:T(8,128)S(1)}, u32[]{:S(2)}, u32[]{:S(2)}) collective-permute-start(f32[3,32,1]{2,1,0:T(8,128)S(1)} %slice.97), channel_id=1, source_target_pairs={{0,16},{16,32},{32,48},{48,64},{64,80},{80,96},{96,112},{112,128},... | collective-permute-start | bytes 1160 | tf_op jit(solution)/shard_map/ppermute | solution.py:149
  32.6 47.7 %copy-start.5 = (f32[3,32,128]{2,1,0:T(8,128)}, f32[3,32,128]{2,1,0:T(8,128)S(1)}, u32[]{:S(2)}) copy-start(f32[3,32,128]{2,1,0:T(8,128)S(1)} %broadcast_subtract_fusion) | copy-start | bytes 147460
  40.9 5.5 %copy-start = (f32[12,3,32,128]{3,2,1,0:T(8,128)S(1)}, f32[12,3,32,128]{3,2,1,0:T(8,128)}, u32[]{:S(2)}) copy-start(f32[12,3,32,128]{3,2,1,0:T(8,128)} %param.10) | copy-start | bytes 1769476
  46.3 34.0 %copy-start.7 = (f32[3,32,128]{2,1,0:T(8,128)}, f32[3,32,128]{2,1,0:T(8,128)S(1)}, u32[]{:S(2)}) copy-start(f32[3,32,128]{2,1,0:T(8,128)S(1)} %get-tuple-element.44) | copy-start | bytes 147460
  80.3 0.7 copy-start.1
  93.6 1.4 copy-start.11
  93.6 2.0 %copy-start.13 = (f32[36,128]{1,0:T(8,128)S(1)}, f32[36,128]{1,0:T(8,128)}, u32[]{:S(2)}) copy-start(f32[36,128]{1,0:T(8,128)} %get-tuple-element.15) | copy-start | bytes 55300
  93.6 2.6 %copy-start.12 = (f32[36,128]{1,0:T(8,128)S(1)}, f32[36,128]{1,0:T(8,128)}, u32[]{:S(2)}) copy-start(f32[36,128]{1,0:T(8,128)} %get-tuple-element.16) | copy-start | bytes 55300
  99.6 23.2 %copy-start.4 = (f32[3,32,128]{2,1,0:T(8,128)S(1)}, f32[3,32,128]{2,1,0:T(8,128)}, u32[]{:S(2)}) copy-start(f32[3,32,128]{2,1,0:T(8,128)} %param.14) | copy-start | bytes 147460
  99.6 23.2 %copy-start.6 = (f32[3,32,128]{2,1,0:T(8,128)S(1)}, f32[3,32,128]{2,1,0:T(8,128)}, u32[]{:S(2)}) copy-start(f32[3,32,128]{2,1,0:T(8,128)} %copy-done.5) | copy-start | bytes 147460
  122.8 0.7 copy-start.2

commit v4 on v3

--- a/solution.py
+++ b/solution.py
@@ -223,25 +223,10 @@
         "tke,tec->tkc", arrived[:, :lev_dev, :], hit, precision=lax.Precision.HIGHEST
     )
     forcing_grid = forcing_grid.reshape(step_count, lev_dev, lat_rows, lon_cols)
-    west_column = from_behind(east_courant[:, :, -1:], "lon", 1)
-    west_wind = jnp.concatenate([west_column, east_courant[:, :, :-1]], axis=2)
-    south_row = from_behind_2(north_courant[:, -1:, :], "lat", 1)
-    south_wind = jnp.concatenate([south_row, north_courant[:, :-1, :]], axis=1)
-    pole_pair = jnp.stack([north_courant[:, -1, :], pole_courant], axis=0)
-    partner_winds = from_behind(pole_pair, "lon", lon_count // 2)
     row_index = jnp.arange(lat_rows, dtype=jnp.int32)[None, :, None]
     at_top = jnp.logical_and(lat_place == lat_count - 1, row_index == lat_rows - 1)
     at_bottom = jnp.logical_and(lat_place == 0, row_index == 0)
     upwind_east = jnp.maximum(east_courant, 0.0)
-    upwind_west = -jnp.minimum(west_wind, 0.0)
-    upwind_north = jnp.maximum(north_courant, 0.0) + jnp.where(
-        at_top, -jnp.minimum(partner_winds[0], 0.0)[:, None, :], 0.0
-    )
-    upwind_south = jnp.where(
-        at_bottom,
-        (jnp.maximum(pole_courant, 0.0) - jnp.minimum(partner_winds[1], 0.0))[:, None, :],
-        -jnp.minimum(south_wind, 0.0),
-    )
     detrain_part = jnp.sum(detrain_share, axis=0)
     adjoint = adjoint_field
     for position in range(step_count):
@@ -259,13 +244,38 @@
             column_sum / total_detrain
         )[:, None]
         planes = tracers * lev_dev
+        col_last = adjoint[:, :, :, -1].reshape(planes, lat_rows)
+        col_first = adjoint[:, :, :, 0].reshape(planes, lat_rows)
+        row_last = adjoint[:, :, -1, :].reshape(planes, lon_cols)
+        row_first = adjoint[:, :, 0, :].reshape(planes, lon_cols)
+        if position == 0:
+            col_last = jnp.concatenate([col_last, east_courant[:, :, -1]], axis=0)
+            col_first = jnp.concatenate([col_first, east_courant[:, :, 0]], axis=0)
+            row_last = jnp.concatenate([row_last, north_courant[:, -1, :]], axis=0)
+            row_first = jnp.concatenate([row_first, pole_courant], axis=0)
         west_halo, east_halo, north_halo, south_halo = halo_swap(
-            adjoint[:, :, :, -1].reshape(planes, lat_rows),
-            adjoint[:, :, :, 0].reshape(planes, lat_rows),
-            adjoint[:, :, -1, :].reshape(planes, lon_cols),
-            adjoint[:, :, 0, :].reshape(planes, lon_cols),
-            2 + position,
-        )
+            col_last, col_first, row_last, row_first, 2 + position
+        )
+        if position == 0:
+            west_wind = jnp.concatenate(
+                [west_halo[planes:, :, None], east_courant[:, :, :-1]], axis=2
+            )
+            partner_top = north_halo[planes:]
+            south_wind = jnp.concatenate(
+                [south_halo[planes:, None, :], north_courant[:, :-1, :]], axis=1
+            )
+            partner_pole = south_halo[planes:]
+            upwind_west = -jnp.minimum(west_wind, 0.0)
+            upwind_north = jnp.maximum(north_courant, 0.0) + jnp.where(
+                at_top, -jnp.minimum(partner_top, 0.0)[:, None, :], 0.0
+            )
+            upwind_south = jnp.where(
+                at_bottom,
+                (jnp.maximum(pole_courant, 0.0) - jnp.minimum(partner_pole, 0.0))[:, None, :],
+                -jnp.minimum(south_wind, 0.0),
+            )
+            west_halo, east_halo = west_halo[:planes], east_halo[:planes]
+            north_halo, south_halo = north_halo[:planes], south_halo[:planes]
         east_side = jnp.concatenate(
             [adjoint[:, :, :, 1:], east_halo.reshape(tracers, lev_dev, lat_rows, 1)], axis=3
         )

time: 145 us -> 146 us (level)
  waiting for transfers between devices: 5.67 us -> 18 us
  starting transfers between devices: 26.1 us -> 14.4 us
  local copies, waits for them, and re-layouts: 22.7 us -> 20.7 us
  Pallas kernels: 70 us -> 71.8 us
    all_to_all x1, waiting for transfers between devices: 0.01 us -> 18 us  [on_device(): arrived = lax.all_to_all(packed, ('lon', 'lat'), 0, 0, tiled=True)]
    ppermute x3 -> x0, starting transfers between devices: 11.8 us -> none  [the longest x2 8.22 us: from_behind(): return lax.ppermute(value, axis, pairs)]
    ppermute x3 -> x0, waiting for transfers between devices: 5.67 us -> none  [the longest x2 5.67 us: from_behind(): return lax.ppermute(value, axis, pairs)]
    concatenate x0 -> x4, other arithmetic: none -> 2.44 us  [the longest x1 0.62 us: on_device(): col_first = jnp.concatenate([col_first, east_courant[:, :, 0]], axis=0)]
    another operation x9 -> x8, local copies, waits for them, and re-layouts: 4.89 us -> 2.5 us  [the longest x2 0.63 us: on_device(): col_last = adjoint[:, :, :, -1].reshape(planes, lat_rows)]
    pallas_call x2, Pallas kernels: 53.7 us -> 55.6 us  [lev_sum(): pl.pallas_call(functools.partial(lev_sum_body, n), out_shape=jax.ShapeDty...]
  transfers between devices with their start and end apart: 4 -> 1, of which waited for: 1 -> 1; matrix products, arithmetic and copies ran while one was open for 2% -> 1% of each run, Pallas kernels for 0% -> 0%
where the time goes in v4:
time: 146 us; the launch traced here: 145 us
  Pallas kernels  71.8 us (49%)
  local copies, waits for them, and re-layouts  20.7 us (14%)
  waiting for transfers between devices  18 us (12%)
  other arithmetic  14.7 us (10%)
  starting transfers between devices  14.4 us (10%)
  matrix products  4.78 us (3%)
    pallas_call x2, Pallas kernels, lev_sum(): pl.pallas_call(functools.partial(lev_sum_body, n), out_shape=jax.ShapeDty...  55.6 us
    all_to_all x1, waiting for transfers between devices, on_device(): arrived = lax.all_to_all(packed, ('lon', 'lat'), 0, 0, tiled=True)  18 us
    pallas_call x2, Pallas kernels, halo_swap(): pl.pallas_call(functools.partial(halo_body, lon_n, lat_n), out_shape=(jax...  16.2 us
    all_to_all x1, starting transfers between devices, on_device(): arrived = lax.all_to_all(packed, ('lon', 'lat'), 0, 0, tiled=True)  14.4 us
    dot_general x1, matrix products, on_device(): jnp.einsum('tke,tec->tkc', arrived[:, :lev_dev, :], hit, precision=lax.Pr...  4.78 us
  transfers between devices with their start and end apart: 1, of which 1 were waited for; matrix products, arithmetic and copies ran while one was open for 1% of the time, Pallas kernels for 0%

profile of v4, /device:TPU:1, one launch (start us, length us, event | category | flops | bytes accessed | tf_op | source)
XLA Modules:
  0.0 144.8 jit_solution(14122577346500223232)
XLA Ops:
  0.0 0.7 copy.85
  0.9 0.7 fusion.25
  1.8 0.7 iota_compare_fusion.2
  2.5 0.7 broadcast_select_fusion
  4.5 1.2 copy.55
  5.7 14.4 %all-to-all-start = ((f32[128,2,4,4]{3,1,2,0:T(2,128)}), f32[128,2,4,4]{3,1,2,0:T(2,128)S(1)}, u32[]{:S(2)}, u32[]{:S(2)}) async-start(f32[128,2,4,4]{3,1,2,0:T(2,128)} %copy.55), calls=%async_computation | async-start | bytes 1048576 | tf_op jit(solution)/shard_map/all_to_all | solution.py:216
  20.2 0.6 broadcast_maximum_fusion
  21.0 18.0 %all-to-all-done = f32[128,2,4,4]{3,1,2,0:T(2,128)S(1)} async-done(((f32[128,2,4,4]{3,1,2,0:T(2,128)}), f32[128,2,4,4]{3,1,2,0:T(2,128)S(1)}, u32[]{:S(2)}, u32[]{:S(2)}) %all-to-all-start) | async-done | bytes 16416 | tf_op jit(solution)/shard_map/all_to_all | solution.py:216
  39.4 4.8 %fusion = f32[2,3,4096]{2,1,0:T(4,128)S(1)} fusion(f32[4096]{0:T(1024)S(1)} %iota_convert_fusion, f32[2,512]{1,0:T(2,128)S(1)} %bitcast.56, f32[2,4,512]{2,1,0:T(4,128)S(1)} %reshape.157), kind=kOutput, calls=%fused_computation | convolution fusion | flops 155189248 | bytes 135168 | tf_op jit(solution)/shard_map/tke,tec->tkc/dot_general | solution.py:222
  44.2 0.6 copy_bitcast_fusion
  44.9 0.7 pad_maximum_fusion.part_ref
  45.6 31.6 %shard_map.100 = f32[13,32,128]{2,1,0:T(8,128)} custom-call(f32[13,32,128]{2,1,0:T(8,128)} %pad_maximum_fusion.part_ref), custom_call_target="tpu_custom_call" | custom-call | tf_op jit(solution)/shard_map/pallas_call | solution.py:130
  77.2 0.7 slice_bitcast_fusion.2
  77.9 0.9 slice_divide_fusion
  80.5 1.1 fusion.30
  82.3 0.6 pad_maximum_fusion.2.col_first
  84.1 8.1 %shard_map.101 = (f32[39,32]{1,0:T(8,128)}, f32[39,32]{1,0:T(8,128)}, f32[39,128]{1,0:T(8,128)}, f32[39,128]{1,0:T(8,128)}) custom-call(f32[39,32]{1,0:T(8,128)} %pad_maximum_fusion.1.col_last, f32[39,32]{1,0:T(8,128)} %pad_maximum_fusion.2.col_first, f32[39,128]{1,0:T(8,128)} %pad_maximum_fusion.3.row_last, f32[39,128]{1,0:T(8,128)} %pad_maximum_fusion.4.row_first), custom_call_target="tpu_custom_call" | custom-call | tf_op jit(solution)/shard_map/pallas_call | solution.py:105
  92.3 1.3 reshape.166
  94.4 0.6 reshape.168
  95.0 0.6 reshape.169
  95.9 2.7 %multiply_reduce_fusion = (f32[12,32,128]{2,1,0:T(8,128)}, f32[12,3,32,128]{3,2,1,0:T(8,128)S(1)}) fusion(f32[3,32,128]{2,1,0:T(8,128)} %param.15, f32[3,32,128]{2,1,0:T(8,128)} %get-tuple-element.45, f32[12,3,31,128]{3,2,1,0:T(8,128)} %get-tuple-element.40, f32[12,3,1,128]{3,2,1,0:T(1,128)} %reshape.169, f32[3,32,128]{2,1,0:T(8,128)S(1)} %fusion.23, ...), kind=kLoop, calls=%fused_computation.37 | loop fusion | flops 3342336 | bytes 4374528 | tf_op jit(solution)/shard_map/reduce_sum | solution.py:235
  98.7 24.0 %shard_map.102 = f32[12,32,128]{2,1,0:T(8,128)} custom-call(f32[12,32,128]{2,1,0:T(8,128)} %get-tuple-element.31.part_ref), custom_call_target="tpu_custom_call" | custom-call | tf_op jit(solution)/shard_map/pallas_call | solution.py:130
  122.6 0.9 broadcast_divide_fusion
  123.6 0.7 copy-done.2
  124.5 1.0 fusion.28
  126.2 0.6 reshape_squeeze.28.col_last
  128.7 8.1 %shard_map.103 = (f32[36,32]{1,0:T(8,128)}, f32[36,32]{1,0:T(8,128)}, f32[36,128]{1,0:T(8,128)}, f32[36,128]{1,0:T(8,128)}) custom-call(f32[36,32]{1,0:T(8,128)} %reshape_squeeze.28.col_last, f32[36,32]{1,0:T(8,128)} %reshape_squeeze.29.col_first, f32[36,128]{1,0:T(8,128)} %reshape_squeeze.30.row_last, f32[36,128]{1,0:T(8,128)} %reshape_squeeze.31.row_first), custom_call_target="tpu_custom_call" | custom-call | tf_op jit(solution)/shard_map/pallas_call | solution.py:105
  136.8 1.3 reshape.170
  138.1 1.3 reshape.171
  139.5 1.3 reshape.172
  140.8 1.3 reshape.173
  142.2 2.6 %fusion.17 = f32[12,3,32,128]{3,2,1,0:T(8,128)} fusion(f32[12,3,32,1]{3,2,1,0:T(8,128)S(1)} %reshape.170, f32[12,3,32,127]{3,2,1,0:T(8,128)} %get-tuple-element.36, f32[12,3,32,127]{3,2,1,0:T(8,128)S(1)} %get-tuple-element.35, f32[12,3,32,1]{3,2,1,0:T(8,128)S(1)} %reshape.171, f32[12,3,1,128]{3,2,1,0:T(1,128)} %reshape.172, ...), kind=kLoop, calls=%fused_computation.29 | loop fusion | flops 2801664 | bytes 4030464 | tf_op jit(solution)/shard_map/add | solution.py:292
  (90 shorter events, 9.5 us)
Async XLA Ops:
  0.0 4.0 %copy-start.18 = (s32[2,256]{1,0:T(2,128)S(1)}, s32[2,256]{1,0:T(2,128)}, u32[]{:S(2)}) copy-start(s32[2,256]{1,0:T(2,128)} %param.17) | copy-start | bytes 6148
  5.7 14.4 %copy-start.8 = (f32[3,32,128]{2,1,0:T(8,128)S(1)}, f32[3,32,128]{2,1,0:T(8,128)}, u32[]{:S(2)}) copy-start(f32[3,32,128]{2,1,0:T(8,128)} %param.11) | copy-start | bytes 147460
  5.7 15.2 %copy-start.3 = (f32[3,32,128]{2,1,0:T(8,128)S(1)}, f32[3,32,128]{2,1,0:T(8,128)}, u32[]{:S(2)}) copy-start(f32[3,32,128]{2,1,0:T(8,128)} %param.14) | copy-start | bytes 147460
  5.7 15.3 %copy-start.13 = (f32[3,32,128]{2,1,0:T(8,128)S(1)}, f32[3,32,128]{2,1,0:T(8,128)}, u32[]{:S(2)}) copy-start(f32[3,32,128]{2,1,0:T(8,128)} %param.12) | copy-start | bytes 147460
  5.7 15.3 %copy-start.12 = (f32[3,32,128]{2,1,0:T(8,128)S(1)}, f32[3,32,128]{2,1,0:T(8,128)}, u32[]{:S(2)}) copy-start(f32[3,32,128]{2,1,0:T(8,128)} %param.15) | copy-start | bytes 147460
  5.7 33.3 %all-to-all-start = ((f32[128,2,4,4]{3,1,2,0:T(2,128)}), f32[128,2,4,4]{3,1,2,0:T(2,128)S(1)}, u32[]{:S(2)}, u32[]{:S(2)}) async-start(f32[128,2,4,4]{3,1,2,0:T(2,128)} %copy.55), calls=%async_computation | async-start | bytes 1048576 | tf_op jit(solution)/shard_map/all_to_all | solution.py:216
  20.9 58.0 %copy-start.5 = (f32[3,32,128]{2,1,0:T(8,128)}, f32[3,32,128]{2,1,0:T(8,128)S(1)}, u32[]{:S(2)}) copy-start(f32[3,32,128]{2,1,0:T(8,128)S(1)} %broadcast_subtract_fusion) | copy-start | bytes 147460
  39.4 5.5 %copy-start = (f32[12,3,32,128]{3,2,1,0:T(8,128)S(1)}, f32[12,3,32,128]{3,2,1,0:T(8,128)}, u32[]{:S(2)}) copy-start(f32[12,3,32,128]{3,2,1,0:T(8,128)} %param.10) | copy-start | bytes 1769476
  44.8 34.0 %copy-start.7 = (f32[3,32,128]{2,1,0:T(8,128)}, f32[3,32,128]{2,1,0:T(8,128)S(1)}, u32[]{:S(2)}) copy-start(f32[3,32,128]{2,1,0:T(8,128)S(1)} %get-tuple-element.46) | copy-start | bytes 147460
  78.9 0.7 copy-start.1
  80.5 3.0 %copy-start.17 = (f32[3,128]{1,0:T(4,128)S(1)}, f32[3,128]{1,0:T(4,128)}, u32[]{:S(2)}) copy-start(f32[3,128]{1,0:T(4,128)} %param.13) | copy-start | bytes 4612
  92.3 1.4 copy-start.14
  92.3 2.1 %copy-start.15 = (f32[39,128]{1,0:T(8,128)S(1)}, f32[39,128]{1,0:T(8,128)}, u32[]{:S(2)}) copy-start(f32[39,128]{1,0:T(8,128)} %get-tuple-element.16) | copy-start | bytes 59908
  92.3 2.1 %copy-start.16 = (f32[39,128]{1,0:T(8,128)S(1)}, f32[39,128]{1,0:T(8,128)}, u32[]{:S(2)}) copy-start(f32[39,128]{1,0:T(8,128)} %get-tuple-element.15) | copy-start | bytes 59908
  95.7 2.9 %copy-start.11 = (f32[3,32,128]{2,1,0:T(8,128)}, f32[3,32,128]{2,1,0:T(8,128)S(1)}, u32[]{:S(2)}) copy-start(f32[3,32,128]{2,1,0:T(8,128)S(1)} %fusion.21) | copy-start | bytes 147460
  95.8 2.8 %copy-start.9 = (f32[3,32,128]{2,1,0:T(8,128)}, f32[3,32,128]{2,1,0:T(8,128)S(1)}, u32[]{:S(2)}) copy-start(f32[3,32,128]{2,1,0:T(8,128)S(1)} %select_add_fusion) | copy-start | bytes 147460
  95.9 2.7 %copy-start.10 = (f32[3,32,128]{2,1,0:T(8,128)}, f32[3,32,128]{2,1,0:T(8,128)S(1)}, u32[]{:S(2)}) copy-start(f32[3,32,128]{2,1,0:T(8,128)S(1)} %fusion.23) | copy-start | bytes 147460
  98.6 25.6 %copy-start.4 = (f32[3,32,128]{2,1,0:T(8,128)S(1)}, f32[3,32,128]{2,1,0:T(8,128)}, u32[]{:S(2)}) copy-start(f32[3,32,128]{2,1,0:T(8,128)} %param.14) | copy-start | bytes 147460
  98.6 25.6 %copy-start.6 = (f32[3,32,128]{2,1,0:T(8,128)S(1)}, f32[3,32,128]{2,1,0:T(8,128)}, u32[]{:S(2)}) copy-start(f32[3,32,128]{2,1,0:T(8,128)} %copy-done.5) | copy-start | bytes 147460
  123.6 0.7 copy-start.2

commit v5 on v4

--- a/solution.py
+++ b/solution.py
@@ -125,6 +125,109 @@
     )(col_last, col_first, row_last, row_first)
 
 
+def exchange_body(lev_n, owners, lat_n, rows_ref, part_ref, rows_out, sum_out,
+                  got, slots, row_send, row_recv, lev_send, lev_recv):
+    lat = lax.axis_index("lat")
+    lev = lax.axis_index("lev")
+    me = lax.axis_index("lon") * lat_n + lat
+
+    def place(peer):
+        return {"lon": peer // lat_n, "lat": lax.rem(peer, lat_n)}
+
+    barrier = pltpu.get_barrier_semaphore()
+
+    def greet(d, carry):
+        peer = lax.rem(me + d, owners)
+        pl.semaphore_signal(barrier, inc=1, device_id=place(peer), device_id_type=MESH)
+        return carry
+
+    lax.fori_loop(1, owners, greet, 0)
+    for d in range(1, lev_n):
+        pl.semaphore_signal(
+            barrier, inc=1, device_id={"lev": lax.rem(lev + d, lev_n)}, device_id_type=MESH
+        )
+    pl.semaphore_wait(barrier, owners - 1 + lev_n - 1)
+    for d in range(1, lev_n):
+        pltpu.make_async_remote_copy(
+            src_ref=part_ref,
+            dst_ref=slots.at[lev],
+            send_sem=lev_send.at[d - 1],
+            recv_sem=lev_recv.at[lev],
+            device_id={"lev": lax.rem(lev + d, lev_n)},
+            device_id_type=MESH,
+        ).start()
+
+    def row_copy(peer, target):
+        return pltpu.make_async_remote_copy(
+            src_ref=rows_ref.at[pl.ds(peer, 1)],
+            dst_ref=got.at[pl.ds(target, 1)],
+            send_sem=row_send.at[peer],
+            recv_sem=row_recv.at[target],
+            device_id=place(peer),
+            device_id_type=MESH,
+        )
+
+    def send(d, carry):
+        row_copy(lax.rem(me + d, owners), me).start()
+        return carry
+
+    lax.fori_loop(1, owners, send, 0)
+    got[pl.ds(me, 1), :] = rows_ref[pl.ds(me, 1), :]
+    slots[lev] = part_ref[...]
+
+    def finish(d, carry):
+        source = lax.rem(me + owners - d, owners)
+        row_copy(lax.rem(me + d, owners), me).wait_send()
+        row_copy(source, source).wait_recv()
+        return carry
+
+    lax.fori_loop(1, owners, finish, 0)
+    for d in range(1, lev_n):
+        sender = lax.rem(lev + lev_n - d, lev_n)
+        copy = pltpu.make_async_remote_copy(
+            src_ref=part_ref,
+            dst_ref=slots.at[sender],
+            send_sem=lev_send.at[d - 1],
+            recv_sem=lev_recv.at[sender],
+            device_id={"lev": sender},
+            device_id_type=MESH,
+        )
+        copy.wait_recv()
+        copy.wait_send()
+    total = slots[0]
+    for s in range(1, lev_n):
+        total = total + slots[s]
+    sum_out[...] = total
+    rows_out[...] = got[...]
+
+
+def exchange(rows, part, collective_id):
+    lev_n = lax.axis_size("lev")
+    lat_n = lax.axis_size("lat")
+    owners = lax.axis_size("lon") * lat_n
+    vmem = pl.BlockSpec(memory_space=pltpu.VMEM)
+    return pl.pallas_call(
+        functools.partial(exchange_body, lev_n, owners, lat_n),
+        out_shape=(
+            jax.ShapeDtypeStruct(rows.shape, rows.dtype),
+            jax.ShapeDtypeStruct(part.shape, part.dtype),
+        ),
+        in_specs=[vmem, vmem],
+        out_specs=(vmem, vmem),
+        scratch_shapes=[
+            pltpu.VMEM(rows.shape, rows.dtype),
+            pltpu.VMEM((lev_n,) + part.shape, part.dtype),
+            pltpu.SemaphoreType.DMA((owners,)),
+            pltpu.SemaphoreType.DMA((owners,)),
+            pltpu.SemaphoreType.DMA((lev_n - 1,)),
+            pltpu.SemaphoreType.DMA((lev_n,)),
+        ],
+        compiler_params=pltpu.CompilerParams(
+            collective_id=collective_id, has_side_effects=True
+        ),
+    )(rows, part)
+
+
 def lev_sum(x, collective_id):
     n = lax.axis_size("lev")
     return pl.pallas_call(
@@ -139,6 +242,9 @@
         ],
         compiler_params=pltpu.CompilerParams(
             collective_id=collective_id, has_side_effects=True
+        ),
+        cost_estimate=pl.CostEstimate(
+            flops=n * x.size, bytes_accessed=(2 * n + 2) * x.size * 4, transcendentals=0
         ),
     )(x)
 
@@ -192,6 +298,7 @@
     step_count = sounding_forcing.shape[0]
     slot_count = sounding_forcing.shape[2]
     grid_cells = lat_rows * lon_cols
+    detrain_part = jnp.sum(detrain_share, axis=0)
     owner_count = lon_count * lat_count
     cap = 4
     live_slots = jnp.arange(slot_count, dtype=jnp.int32)[None, :] < sounding_count
@@ -213,7 +320,13 @@
     packed = jnp.concatenate([bucket_values, bucket_cell[:, None, :]], axis=1)
     packed = packed.reshape(step_count, lev_dev + 1, owner_count, cap)
     packed = jnp.transpose(packed, (2, 0, 1, 3))
-    arrived = lax.all_to_all(packed, ("lon", "lat"), 0, 0, tiled=True)
+    row_width = step_count * (lev_dev + 1) * cap
+    rows = jnp.pad(packed.reshape(owner_count, row_width), ((0, 0), (0, 128 - row_width)))
+    early_part = jnp.concatenate(
+        [jnp.sum(detrain_share[None] * adjoint_field, axis=1), detrain_part[None]], axis=0
+    )
+    arrived, early = exchange(rows, early_part, 0)
+    arrived = arrived[:, :row_width].reshape(owner_count, step_count, lev_dev + 1, cap)
     arrived = jnp.transpose(arrived, (1, 2, 0, 3)).reshape(
         step_count, lev_dev + 1, owner_count * cap
     )
@@ -227,18 +340,17 @@
     at_top = jnp.logical_and(lat_place == lat_count - 1, row_index == lat_rows - 1)
     at_bottom = jnp.logical_and(lat_place == 0, row_index == 0)
     upwind_east = jnp.maximum(east_courant, 0.0)
-    detrain_part = jnp.sum(detrain_share, axis=0)
+    forcing_part = jnp.sum(detrain_share * forcing_grid[step_count - 1], axis=0)
+    forcing_sum = lev_sum(forcing_part[None], 4)[0]
     adjoint = adjoint_field
     for position in range(step_count):
         step_now = step_count - 1 - position
         adjoint = adjoint + forcing_grid[step_now][None]
-        partial_sum = jnp.sum(detrain_share[None] * adjoint, axis=1)
         if position == 0:
-            reduced = lev_sum(
-                jnp.concatenate([partial_sum, detrain_part[None]], axis=0), 0
-            )
-            column_sum, total_detrain = reduced[:tracers], reduced[tracers]
+            column_sum = early[:tracers] + forcing_sum[None]
+            total_detrain = early[tracers]
         else:
+            partial_sum = jnp.sum(detrain_share[None] * adjoint, axis=1)
             column_sum = lev_sum(partial_sum, 1)
         adjoint = (1.0 - mix_fraction)[None] * adjoint + mix_fraction[None] * (
             column_sum / total_detrain

time: 146 us -> 132 us (0.904)
  Pallas kernels: 71.8 us -> 93.5 us
  waiting for transfers between devices: 18 us -> 0 us
  starting transfers between devices: 14.4 us -> 0 us
  local copies, waits for them, and re-layouts: 20.7 us -> 17.1 us
    pallas_call x0 -> x1, Pallas kernels: none -> 41.2 us  [exchange(): pl.pallas_call(functools.partial(exchange_body, lev_n, owners, lat_n), ou...]
    pallas_call x2, Pallas kernels: 55.6 us -> 36 us  [lev_sum(): pl.pallas_call(functools.partial(lev_sum_body, n), out_shape=jax.ShapeDty...]
    all_to_all x1 -> x0, waiting for transfers between devices: 18 us -> none  [on_device(): arrived = lax.all_to_all(packed, ('lon', 'lat'), 0, 0, tiled=True)]
    all_to_all x1 -> x0, starting transfers between devices: 14.4 us -> none  [on_device(): arrived = lax.all_to_all(packed, ('lon', 'lat'), 0, 0, tiled=True)]
  transfers between devices with their start and end apart: 1 -> 0, of which waited for: 1 -> 0; matrix products, arithmetic and copies ran while one was open for 1% -> 0% of each run, Pallas kernels for 0% -> 0%
where the time goes in v5:
time: 132 us; the launch traced here: 131 us
  Pallas kernels  93.5 us (71%)
  local copies, waits for them, and re-layouts  17.1 us (13%)
  other arithmetic  14.7 us (11%)
  matrix products  4.78 us (4%)
    pallas_call x1, Pallas kernels, exchange(): pl.pallas_call(functools.partial(exchange_body, lev_n, owners, lat_n), ou...  41.2 us
    pallas_call x2, Pallas kernels, lev_sum(): pl.pallas_call(functools.partial(lev_sum_body, n), out_shape=jax.ShapeDty...  36 us
    pallas_call x2, Pallas kernels, halo_swap(): pl.pallas_call(functools.partial(halo_body, lon_n, lat_n), out_shape=(jax...  16.3 us
    dot_general x1, matrix products, on_device(): jnp.einsum('tke,tec->tkc', arrived[:, :lev_dev, :], hit, precision=lax.Pr...  4.78 us
    reshape x2, local copies, waits for them, and re-layouts, on_device(): east_halo.reshape(tracers, lev_dev, lat_rows, 1)  2.65 us

profile of v5, /device:TPU:1, one launch (start us, length us, event | category | flops | bytes accessed | tf_op | source)
XLA Modules:
  0.0 130.6 jit_solution(7232604380295016692)
XLA Ops:
  0.0 0.7 copy.97
  0.9 0.7 fusion.25
  1.8 0.7 iota_compare_fusion.2
  2.5 0.7 broadcast_select_fusion
  4.8 0.6 pad.4.rows_ref
  5.5 0.7 pad_maximum_fusion.part_ref
  6.2 41.2 %shard_map.100 = (f32[128,128]{1,0:T(8,128)}, f32[13,32,128]{2,1,0:T(8,128)}) custom-call(f32[128,128]{1,0:T(8,128)} %pad.4.rows_ref, f32[13,32,128]{2,1,0:T(8,128)} %pad_maximum_fusion.part_ref), custom_call_target="tpu_custom_call" | custom-call | tf_op jit(solution)/shard_map/pallas_call | solution.py:209
  47.4 0.9 copy.63
  48.9 4.8 %fusion = f32[2,3,4096]{2,1,0:T(4,128)S(1)} fusion(f32[4096]{0:T(1024)S(1)} %iota_convert_fusion, f32[2,512]{1,0:T(2,128)S(1)} %bitcast.67, f32[2,4,512]{2,1,0:T(4,128)S(1)} %reshape.166), kind=kOutput, calls=%fused_computation | convolution fusion | flops 155189248 | bytes 135168 | tf_op jit(solution)/shard_map/tke,tec->tkc/dot_general | solution.py:335
  53.7 0.6 multiply_reduce_fusion.2
  54.4 11.1 %shard_map.101 = f32[1,32,128]{2,1,0:T(8,128)} custom-call(f32[1,32,128]{2,1,0:T(8,128)} %bitcast.57), custom_call_target="tpu_custom_call" | custom-call | flops 16384 | bytes 163840 | tf_op jit(solution)/shard_map/pallas_call | solution.py:233
  65.5 0.7 add_divide_fusion
  67.3 0.6 pad_maximum_fusion.1.col_last
  67.9 0.6 pad_maximum_fusion.2.col_first
  69.3 0.6 pad_maximum_fusion.4.row_first
  69.9 8.1 %shard_map.102 = (f32[39,32]{1,0:T(8,128)}, f32[39,32]{1,0:T(8,128)}, f32[39,128]{1,0:T(8,128)}, f32[39,128]{1,0:T(8,128)}) custom-call(f32[39,32]{1,0:T(8,128)} %pad_maximum_fusion.1.col_last, f32[39,32]{1,0:T(8,128)} %pad_maximum_fusion.2.col_first, f32[39,128]{1,0:T(8,128)} %pad_maximum_fusion.3.row_last, f32[39,128]{1,0:T(8,128)} %pad_maximum_fusion.4.row_first), custom_call_target="tpu_custom_call" | custom-call | tf_op jit(solution)/shard_map/pallas_call | solution.py:105
  78.1 1.3 %reshape.176 = f32[12,3,32,1]{3,2,1,0:T(8,128)S(1)} reshape(f32[36,32]{1,0:T(8,128)} %bitcast.64) | data formatting | bytes 9216 | tf_op jit(solution)/shard_map/reshape | solution.py:392
  81.1 1.4 %multiply_reduce_fusion = (f32[12,32,128]{2,1,0:T(8,128)}, f32[12,3,32,128]{3,2,1,0:T(8,128)S(1)}) fusion(f32[3,32,128]{2,1,0:T(8,128)S(1)} %copy-done.3, f32[3,32,128]{2,1,0:T(8,128)S(1)} %bitcast.54, f32[12,3,31,128]{3,2,1,0:T(8,128)S(1)} %get-tuple-element.46, f32[12,3,1,128]{3,2,1,0:T(1,128)S(1)} %reshape.179, f32[3,32,128]{2,1,0:T(8,128)S(1)} %fusion.23, ...), kind=kLoop, calls=%fused_computation.37 | loop fusion | flops 3342336 | bytes 4374528 | tf_op jit(solution)/shard_map/reduce_sum | solution.py:353
  82.5 25.0 %shard_map.103 = f32[12,32,128]{2,1,0:T(8,128)} custom-call(f32[12,32,128]{2,1,0:T(8,128)} %get-tuple-element.35.part_ref), custom_call_target="tpu_custom_call" | custom-call | flops 196608 | bytes 1966080 | tf_op jit(solution)/shard_map/pallas_call | solution.py:233
  107.5 1.6 %broadcast_divide_fusion = f32[12,32,128]{2,1,0:T(8,128)} fusion(f32[12,32,128]{2,1,0:T(8,128)} %shard_map.103, f32[32,128]{1,0:T(8,128)S(1)} %slice_bitcast_fusion.2), kind=kLoop, calls=%fused_computation.44 | loop fusion | flops 49152 | bytes 409600 | tf_op jit(solution)/shard_map/div | solution.py:356
  109.1 1.0 multiply_add_fusion
  110.2 1.0 fusion.28
  111.9 0.6 reshape_squeeze.28.col_last
  112.5 0.6 reshape_squeeze.29.col_first
  113.2 0.6 reshape_squeeze.30.row_last
  113.8 0.6 reshape_squeeze.31.row_first
  114.5 8.1 %shard_map.104 = (f32[36,32]{1,0:T(8,128)}, f32[36,32]{1,0:T(8,128)}, f32[36,128]{1,0:T(8,128)}, f32[36,128]{1,0:T(8,128)}) custom-call(f32[36,32]{1,0:T(8,128)} %reshape_squeeze.28.col_last, f32[36,32]{1,0:T(8,128)} %reshape_squeeze.29.col_first, f32[36,128]{1,0:T(8,128)} %reshape_squeeze.30.row_last, f32[36,128]{1,0:T(8,128)} %reshape_squeeze.31.row_first), custom_call_target="tpu_custom_call" | custom-call | tf_op jit(solution)/shard_map/pallas_call | solution.py:105
  122.6 1.3 %reshape.180 = f32[12,3,32,1]{3,2,1,0:T(8,128)S(1)} reshape(f32[36,32]{1,0:T(8,128)} %get-tuple-element.21) | data formatting | bytes 9216 | tf_op jit(solution)/shard_map/reshape | solution.py:392
  123.9 1.3 %reshape.181 = f32[12,3,32,1]{3,2,1,0:T(8,128)S(1)} reshape(f32[36,32]{1,0:T(8,128)} %get-tuple-element.22) | data formatting | bytes 9216 | tf_op jit(solution)/shard_map/reshape | solution.py:395
  125.2 1.4 %reshape.182 = f32[12,3,1,128]{3,2,1,0:T(1,128)} reshape(f32[36,128]{1,0:T(8,128)} %get-tuple-element.23) | data formatting | bytes 36864 | tf_op jit(solution)/shard_map/reshape | solution.py:398
  126.6 1.3 %reshape.183 = f32[12,3,1,128]{3,2,1,0:T(1,128)} reshape(f32[36,128]{1,0:T(8,128)} %get-tuple-element.24) | data formatting | bytes 36864 | tf_op jit(solution)/shard_map/reshape | solution.py:401
  127.9 2.6 %fusion.17 = f32[12,3,32,128]{3,2,1,0:T(8,128)} fusion(f32[12,3,32,1]{3,2,1,0:T(8,128)S(1)} %reshape.180, f32[12,3,32,127]{3,2,1,0:T(8,128)} %get-tuple-element.42, f32[12,3,32,127]{3,2,1,0:T(8,128)S(1)} %get-tuple-element.41, f32[12,3,32,1]{3,2,1,0:T(8,128)S(1)} %reshape.181, f32[12,3,1,128]{3,2,1,0:T(1,128)} %reshape.182, ...), kind=kLoop, calls=%fused_computation.29 | loop fusion | flops 2801664 | bytes 4030464 | tf_op jit(solution)/shard_map/add | solution.py:404
  (86 shorter events, 6.7 us)
Async XLA Ops:
  1.8 2.4 %copy-start.15 = (s32[2,256]{1,0:T(2,128)S(1)}, s32[2,256]{1,0:T(2,128)}, u32[]{:S(2)}) copy-start(s32[2,256]{1,0:T(2,128)} %param.17) | copy-start | bytes 6148
  3.6 1.8 %copy-start = (f32[12,3,32,128]{3,2,1,0:T(8,128)S(1)}, f32[12,3,32,128]{3,2,1,0:T(8,128)}, u32[]{:S(2)}) copy-start(f32[12,3,32,128]{3,2,1,0:T(8,128)} %param.10) | copy-start | bytes 1769476
  3.6 1.8 %copy-start.3 = (f32[3,32,128]{2,1,0:T(8,128)S(1)}, f32[3,32,128]{2,1,0:T(8,128)}, u32[]{:S(2)}) copy-start(f32[3,32,128]{2,1,0:T(8,128)} %param.15) | copy-start | bytes 147460
  48.9 4.8 %copy-start.1 = (f32[3,32,128]{2,1,0:T(8,128)S(1)}, f32[3,32,128]{2,1,0:T(8,128)}, u32[]{:S(2)}) copy-start(f32[3,32,128]{2,1,0:T(8,128)} %param.14) | copy-start | bytes 147460
  53.7 11.7 %copy-start.9 = (f32[13,32,128]{2,1,0:T(8,128)S(1)}, f32[13,32,128]{2,1,0:T(8,128)}, u32[]{:S(2)}) copy-start(f32[13,32,128]{2,1,0:T(8,128)} %get-tuple-element.16) | copy-start | bytes 638980
  54.4 54.8 %copy-start.2 = (f32[3,32,128]{2,1,0:T(8,128)}, f32[3,32,128]{2,1,0:T(8,128)S(1)}, u32[]{:S(2)}) copy-start(f32[3,32,128]{2,1,0:T(8,128)S(1)} %get-tuple-element.51) | copy-start | bytes 147460
  66.3 0.8 copy-start.4
  66.3 2.3 %copy-start.10 = (f32[3,32,128]{2,1,0:T(8,128)S(1)}, f32[3,32,128]{2,1,0:T(8,128)}, u32[]{:S(2)}) copy-start(f32[3,32,128]{2,1,0:T(8,128)} %param.12) | copy-start | bytes 147460
  66.3 3.0 %copy-start.14 = (f32[3,128]{1,0:T(4,128)S(1)}, f32[3,128]{1,0:T(4,128)}, u32[]{:S(2)}) copy-start(f32[3,128]{1,0:T(4,128)} %param.13) | copy-start | bytes 4612
  78.1 1.4 %copy-start.11 = (f32[39,32]{1,0:T(8,128)S(1)}, f32[39,32]{1,0:T(8,128)}, u32[]{:S(2)}) copy-start(f32[39,32]{1,0:T(8,128)} %get-tuple-element.18) | copy-start | bytes 14980
  78.1 2.2 %copy-start.12 = (f32[39,128]{1,0:T(8,128)S(1)}, f32[39,128]{1,0:T(8,128)}, u32[]{:S(2)}) copy-start(f32[39,128]{1,0:T(8,128)} %get-tuple-element.20) | copy-start | bytes 59908
  79.4 1.0 copy-start.13
  80.2 0.7 copy-start.8
  80.4 0.6 copy-start.5
  80.5 0.6 copy-start.6
  81.1 1.4 %copy-start.7 = (f32[3,32,128]{2,1,0:T(8,128)}, f32[3,32,128]{2,1,0:T(8,128)S(1)}, u32[]{:S(2)}) copy-start(f32[3,32,128]{2,1,0:T(8,128)S(1)} %broadcast_maximum_fusion) | copy-start | bytes 147460

commit v6 on v5

--- a/solution.py
+++ b/solution.py
@@ -10,43 +10,17 @@
 MESH = pl.DeviceIdType.MESH
 
 
-def lev_sum_body(n, part_ref, out_ref, slots, send_sem, recv_sem):
-    me = lax.axis_index("lev")
+def lev_sum_body(n, part_ref, out_ref, pieces, reduced, sends, recvs, gsends, grecvs):
+    lev = lax.axis_index("lev")
     barrier = pltpu.get_barrier_semaphore()
     for d in range(1, n):
         pl.semaphore_signal(
-            barrier, inc=1, device_id={"lev": lax.rem(me + d, n)}, device_id_type=MESH
+            barrier, inc=1, device_id={"lev": lax.rem(lev + d, n)}, device_id_type=MESH
         )
     pl.semaphore_wait(barrier, n - 1)
-    sends = []
-    for d in range(1, n):
-        copy = pltpu.make_async_remote_copy(
-            src_ref=part_ref,
-            dst_ref=slots.at[me],
-            send_sem=send_sem.at[d - 1],
-            recv_sem=recv_sem.at[me],
-            device_id={"lev": lax.rem(me + d, n)},
-            device_id_type=MESH,
-        )
-        copy.start()
-        sends.append(copy)
-    slots[me] = part_ref[...]
-    for d in range(1, n):
-        sender = lax.rem(me + n - d, n)
-        pltpu.make_async_remote_copy(
-            src_ref=part_ref,
-            dst_ref=slots.at[sender],
-            send_sem=send_sem.at[d - 1],
-            recv_sem=recv_sem.at[sender],
-            device_id={"lev": sender},
-            device_id_type=MESH,
-        ).wait_recv()
-    for copy in sends:
-        copy.wait_send()
-    total = slots[0]
-    for s in range(1, n):
-        total = total + slots[s]
-    out_ref[...] = total
+    scatter_start(n, part_ref, pieces, sends, recvs)
+    scatter_finish_gather_start(n, part_ref, pieces, reduced, sends, recvs, gsends, grecvs)
+    gather_finish(n, out_ref, reduced, gsends, grecvs)
 
 
 def halo_body(lon_n, lat_n, col_last, col_first, row_last, row_first,
@@ -125,8 +99,73 @@
     )(col_last, col_first, row_last, row_first)
 
 
+def lev_copy(src, dst, send, recv, peer):
+    return pltpu.make_async_remote_copy(
+        src_ref=src, dst_ref=dst, send_sem=send, recv_sem=recv,
+        device_id={"lev": peer}, device_id_type=MESH,
+    )
+
+
+def scatter_start(n, part_ref, pieces, sends, recvs):
+    lev = lax.axis_index("lev")
+    rows = part_ref.shape[1] // n
+    for d in range(1, n):
+        peer = lax.rem(lev + d, n)
+        lev_copy(
+            part_ref.at[:, pl.ds(pl.multiple_of(peer * rows, rows), rows), :],
+            pieces.at[lev], sends.at[d - 1], recvs.at[lev], peer,
+        ).start()
+    pieces[lev] = part_ref[:, pl.ds(pl.multiple_of(lev * rows, rows), rows), :]
+
+
+def scatter_finish_gather_start(n, part_ref, pieces, reduced, sends, recvs, gsends, grecvs):
+    lev = lax.axis_index("lev")
+    rows = part_ref.shape[1] // n
+    for d in range(1, n):
+        sender = lax.rem(lev + n - d, n)
+        peer = lax.rem(lev + d, n)
+        lev_copy(
+            part_ref.at[:, pl.ds(0, rows), :], pieces.at[sender],
+            sends.at[d - 1], recvs.at[sender], sender,
+        ).wait_recv()
+        lev_copy(
+            part_ref.at[:, pl.ds(0, rows), :], pieces.at[sender],
+            sends.at[d - 1], recvs.at[sender], peer,
+        ).wait_send()
+    total = pieces[0]
+    for s in range(1, n):
+        total = total + pieces[s]
+    reduced[lev] = total
+    for d in range(1, n):
+        peer = lax.rem(lev + d, n)
+        lev_copy(reduced.at[lev], reduced.at[lev], gsends.at[d - 1], grecvs.at[lev], peer).start()
+
+
+def gather_finish(n, out_ref, reduced, gsends, grecvs):
+    lev = lax.axis_index("lev")
+    rows = out_ref.shape[1] // n
+    for d in range(1, n):
+        sender = lax.rem(lev + n - d, n)
+        lev_copy(reduced.at[sender], reduced.at[sender], gsends.at[d - 1], grecvs.at[sender], sender).wait_recv()
+        lev_copy(reduced.at[lev], reduced.at[lev], gsends.at[d - 1], grecvs.at[lev], lax.rem(lev + d, n)).wait_send()
+    for q in range(n):
+        out_ref[:, q * rows:(q + 1) * rows, :] = reduced[q]
+
+
+def lev_scratch(n, shape, dtype):
+    piece = (shape[0], shape[1] // n, shape[2])
+    return [
+        pltpu.VMEM((n,) + piece, dtype),
+        pltpu.VMEM((n,) + piece, dtype),
+        pltpu.SemaphoreType.DMA((n - 1,)),
+        pltpu.SemaphoreType.DMA((n,)),
+        pltpu.SemaphoreType.DMA((n - 1,)),
+        pltpu.SemaphoreType.DMA((n,)),
+    ]
+
+
 def exchange_body(lev_n, owners, lat_n, rows_ref, part_ref, rows_out, sum_out,
-                  got, slots, row_send, row_recv, lev_send, lev_recv):
+                  got, row_send, row_recv, pieces, reduced, sends, recvs, gsends, grecvs):
     lat = lax.axis_index("lat")
     lev = lax.axis_index("lev")
     me = lax.axis_index("lon") * lat_n + lat
@@ -147,15 +186,7 @@
             barrier, inc=1, device_id={"lev": lax.rem(lev + d, lev_n)}, device_id_type=MESH
         )
     pl.semaphore_wait(barrier, owners - 1 + lev_n - 1)
-    for d in range(1, lev_n):
-        pltpu.make_async_remote_copy(
-            src_ref=part_ref,
-            dst_ref=slots.at[lev],
-            send_sem=lev_send.at[d - 1],
-            recv_sem=lev_recv.at[lev],
-            device_id={"lev": lax.rem(lev + d, lev_n)},
-            device_id_type=MESH,
-        ).start()
+    scatter_start(lev_n, part_ref, pieces, sends, recvs)
 
     def row_copy(peer, target):
         return pltpu.make_async_remote_copy(
@@ -173,7 +204,7 @@
 
     lax.fori_loop(1, owners, send, 0)
     got[pl.ds(me, 1), :] = rows_ref[pl.ds(me, 1), :]
-    slots[lev] = part_ref[...]
+    scatter_finish_gather_start(lev_n, part_ref, pieces, reduced, sends, recvs, gsends, grecvs)
 
     def finish(d, carry):
         source = lax.rem(me + owners - d, owners)
@@ -182,22 +213,7 @@
         return carry
 
     lax.fori_loop(1, owners, finish, 0)
-    for d in range(1, lev_n):
-        sender = lax.rem(lev + lev_n - d, lev_n)
-        copy = pltpu.make_async_remote_copy(
-            src_ref=part_ref,
-            dst_ref=slots.at[sender],
-            send_sem=lev_send.at[d - 1],
-            recv_sem=lev_recv.at[sender],
-            device_id={"lev": sender},
-            device_id_type=MESH,
-        )
-        copy.wait_recv()
-        copy.wait_send()
-    total = slots[0]
-    for s in range(1, lev_n):
-        total = total + slots[s]
-    sum_out[...] = total
+    gather_finish(lev_n, sum_out, reduced, gsends, grecvs)
     rows_out[...] = got[...]
 
 
@@ -216,12 +232,9 @@
         out_specs=(vmem, vmem),
         scratch_shapes=[
             pltpu.VMEM(rows.shape, rows.dtype),
-            pltpu.VMEM((lev_n,) + part.shape, part.dtype),
             pltpu.SemaphoreType.DMA((owners,)),
             pltpu.SemaphoreType.DMA((owners,)),
-            pltpu.SemaphoreType.DMA((lev_n - 1,)),
-            pltpu.SemaphoreType.DMA((lev_n,)),
-        ],
+        ] + lev_scratch(lev_n, part.shape, part.dtype),
         compiler_params=pltpu.CompilerParams(
             collective_id=collective_id, has_side_effects=True
         ),
@@ -235,11 +248,7 @@
         out_shape=jax.ShapeDtypeStruct(x.shape, x.dtype),
         in_specs=[pl.BlockSpec(memory_space=pltpu.VMEM)],
         out_specs=pl.BlockSpec(memory_space=pltpu.VMEM),
-        scratch_shapes=[
-            pltpu.VMEM((n,) + x.shape, x.dtype),
-            pltpu.SemaphoreType.DMA((n - 1,)),
-            pltpu.SemaphoreType.DMA((n,)),
-        ],
+        scratch_shapes=lev_scratch(n, x.shape, x.dtype),
         compiler_params=pltpu.CompilerParams(
             collective_id=collective_id, has_side_effects=True
         ),
@@ -330,12 +339,13 @@
     arrived = jnp.transpose(arrived, (1, 2, 0, 3)).reshape(
         step_count, lev_dev + 1, owner_count * cap
     )
-    cell_iota = jnp.arange(grid_cells, dtype=jnp.int32).astype(jnp.float32)
-    hit = (arrived[:, lev_dev, :, None] == cell_iota[None, None, :]).astype(jnp.float32)
+    cells = arrived[:, lev_dev, :].astype(jnp.int32)
+    row_hit = (cells // lon_cols)[:, :, None] == jnp.arange(lat_rows, dtype=jnp.int32)
+    col_hit = (cells % lon_cols)[:, :, None] == jnp.arange(lon_cols, dtype=jnp.int32)
+    spread = jnp.where(row_hit[:, None, :, :], arrived[:, :lev_dev, :, None], 0.0)
     forcing_grid = jnp.einsum(
-        "tke,tec->tkc", arrived[:, :lev_dev, :], hit, precision=lax.Precision.HIGHEST
-    )
-    forcing_grid = forcing_grid.reshape(step_count, lev_dev, lat_rows, lon_cols)
+        "tker,tec->tkrc", spread, col_hit.astype(jnp.float32), precision=lax.Precision.HIGHEST
+    )
     row_index = jnp.arange(lat_rows, dtype=jnp.int32)[None, :, None]
     at_top = jnp.logical_and(lat_place == lat_count - 1, row_index == lat_rows - 1)
     at_bottom = jnp.logical_and(lat_place == 0, row_index == 0)

time: 132 us -> 119 us (0.902)
  Pallas kernels: 93.5 us -> 86.4 us
  matrix products: 4.78 us -> 0.47 us
    pallas_call x2, Pallas kernels: 36 us -> 26.9 us  [lev_sum(): pl.pallas_call(functools.partial(lev_sum_body, n), out_shape=jax.ShapeDty...]
    pallas_call x2, Pallas kernels: 16.3 us -> 21.2 us  [halo_swap(): pl.pallas_call(functools.partial(halo_body, lon_n, lat_n), out_shape=(jax...]
    dot_general x1, matrix products: 4.78 us -> 0.47 us  [on_device(): jnp.einsum('tker,tec->tkrc', spread, col_hit.astype(jnp.float32), precisi...]
    pallas_call x1, Pallas kernels: 41.2 us -> 38.2 us  [exchange(): pl.pallas_call(functools.partial(exchange_body, lev_n, owners, lat_n), ou...]
where the time goes in v6:
time: 119 us; the launch traced here: 118 us
  Pallas kernels  86.4 us (73%)
  local copies, waits for them, and re-layouts  17 us (14%)
  other arithmetic  13.6 us (11%)
    pallas_call x1, Pallas kernels, exchange(): pl.pallas_call(functools.partial(exchange_body, lev_n, owners, lat_n), ou...  38.2 us
    pallas_call x2, Pallas kernels, lev_sum(): pl.pallas_call(functools.partial(lev_sum_body, n), out_shape=jax.ShapeDty...  26.9 us
    pallas_call x2, Pallas kernels, halo_swap(): pl.pallas_call(functools.partial(halo_body, lon_n, lat_n), out_shape=(jax...  21.2 us
    reshape x2, local copies, waits for them, and re-layouts, on_device(): east_halo.reshape(tracers, lev_dev, lat_rows, 1)  2.65 us
    add x1, other arithmetic, on_device(): adjoint + upwind_east * (east_side - adjoint)  2.63 us

profile of v6, /device:TPU:1, one launch (start us, length us, event | category | flops | bytes accessed | tf_op | source)
XLA Modules:
  0.0 117.9 jit_solution(12604237352528036540)
XLA Ops:
  0.0 0.7 copy.104
  0.9 0.7 fusion.28
  1.8 0.7 iota_compare_fusion.4
  2.5 0.7 broadcast_select_fusion
  4.8 0.6 pad.4.rows_ref
  5.5 0.7 pad_maximum_fusion.part_ref
  6.2 38.2 %shard_map.100 = (f32[128,128]{1,0:T(8,128)}, f32[13,32,128]{2,1,0:T(8,128)}) custom-call(f32[128,128]{1,0:T(8,128)} %pad.4.rows_ref, f32[13,32,128]{2,1,0:T(8,128)} %pad_maximum_fusion.part_ref), custom_call_target="tpu_custom_call" | custom-call | tf_op jit(solution)/shard_map/pallas_call | solution.py:225
  44.5 0.9 copy.62
  46.5 0.6 multiply_reduce_fusion.2
  47.1 11.0 %shard_map.101 = f32[1,32,128]{2,1,0:T(8,128)} custom-call(f32[1,32,128]{2,1,0:T(8,128)} %bitcast.72), custom_call_target="tpu_custom_call" | custom-call | flops 16384 | bytes 163840 | tf_op jit(solution)/shard_map/pallas_call | solution.py:246
  58.1 0.7 add_divide_fusion
  59.1 0.6 slice_reduce_fusion.2
  60.0 0.6 pad_maximum_fusion.1
  60.8 0.6 pad_maximum_fusion.3
  61.4 8.1 %shard_map.102 = (f32[39,32]{1,0:T(8,128)}, f32[39,32]{1,0:T(8,128)}, f32[39,128]{1,0:T(8,128)}, f32[39,128]{1,0:T(8,128)}) custom-call(f32[39,32]{1,0:T(8,128)} %get-tuple-element.51.col_last, f32[39,32]{1,0:T(8,128)} %get-tuple-element.52.col_first, f32[39,128]{1,0:T(8,128)} %get-tuple-element.53.row_last, f32[39,128]{1,0:T(8,128)} %get-tuple-element.54.row_first), custom_call_target="tpu_custom_call" | custom-call | tf_op jit(solution)/shard_map/pallas_call | solution.py:79
  69.6 1.3 %reshape.205 = f32[12,3,32,1]{3,2,1,0:T(8,128)S(1)} reshape(f32[36,32]{1,0:T(8,128)} %bitcast.79) | data formatting | bytes 9216 | tf_op jit(solution)/shard_map/reshape | solution.py:402
  71.0 0.6 reshape.206
  72.7 1.4 %multiply_reduce_fusion = (f32[12,32,128]{2,1,0:T(8,128)}, f32[12,3,32,128]{3,2,1,0:T(8,128)S(1)}) fusion(f32[3,32,128]{2,1,0:T(8,128)S(1)} %copy-done.3, f32[3,32,128]{2,1,0:T(8,128)S(1)} %get-tuple-element.46, f32[12,3,31,128]{3,2,1,0:T(8,128)S(1)} %get-tuple-element.44, f32[12,3,1,128]{3,2,1,0:T(1,128)S(1)} %reshape.208, f32[3,32,128]{2,1,0:T(8,128)S(1)} %fusion.27, ...), kind=kLoop, calls=%fused_computation.33 | loop fusion | flops 3342336 | bytes 4374528 | tf_op jit(solution)/shard_map/reduce_sum | solution.py:363
  74.0 15.9 %shard_map.103 = f32[12,32,128]{2,1,0:T(8,128)} custom-call(f32[12,32,128]{2,1,0:T(8,128)} %get-tuple-element.35.part_ref), custom_call_target="tpu_custom_call" | custom-call | flops 196608 | bytes 1966080 | tf_op jit(solution)/shard_map/pallas_call | solution.py:246
  89.9 1.6 %broadcast_divide_fusion = f32[12,32,128]{2,1,0:T(8,128)} fusion(f32[12,32,128]{2,1,0:T(8,128)} %shard_map.103, f32[32,128]{1,0:T(8,128)S(1)} %slice_bitcast_fusion.2), kind=kLoop, calls=%fused_computation.49 | loop fusion | flops 49152 | bytes 409600 | tf_op jit(solution)/shard_map/div | solution.py:366
  91.5 1.0 multiply_add_fusion
  92.7 1.0 fusion.32
  94.3 0.6 reshape_squeeze.28.col_last
  94.9 0.6 reshape_squeeze.29.col_first
  95.7 0.6 reshape_squeeze.30.row_last
  96.3 0.6 reshape_squeeze.31.row_first
  96.9 13.1 %shard_map.104 = (f32[36,32]{1,0:T(8,128)}, f32[36,32]{1,0:T(8,128)}, f32[36,128]{1,0:T(8,128)}, f32[36,128]{1,0:T(8,128)}) custom-call(f32[36,32]{1,0:T(8,128)} %reshape_squeeze.28.col_last, f32[36,32]{1,0:T(8,128)} %reshape_squeeze.29.col_first, f32[36,128]{1,0:T(8,128)} %reshape_squeeze.30.row_last, f32[36,128]{1,0:T(8,128)} %reshape_squeeze.31.row_first), custom_call_target="tpu_custom_call" | custom-call | tf_op jit(solution)/shard_map/pallas_call | solution.py:79
  110.0 1.3 %reshape.209 = f32[12,3,32,1]{3,2,1,0:T(8,128)S(1)} reshape(f32[36,32]{1,0:T(8,128)} %get-tuple-element.21) | data formatting | bytes 9216 | tf_op jit(solution)/shard_map/reshape | solution.py:402
  111.3 1.3 %reshape.210 = f32[12,3,32,1]{3,2,1,0:T(8,128)S(1)} reshape(f32[36,32]{1,0:T(8,128)} %get-tuple-element.22) | data formatting | bytes 9216 | tf_op jit(solution)/shard_map/reshape | solution.py:405
  112.6 1.4 %reshape.211 = f32[12,3,1,128]{3,2,1,0:T(1,128)} reshape(f32[36,128]{1,0:T(8,128)} %get-tuple-element.23) | data formatting | bytes 36864 | tf_op jit(solution)/shard_map/reshape | solution.py:408
  114.0 1.3 %reshape.212 = f32[12,3,1,128]{3,2,1,0:T(1,128)} reshape(f32[36,128]{1,0:T(8,128)} %get-tuple-element.24) | data formatting | bytes 36864 | tf_op jit(solution)/shard_map/reshape | solution.py:411
  115.3 2.6 %fusion.13 = f32[12,3,32,128]{3,2,1,0:T(8,128)} fusion(f32[12,3,32,1]{3,2,1,0:T(8,128)S(1)} %reshape.209, f32[12,3,32,127]{3,2,1,0:T(8,128)} %get-tuple-element.40, f32[12,3,32,127]{3,2,1,0:T(8,128)S(1)} %get-tuple-element.39, f32[12,3,32,1]{3,2,1,0:T(8,128)S(1)} %reshape.210, f32[12,3,1,128]{3,2,1,0:T(1,128)} %reshape.211, ...), kind=kLoop, calls=%fused_computation.25 | loop fusion | flops 2801664 | bytes 4030464 | tf_op jit(solution)/shard_map/add | solution.py:414
  (84 shorter events, 5.4 us)
Async XLA Ops:
  1.8 2.4 %copy-start.15 = (s32[2,256]{1,0:T(2,128)S(1)}, s32[2,256]{1,0:T(2,128)}, u32[]{:S(2)}) copy-start(s32[2,256]{1,0:T(2,128)} %param.17) | copy-start | bytes 6148
  3.6 1.8 %copy-start = (f32[12,3,32,128]{3,2,1,0:T(8,128)S(1)}, f32[12,3,32,128]{3,2,1,0:T(8,128)}, u32[]{:S(2)}) copy-start(f32[12,3,32,128]{3,2,1,0:T(8,128)} %param.10) | copy-start | bytes 1769476
  3.6 1.8 %copy-start.3 = (f32[3,32,128]{2,1,0:T(8,128)S(1)}, f32[3,32,128]{2,1,0:T(8,128)}, u32[]{:S(2)}) copy-start(f32[3,32,128]{2,1,0:T(8,128)} %param.15) | copy-start | bytes 147460
  45.6 12.5 %copy-start.9 = (f32[13,32,128]{2,1,0:T(8,128)S(1)}, f32[13,32,128]{2,1,0:T(8,128)}, u32[]{:S(2)}) copy-start(f32[13,32,128]{2,1,0:T(8,128)} %get-tuple-element.16) | copy-start | bytes 638980
  46.0 12.9 %copy-start.1 = (f32[3,32,128]{2,1,0:T(8,128)S(1)}, f32[3,32,128]{2,1,0:T(8,128)}, u32[]{:S(2)}) copy-start(f32[3,32,128]{2,1,0:T(8,128)} %param.14) | copy-start | bytes 147460
  58.9 32.6 %copy-start.2 = (f32[3,32,128]{2,1,0:T(8,128)}, f32[3,32,128]{2,1,0:T(8,128)S(1)}, u32[]{:S(2)}) copy-start(f32[3,32,128]{2,1,0:T(8,128)S(1)} %broadcast_subtract_fusion) | copy-start | bytes 147460
  59.0 0.8 copy-start.4
  59.1 1.7 %copy-start.10 = (f32[3,32,128]{2,1,0:T(8,128)S(1)}, f32[3,32,128]{2,1,0:T(8,128)}, u32[]{:S(2)}) copy-start(f32[3,32,128]{2,1,0:T(8,128)} %param.12) | copy-start | bytes 147460
  59.1 1.7 %copy-start.14 = (f32[3,128]{1,0:T(4,128)S(1)}, f32[3,128]{1,0:T(4,128)}, u32[]{:S(2)}) copy-start(f32[3,128]{1,0:T(4,128)} %param.13) | copy-start | bytes 4612
  69.6 1.4 %copy-start.11 = (f32[39,32]{1,0:T(8,128)S(1)}, f32[39,32]{1,0:T(8,128)}, u32[]{:S(2)}) copy-start(f32[39,32]{1,0:T(8,128)} %get-tuple-element.18) | copy-start | bytes 14980
  69.6 2.2 %copy-start.12 = (f32[39,128]{1,0:T(8,128)S(1)}, f32[39,128]{1,0:T(8,128)}, u32[]{:S(2)}) copy-start(f32[39,128]{1,0:T(8,128)} %get-tuple-element.20) | copy-start | bytes 59908
  71.0 1.0 copy-start.13
  71.8 0.7 copy-start.8
  71.9 0.6 copy-start.5
  72.0 0.6 copy-start.6
  72.6 1.4 %copy-start.7 = (f32[3,32,128]{2,1,0:T(8,128)}, f32[3,32,128]{2,1,0:T(8,128)S(1)}, u32[]{:S(2)}) copy-start(f32[3,32,128]{2,1,0:T(8,128)S(1)} %broadcast_maximum_fusion) | copy-start | bytes 147460

commit v7 on v6

--- a/solution.py
+++ b/solution.py
@@ -239,6 +239,45 @@
             collective_id=collective_id, has_side_effects=True
         ),
     )(rows, part)
+
+
+def lev_direct_body(n, part_ref, out_ref, slots, send_sem, recv_sem):
+    me = lax.axis_index("lev")
+    barrier = pltpu.get_barrier_semaphore()
+    for d in range(1, n):
+        pl.semaphore_signal(
+            barrier, inc=1, device_id={"lev": lax.rem(me + d, n)}, device_id_type=MESH
+        )
+    pl.semaphore_wait(barrier, n - 1)
+    for d in range(1, n):
+        lev_copy(part_ref, slots.at[me], send_sem.at[d - 1], recv_sem.at[me], lax.rem(me + d, n)).start()
+    slots[me] = part_ref[...]
+    for d in range(1, n):
+        sender = lax.rem(me + n - d, n)
+        lev_copy(part_ref, slots.at[sender], send_sem.at[d - 1], recv_sem.at[sender], sender).wait_recv()
+        lev_copy(part_ref, slots.at[sender], send_sem.at[d - 1], recv_sem.at[sender], lax.rem(me + d, n)).wait_send()
+    total = slots[0]
+    for s in range(1, n):
+        total = total + slots[s]
+    out_ref[...] = total
+
+
+def lev_direct(x, collective_id):
+    n = lax.axis_size("lev")
+    return pl.pallas_call(
+        functools.partial(lev_direct_body, n),
+        out_shape=jax.ShapeDtypeStruct(x.shape, x.dtype),
+        in_specs=[pl.BlockSpec(memory_space=pltpu.VMEM)],
+        out_specs=pl.BlockSpec(memory_space=pltpu.VMEM),
+        scratch_shapes=[
+            pltpu.VMEM((n,) + x.shape, x.dtype),
+            pltpu.SemaphoreType.DMA((n - 1,)),
+            pltpu.SemaphoreType.DMA((n,)),
+        ],
+        compiler_params=pltpu.CompilerParams(
+            collective_id=collective_id, has_side_effects=True
+        ),
+    )(x)
 
 
 def lev_sum(x, collective_id):
@@ -351,7 +390,7 @@
     at_bottom = jnp.logical_and(lat_place == 0, row_index == 0)
     upwind_east = jnp.maximum(east_courant, 0.0)
     forcing_part = jnp.sum(detrain_share * forcing_grid[step_count - 1], axis=0)
-    forcing_sum = lev_sum(forcing_part[None], 4)[0]
+    forcing_sum = lev_direct(forcing_part[None], 4)[0]
     adjoint = adjoint_field
     for position in range(step_count):
         step_now = step_count - 1 - position

time: 119 us -> 113 us (0.950)
  Pallas kernels: 86.4 us -> 80.2 us
    pallas_call x2 -> x1, Pallas kernels: 26.9 us -> 14.1 us  [lev_sum(): pl.pallas_call(functools.partial(lev_sum_body, n), out_shape=jax.ShapeDty...]
    pallas_call x0 -> x1, Pallas kernels: none -> 8.92 us  [lev_direct(): pl.pallas_call(functools.partial(lev_direct_body, n), out_shape=jax.Shape...]
    pallas_call x2, Pallas kernels: 21.2 us -> 18.9 us  [halo_swap(): pl.pallas_call(functools.partial(halo_body, lon_n, lat_n), out_shape=(jax...]
where the time goes in v7:
time: 113 us; the launch traced here: 112 us
  Pallas kernels  80.2 us (71%)
  local copies, waits for them, and re-layouts  17 us (15%)
  other arithmetic  13.6 us (12%)
    pallas_call x1, Pallas kernels, exchange(): pl.pallas_call(functools.partial(exchange_body, lev_n, owners, lat_n), ou...  38.2 us
    pallas_call x2, Pallas kernels, halo_swap(): pl.pallas_call(functools.partial(halo_body, lon_n, lat_n), out_shape=(jax...  18.9 us
    pallas_call x1, Pallas kernels, lev_sum(): pl.pallas_call(functools.partial(lev_sum_body, n), out_shape=jax.ShapeDty...  14.1 us
    pallas_call x1, Pallas kernels, lev_direct(): pl.pallas_call(functools.partial(lev_direct_body, n), out_shape=jax.Shape...  8.92 us
    reshape x2, local copies, waits for them, and re-layouts, on_device(): east_halo.reshape(tracers, lev_dev, lat_rows, 1)  2.65 us
    add x1, other arithmetic, on_device(): adjoint + upwind_east * (east_side - adjoint)  2.63 us
    div x2, other arithmetic, on_device(): column_sum / total_detrain  2.37 us

profile of v7, /device:TPU:1, one launch (start us, length us, event | category | flops | bytes accessed | tf_op | source)
XLA Modules:
  0.0 111.8 jit_solution(2016303900246564023)
XLA Ops:
  0.0 0.7 copy.104
  0.9 0.7 fusion.28
  1.8 0.7 iota_compare_fusion.4
  2.5 0.7 broadcast_select_fusion
  4.8 0.6 pad.4.rows_ref
  5.5 0.7 pad_maximum_fusion.part_ref
  6.2 38.2 %shard_map.100 = (f32[128,128]{1,0:T(8,128)}, f32[13,32,128]{2,1,0:T(8,128)}) custom-call(f32[128,128]{1,0:T(8,128)} %pad.4.rows_ref, f32[13,32,128]{2,1,0:T(8,128)} %pad_maximum_fusion.part_ref), custom_call_target="tpu_custom_call" | custom-call | tf_op jit(solution)/shard_map/pallas_call | solution.py:225
  44.5 0.9 copy.62
  46.5 0.6 multiply_reduce_fusion.2
  47.1 8.9 %shard_map.101 = f32[1,32,128]{2,1,0:T(8,128)} custom-call(f32[1,32,128]{2,1,0:T(8,128)} %bitcast.72), custom_call_target="tpu_custom_call" | custom-call | tf_op jit(solution)/shard_map/pallas_call | solution.py:267
  56.0 0.7 add_divide_fusion
  57.0 0.6 slice_reduce_fusion.2
  57.9 0.6 pad_maximum_fusion.1
  58.7 0.6 pad_maximum_fusion.3
  59.3 8.1 %shard_map.102 = (f32[39,32]{1,0:T(8,128)}, f32[39,32]{1,0:T(8,128)}, f32[39,128]{1,0:T(8,128)}, f32[39,128]{1,0:T(8,128)}) custom-call(f32[39,32]{1,0:T(8,128)} %get-tuple-element.51.col_last, f32[39,32]{1,0:T(8,128)} %get-tuple-element.52.col_first, f32[39,128]{1,0:T(8,128)} %get-tuple-element.53.row_last, f32[39,128]{1,0:T(8,128)} %get-tuple-element.54.row_first), custom_call_target="tpu_custom_call" | custom-call | tf_op jit(solution)/shard_map/pallas_call | solution.py:79
  67.5 1.3 %reshape.205 = f32[12,3,32,1]{3,2,1,0:T(8,128)S(1)} reshape(f32[36,32]{1,0:T(8,128)} %bitcast.79) | data formatting | bytes 9216 | tf_op jit(solution)/shard_map/reshape | solution.py:441
  68.9 0.6 reshape.206
  70.6 1.4 %multiply_reduce_fusion = (f32[12,32,128]{2,1,0:T(8,128)}, f32[12,3,32,128]{3,2,1,0:T(8,128)S(1)}) fusion(f32[3,32,128]{2,1,0:T(8,128)S(1)} %copy-done.3, f32[3,32,128]{2,1,0:T(8,128)S(1)} %get-tuple-element.46, f32[12,3,31,128]{3,2,1,0:T(8,128)S(1)} %get-tuple-element.44, f32[12,3,1,128]{3,2,1,0:T(1,128)S(1)} %reshape.208, f32[3,32,128]{2,1,0:T(8,128)S(1)} %fusion.27, ...), kind=kLoop, calls=%fused_computation.33 | loop fusion | flops 3342336 | bytes 4374528 | tf_op jit(solution)/shard_map/reduce_sum | solution.py:402
  71.9 14.1 %shard_map.103 = f32[12,32,128]{2,1,0:T(8,128)} custom-call(f32[12,32,128]{2,1,0:T(8,128)} %get-tuple-element.35.part_ref), custom_call_target="tpu_custom_call" | custom-call | flops 196608 | bytes 1966080 | tf_op jit(solution)/shard_map/pallas_call | solution.py:285
  86.1 1.6 %broadcast_divide_fusion = f32[12,32,128]{2,1,0:T(8,128)} fusion(f32[12,32,128]{2,1,0:T(8,128)} %shard_map.103, f32[32,128]{1,0:T(8,128)S(1)} %slice_bitcast_fusion.2), kind=kLoop, calls=%fused_computation.49 | loop fusion | flops 49152 | bytes 409600 | tf_op jit(solution)/shard_map/div | solution.py:405
  87.7 1.0 multiply_add_fusion
  88.8 1.0 fusion.32
  90.5 0.6 reshape_squeeze.28.col_last
  91.1 0.6 reshape_squeeze.29.col_first
  91.8 0.6 reshape_squeeze.30.row_last
  92.4 0.6 reshape_squeeze.31.row_first
  93.0 10.8 %shard_map.104 = (f32[36,32]{1,0:T(8,128)}, f32[36,32]{1,0:T(8,128)}, f32[36,128]{1,0:T(8,128)}, f32[36,128]{1,0:T(8,128)}) custom-call(f32[36,32]{1,0:T(8,128)} %reshape_squeeze.28.col_last, f32[36,32]{1,0:T(8,128)} %reshape_squeeze.29.col_first, f32[36,128]{1,0:T(8,128)} %reshape_squeeze.30.row_last, f32[36,128]{1,0:T(8,128)} %reshape_squeeze.31.row_first), custom_call_target="tpu_custom_call" | custom-call | tf_op jit(solution)/shard_map/pallas_call | solution.py:79
  103.8 1.3 %reshape.209 = f32[12,3,32,1]{3,2,1,0:T(8,128)S(1)} reshape(f32[36,32]{1,0:T(8,128)} %get-tuple-element.21) | data formatting | bytes 9216 | tf_op jit(solution)/shard_map/reshape | solution.py:441
  105.1 1.3 %reshape.210 = f32[12,3,32,1]{3,2,1,0:T(8,128)S(1)} reshape(f32[36,32]{1,0:T(8,128)} %get-tuple-element.22) | data formatting | bytes 9216 | tf_op jit(solution)/shard_map/reshape | solution.py:444
  106.5 1.4 %reshape.211 = f32[12,3,1,128]{3,2,1,0:T(1,128)} reshape(f32[36,128]{1,0:T(8,128)} %get-tuple-element.23) | data formatting | bytes 36864 | tf_op jit(solution)/shard_map/reshape | solution.py:447
  107.8 1.3 %reshape.212 = f32[12,3,1,128]{3,2,1,0:T(1,128)} reshape(f32[36,128]{1,0:T(8,128)} %get-tuple-element.24) | data formatting | bytes 36864 | tf_op jit(solution)/shard_map/reshape | solution.py:450
  109.2 2.6 %fusion.13 = f32[12,3,32,128]{3,2,1,0:T(8,128)} fusion(f32[12,3,32,1]{3,2,1,0:T(8,128)S(1)} %reshape.209, f32[12,3,32,127]{3,2,1,0:T(8,128)} %get-tuple-element.40, f32[12,3,32,127]{3,2,1,0:T(8,128)S(1)} %get-tuple-element.39, f32[12,3,32,1]{3,2,1,0:T(8,128)S(1)} %reshape.210, f32[12,3,1,128]{3,2,1,0:T(1,128)} %reshape.211, ...), kind=kLoop, calls=%fused_computation.25 | loop fusion | flops 2801664 | bytes 4030464 | tf_op jit(solution)/shard_map/add | solution.py:453
  (84 shorter events, 5.4 us)
Async XLA Ops:
  1.8 2.4 %copy-start.15 = (s32[2,256]{1,0:T(2,128)S(1)}, s32[2,256]{1,0:T(2,128)}, u32[]{:S(2)}) copy-start(s32[2,256]{1,0:T(2,128)} %param.17) | copy-start | bytes 6148
  3.6 1.8 %copy-start = (f32[12,3,32,128]{3,2,1,0:T(8,128)S(1)}, f32[12,3,32,128]{3,2,1,0:T(8,128)}, u32[]{:S(2)}) copy-start(f32[12,3,32,128]{3,2,1,0:T(8,128)} %param.10) | copy-start | bytes 1769476
  3.6 1.8 %copy-start.3 = (f32[3,32,128]{2,1,0:T(8,128)S(1)}, f32[3,32,128]{2,1,0:T(8,128)}, u32[]{:S(2)}) copy-start(f32[3,32,128]{2,1,0:T(8,128)} %param.15) | copy-start | bytes 147460
  45.6 10.4 %copy-start.9 = (f32[13,32,128]{2,1,0:T(8,128)S(1)}, f32[13,32,128]{2,1,0:T(8,128)}, u32[]{:S(2)}) copy-start(f32[13,32,128]{2,1,0:T(8,128)} %get-tuple-element.16) | copy-start | bytes 638980
  46.0 10.8 %copy-start.1 = (f32[3,32,128]{2,1,0:T(8,128)S(1)}, f32[3,32,128]{2,1,0:T(8,128)}, u32[]{:S(2)}) copy-start(f32[3,32,128]{2,1,0:T(8,128)} %param.14) | copy-start | bytes 147460
  56.8 30.9 %copy-start.2 = (f32[3,32,128]{2,1,0:T(8,128)}, f32[3,32,128]{2,1,0:T(8,128)S(1)}, u32[]{:S(2)}) copy-start(f32[3,32,128]{2,1,0:T(8,128)S(1)} %broadcast_subtract_fusion) | copy-start | bytes 147460
  56.9 0.8 copy-start.4
  57.0 1.7 %copy-start.10 = (f32[3,32,128]{2,1,0:T(8,128)S(1)}, f32[3,32,128]{2,1,0:T(8,128)}, u32[]{:S(2)}) copy-start(f32[3,32,128]{2,1,0:T(8,128)} %param.12) | copy-start | bytes 147460
  57.0 1.7 %copy-start.14 = (f32[3,128]{1,0:T(4,128)S(1)}, f32[3,128]{1,0:T(4,128)}, u32[]{:S(2)}) copy-start(f32[3,128]{1,0:T(4,128)} %param.13) | copy-start | bytes 4612
  67.5 1.4 %copy-start.11 = (f32[39,32]{1,0:T(8,128)S(1)}, f32[39,32]{1,0:T(8,128)}, u32[]{:S(2)}) copy-start(f32[39,32]{1,0:T(8,128)} %get-tuple-element.18) | copy-start | bytes 14980
  67.5 2.2 %copy-start.12 = (f32[39,128]{1,0:T(8,128)S(1)}, f32[39,128]{1,0:T(8,128)}, u32[]{:S(2)}) copy-start(f32[39,128]{1,0:T(8,128)} %get-tuple-element.20) | copy-start | bytes 59908
  68.9 1.0 copy-start.13
  69.7 0.7 copy-start.8
  69.8 0.6 copy-start.5
  69.9 0.6 copy-start.6
  70.6 1.4 %copy-start.7 = (f32[3,32,128]{2,1,0:T(8,128)}, f32[3,32,128]{2,1,0:T(8,128)S(1)}, u32[]{:S(2)}) copy-start(f32[3,32,128]{2,1,0:T(8,128)S(1)} %broadcast_maximum_fusion) | copy-start | bytes 147460

commit v8 on v7

--- a/solution.py
+++ b/solution.py
@@ -437,17 +437,27 @@
             )
             west_halo, east_halo = west_halo[:planes], east_halo[:planes]
             north_halo, south_halo = north_halo[:planes], south_halo[:planes]
-        east_side = jnp.concatenate(
-            [adjoint[:, :, :, 1:], east_halo.reshape(tracers, lev_dev, lat_rows, 1)], axis=3
-        )
-        west_side = jnp.concatenate(
-            [west_halo.reshape(tracers, lev_dev, lat_rows, 1), adjoint[:, :, :, :-1]], axis=3
-        )
-        north_side = jnp.concatenate(
-            [adjoint[:, :, 1:, :], north_halo.reshape(tracers, lev_dev, 1, lon_cols)], axis=2
-        )
-        south_side = jnp.concatenate(
-            [south_halo.reshape(tracers, lev_dev, 1, lon_cols), adjoint[:, :, :-1, :]], axis=2
+        lane = jnp.arange(lon_cols, dtype=jnp.int32)
+        sub = jnp.arange(lat_rows, dtype=jnp.int32)[:, None]
+        east_side = jnp.where(
+            lane == lon_cols - 1,
+            east_halo.reshape(tracers, lev_dev, lat_rows)[..., None],
+            jnp.roll(adjoint, -1, axis=3),
+        )
+        west_side = jnp.where(
+            lane == 0,
+            west_halo.reshape(tracers, lev_dev, lat_rows)[..., None],
+            jnp.roll(adjoint, 1, axis=3),
+        )
+        north_side = jnp.where(
+            sub == lat_rows - 1,
+            north_halo.reshape(tracers, lev_dev, 1, lon_cols),
+            jnp.roll(adjoint, -1, axis=2),
+        )
+        south_side = jnp.where(
+            sub == 0,
+            south_halo.reshape(tracers, lev_dev, 1, lon_cols),
+            jnp.roll(adjoint, 1, axis=2),
         )
         adjoint = (
             adjoint

time: 113 us -> 138 us (1.22)
  local copies, waits for them, and re-layouts: 17 us -> 29.6 us
  other arithmetic: 13.6 us -> 24.7 us
    broadcast_in_dim x0 -> x8, local copies, waits for them, and re-layouts: none -> 8.36 us  [the longest x2 2.09 us: on_device(): jnp.where(sub == lat_rows - 1, north_halo.reshape(tracers, lev_dev, 1, lo...]
    reshape x8 -> x0, local copies, waits for them, and re-layouts: 7.3 us -> none  [the longest x2 2.65 us: on_device(): east_halo.reshape(tracers, lev_dev, lat_rows, 1)]
    slice x2, local copies, waits for them, and re-layouts: 1.17 us -> 3.71 us  [on_device(): col_first = adjoint[:, :, :, 0].reshape(planes, lat_rows)]
    reduce_sum x1, other arithmetic: 1.37 us -> 3.02 us  [on_device(): partial_sum = jnp.sum(detrain_share[None] * adjoint, axis=1)]
    another operation x2, local copies, waits for them, and re-layouts: 0.63 us -> 2.17 us  [on_device(): col_first = adjoint[:, :, :, 0].reshape(planes, lat_rows)]
    another operation x2, local copies, waits for them, and re-layouts: 0.64 us -> 2.1 us  [on_device(): col_last = adjoint[:, :, :, -1].reshape(planes, lat_rows)]
    slice x1, local copies, waits for them, and re-layouts: 0.16 us -> 1.6 us  [on_device(): col_first = jnp.concatenate([col_first, east_courant[:, :, 0]], axis=0)]
    max x1, other arithmetic: 0.01 us -> 1.44 us  [on_device(): upwind_east = jnp.maximum(east_courant, 0.0)]
where the time goes in v8:
time: 138 us; the launch traced here: 136 us
  Pallas kernels  80.3 us (58%)
  local copies, waits for them, and re-layouts  29.6 us (21%)
  other arithmetic  24.7 us (18%)
    pallas_call x1, Pallas kernels, exchange(): pl.pallas_call(functools.partial(exchange_body, lev_n, owners, lat_n), ou...  38.2 us
    pallas_call x2, Pallas kernels, halo_swap(): pl.pallas_call(functools.partial(halo_body, lon_n, lat_n), out_shape=(jax...  18.9 us
    pallas_call x1, Pallas kernels, lev_sum(): pl.pallas_call(functools.partial(lev_sum_body, n), out_shape=jax.ShapeDty...  14.3 us
    pallas_call x1, Pallas kernels, lev_direct(): pl.pallas_call(functools.partial(lev_direct_body, n), out_shape=jax.Shape...  8.92 us
    slice x2, local copies, waits for them, and re-layouts, on_device(): col_first = adjoint[:, :, :, 0].reshape(planes, lat_rows)  3.71 us
    reduce_sum x1, other arithmetic, on_device(): partial_sum = jnp.sum(detrain_share[None] * adjoint, axis=1)  3.02 us
    add x1, other arithmetic, on_device(): adjoint + upwind_east * (east_side - adjoint)  2.95 us

profile of v8, /device:TPU:1, one launch (start us, length us, event | category | flops | bytes accessed | tf_op | source)
XLA Modules:
  0.0 135.6 jit_solution(13608949307353439220)
XLA Ops:
  5.1 1.6 %slice_reduce_fusion = (f32[3,32]{1,0:T(4,128)}, f32[3,32]{1,0:T(4,128)}) fusion(f32[3,32,128]{2,1,0:T(8,128)} %param.11), kind=kLoop, calls=%fused_computation.62 | loop fusion | bytes 1536 | tf_op jit(solution)/shard_map/slice | solution.py:414
  7.4 0.8 reduce_sum.60
  8.2 0.8 broadcast_subtract_fusion
  9.0 1.4 %broadcast_maximum_fusion = f32[3,32,128]{2,1,0:T(8,128)} fusion(f32[3,32,128]{2,1,0:T(8,128)} %param.11), kind=kLoop, calls=%fused_computation.65 | loop fusion | flops 12288 | bytes 98304 | tf_op jit(solution)/shard_map/max | solution.py:391
  14.4 38.2 %shard_map.100 = (f32[128,128]{1,0:T(8,128)}, f32[13,32,128]{2,1,0:T(8,128)}) custom-call(f32[128,128]{1,0:T(8,128)} %pad.4.rows_ref, f32[13,32,128]{2,1,0:T(8,128)} %pad_maximum_fusion.part_ref), custom_call_target="tpu_custom_call" | custom-call | tf_op jit(solution)/shard_map/pallas_call | solution.py:225
  52.7 0.9 copy.38
  53.6 0.7 slice_bitcast_fusion.2
  56.0 8.9 %shard_map.101 = f32[1,32,128]{2,1,0:T(8,128)} custom-call(f32[1,32,128]{2,1,0:T(8,128)} %bitcast.72), custom_call_target="tpu_custom_call" | custom-call | tf_op jit(solution)/shard_map/pallas_call | solution.py:267
  65.0 0.7 add_divide_fusion
  68.6 0.9 fusion.42
  69.5 1.9 %slice_reduce_fusion.8 = (f32[12,3,32]{2,1,0:T(4,128)}, f32[12,3,32]{2,1,0:T(4,128)}, f32[12,3,32,1]{3,2,1,0:T(8,128)}, f32[12,3,32,1]{3,2,1,0:T(8,128)}) fusion(f32[12,3,32,128]{3,2,1,0:T(8,128)S(1)} %multiply_add_fusion.1), kind=kLoop, calls=%fused_computation.107 | loop fusion | bytes 27648 | tf_op jit(solution)/shard_map/slice | solution.py:409
  71.3 0.8 reshape_squeeze.25
  72.2 0.8 reshape_squeeze.24
  72.9 1.3 pad_maximum_fusion.1
  74.2 8.1 %shard_map.102 = (f32[39,32]{1,0:T(8,128)}, f32[39,32]{1,0:T(8,128)}, f32[39,128]{1,0:T(8,128)}, f32[39,128]{1,0:T(8,128)}) custom-call(f32[39,32]{1,0:T(8,128)} %get-tuple-element.59.col_last, f32[39,32]{1,0:T(8,128)} %get-tuple-element.60.col_first, f32[39,128]{1,0:T(8,128)} %get-tuple-element.61.row_last, f32[39,128]{1,0:T(8,128)} %get-tuple-element.62.row_first), custom_call_target="tpu_custom_call" | custom-call | tf_op jit(solution)/shard_map/pallas_call | solution.py:79
  83.7 1.3 broadcast_in_dim.254
  85.8 1.4 broadcast_in_dim.267
  87.1 1.4 broadcast_in_dim.262
  88.5 1.3 broadcast_in_dim.257
  89.8 1.5 %fusion.35 = f32[3,32,128]{2,1,0:T(8,128)} fusion(f32[3,31,128]{2,1,0:T(8,128)} %bitcast.68, f32[3,1,128]{2,1,0:T(1,128)S(1)} %copy.42, f32[3,128]{1,0:T(4,128)S(1)} %get-tuple-element.55, pred[32]{0:T(512)(128)(4,1)} %broadcast_and_fusion), kind=kLoop, calls=%fused_computation.60 | loop fusion | flops 49152 | bytes 99872 | tf_op jit(solution)/shard_map/jit(_where)/select_n | solution.py:433
  91.3 1.5 %select_add_fusion = f32[3,32,128]{2,1,0:T(8,128)} fusion(f32[3,32,128]{2,1,0:T(8,128)} %param.12, f32[3,128]{1,0:T(4,128)S(1)} %minimum_negate_fusion, pred[32]{0:T(512)(128)(4,1)} %broadcast_and_fusion.1), kind=kLoop, calls=%fused_computation.61 | loop fusion | flops 36864 | bytes 99872 | tf_op jit(solution)/shard_map/add | solution.py:430
  93.0 3.0 %multiply_reduce_fusion = (f32[12,32,128]{2,1,0:T(8,128)}, f32[12,3,32,128]{3,2,1,0:T(8,128)S(1)}) fusion(f32[3,32,128]{2,1,0:T(8,128)} %param.15, f32[3,32,128]{2,1,0:T(8,128)} %get-tuple-element.54, f32[12,3,31,128]{3,2,1,0:T(8,128)S(1)} %copy-done.1, f32[12,3,1,128]{3,2,1,0:T(1,128)} %get-tuple-element.52, f32[12,3,128]{2,1,0:T(4,128)} %broadcast_in_dim.267, ...), kind=kLoop, calls=%fused_computation.37 | loop fusion | flops 3932160 | bytes 4420928 | tf_op jit(solution)/shard_map/reduce_sum | solution.py:402
  96.0 14.3 %shard_map.103 = f32[12,32,128]{2,1,0:T(8,128)} custom-call(f32[12,32,128]{2,1,0:T(8,128)} %get-tuple-element.35.part_ref), custom_call_target="tpu_custom_call" | custom-call | flops 196608 | bytes 1966080 | tf_op jit(solution)/shard_map/pallas_call | solution.py:285
  110.3 0.9 broadcast_divide_fusion
  114.2 1.9 %slice_reduce_fusion.6 = (f32[12,3,32]{2,1,0:T(4,128)}, f32[12,3,32]{2,1,0:T(4,128)}, f32[12,3,32,1]{3,2,1,0:T(8,128)}, f32[12,3,32,1]{3,2,1,0:T(8,128)}) fusion(f32[12,3,32,128]{3,2,1,0:T(8,128)S(1)} %multiply_add_fusion), kind=kLoop, calls=%fused_computation.105 | loop fusion | bytes 27648 | tf_op jit(solution)/shard_map/slice | solution.py:409
  116.1 1.4 %reshape_squeeze.29.col_first = f32[36,32]{1,0:T(8,128)} reshape(f32[12,3,32]{2,1,0:T(4,128)} %get-tuple-element.27) | data formatting | bytes 9216 | tf_op jit(solution)/shard_map/reshape;squeeze | solution.py:409
  117.5 1.4 reshape_squeeze.28.col_last
  118.8 10.8 %shard_map.104 = (f32[36,32]{1,0:T(8,128)}, f32[36,32]{1,0:T(8,128)}, f32[36,128]{1,0:T(8,128)}, f32[36,128]{1,0:T(8,128)}) custom-call(f32[36,32]{1,0:T(8,128)} %reshape_squeeze.28.col_last, f32[36,32]{1,0:T(8,128)} %reshape_squeeze.29.col_first, f32[36,128]{1,0:T(8,128)} %reshape_squeeze.30.row_last, f32[36,128]{1,0:T(8,128)} %reshape_squeeze.31.row_first), custom_call_target="tpu_custom_call" | custom-call | tf_op jit(solution)/shard_map/pallas_call | solution.py:79
  129.6 0.7 broadcast_in_dim.269
  130.3 0.7 broadcast_in_dim.271
  131.1 0.7 broadcast_in_dim.273
  132.6 2.9 %fusion.18 = f32[12,3,32,128]{3,2,1,0:T(8,128)} fusion(f32[12,3,32,1]{3,2,1,0:T(8,128)} %get-tuple-element.39, f32[12,3,32,127]{3,2,1,0:T(8,128)S(1)} %get-tuple-element.44, f32[12,3,32,127]{3,2,1,0:T(8,128)S(1)} %get-tuple-element.43, f32[12,3,32,1]{3,2,1,0:T(8,128)} %get-tuple-element.40, f32[12,3,1,128]{3,2,1,0:T(1,128)} %get-tuple-element.37, ...), kind=kLoop, calls=%fused_computation.26 | loop fusion | flops 3391488 | bytes 4076864 | tf_op jit(solution)/shard_map/add | solution.py:463
  (90 shorter events, 20.1 us)
Async XLA Ops:
  0.0 11.7 %copy-start.8 = (f32[3,32,128]{2,1,0:T(8,128)S(1)}, f32[3,32,128]{2,1,0:T(8,128)}, u32[]{:S(2)}) copy-start(f32[3,32,128]{2,1,0:T(8,128)} %param.15) | copy-start | bytes 147460
  0.0 11.7 %copy-start = (f32[12,3,32,128]{3,2,1,0:T(8,128)S(1)}, f32[12,3,32,128]{3,2,1,0:T(8,128)}, u32[]{:S(2)}) copy-start(f32[12,3,32,128]{3,2,1,0:T(8,128)} %param.10) | copy-start | bytes 1769476
  9.0 57.4 %copy-start.6 = (f32[3,32,128]{2,1,0:T(8,128)}, f32[3,32,128]{2,1,0:T(8,128)S(1)}, u32[]{:S(2)}) copy-start(f32[3,32,128]{2,1,0:T(8,128)S(1)} %broadcast_subtract_fusion) | copy-start | bytes 147460
  54.5 10.4 %copy-start.12 = (f32[13,32,128]{2,1,0:T(8,128)S(1)}, f32[13,32,128]{2,1,0:T(8,128)}, u32[]{:S(2)}) copy-start(f32[13,32,128]{2,1,0:T(8,128)} %get-tuple-element.16) | copy-start | bytes 638980
  54.9 11.5 %copy-start.4 = (f32[3,32,128]{2,1,0:T(8,128)S(1)}, f32[3,32,128]{2,1,0:T(8,128)}, u32[]{:S(2)}) copy-start(f32[3,32,128]{2,1,0:T(8,128)} %param.14) | copy-start | bytes 147460
  65.7 0.8 copy-start.2
  66.4 0.6 copy-start.11
  66.4 1.3 copy-start.13
  71.3 21.6 %copy-start.9 = (f32[3,32,128]{2,1,0:T(8,128)S(1)}, f32[3,32,128]{2,1,0:T(8,128)}, u32[]{:S(2)}) copy-start(f32[3,32,128]{2,1,0:T(8,128)} %param.11) | copy-start | bytes 147460
  71.3 21.6 %copy-start.1 = (f32[12,3,31,128]{3,2,1,0:T(8,128)S(1)}, f32[12,3,31,128]{3,2,1,0:T(8,128)}, u32[]{:S(2)}) copy-start(f32[12,3,31,128]{3,2,1,0:T(8,128)} %get-tuple-element.50) | copy-start | bytes 1714180
  93.0 3.0 %copy-start.10 = (f32[3,32,128]{2,1,0:T(8,128)}, f32[3,32,128]{2,1,0:T(8,128)S(1)}, u32[]{:S(2)}) copy-start(f32[3,32,128]{2,1,0:T(8,128)S(1)} %fusion.33) | copy-start | bytes 147460
  96.0 15.2 %copy-start.5 = (f32[3,32,128]{2,1,0:T(8,128)S(1)}, f32[3,32,128]{2,1,0:T(8,128)}, u32[]{:S(2)}) copy-start(f32[3,32,128]{2,1,0:T(8,128)} %param.14) | copy-start | bytes 147460
  96.0 15.2 %copy-start.7 = (f32[3,32,128]{2,1,0:T(8,128)S(1)}, f32[3,32,128]{2,1,0:T(8,128)}, u32[]{:S(2)}) copy-start(f32[3,32,128]{2,1,0:T(8,128)} %copy-done.6) | copy-start | bytes 147460
  111.3 0.7 copy-start.3
  114.2 18.4 %copy-start.14 = (pred[128]{0:T(512)(128)(4,1)S(1)}, pred[128]{0:T(512)(128)(4,1)}, u32[]{:S(2)}) copy-start(pred[128]{0:T(512)(128)(4,1)} %get-tuple-element.65) | copy-start | bytes 388
  114.2 18.4 %copy-start.15 = (pred[128]{0:T(512)(128)(4,1)S(1)}, pred[128]{0:T(512)(128)(4,1)}, u32[]{:S(2)}) copy-start(pred[128]{0:T(512)(128)(4,1)} %get-tuple-element.66) | copy-start | bytes 388
  114.2 18.4 %copy-start.16 = (pred[32]{0:T(512)(128)(4,1)S(1)}, pred[32]{0:T(512)(128)(4,1)}, u32[]{:S(2)}) copy-start(pred[32]{0:T(512)(128)(4,1)} %get-tuple-element.63) | copy-start | bytes 100
  114.2 18.4 %copy-start.17 = (pred[32]{0:T(512)(128)(4,1)S(1)}, pred[32]{0:T(512)(128)(4,1)}, u32[]{:S(2)}) copy-start(pred[32]{0:T(512)(128)(4,1)} %get-tuple-element.64) | copy-start | bytes 100

commit v9 on v7

--- a/solution.py
+++ b/solution.py
@@ -278,6 +278,118 @@
             collective_id=collective_id, has_side_effects=True
         ),
     )(x)
+
+
+def halo_places(lon_n, lat_n):
+    lon = lax.axis_index("lon")
+    lat = lax.axis_index("lat")
+    half = lon_n // 2
+    top = lat // (lat_n - 1)
+    inner = (lat + lat_n - 1) // lat_n
+    east = {"lon": lax.rem(lon + 1, lon_n)}
+    west = {"lon": lax.rem(lon + lon_n - 1, lon_n)}
+    up = {"lon": lax.rem(lon + half * top, lon_n), "lat": lat + 1 - top}
+    down = {"lon": lax.rem(lon + half * (1 - inner), lon_n), "lat": lat - inner}
+    return east, west, up, down, 1 - top, 1 - inner
+
+
+def mix_halo_body(lev_n, lon_n, lat_n, p_ref, pc_ref, ar_ref, ac_ref, mr_ref, mc_ref, tr_ref, tc_ref,
+                  cs_out, west_out, east_out, north_out, south_out,
+                  pieces, reduced, sends, recvs, gsends, grecvs,
+                  pc_slots, pc_send, pc_recv, colbuf, rowbuf, cols, rows, h_send, col_sem, row_sem):
+    lev = lax.axis_index("lev")
+    east, west, up, down, up_slot, down_slot = halo_places(lon_n, lat_n)
+    barrier = pltpu.get_barrier_semaphore()
+    for d in range(1, lev_n):
+        pl.semaphore_signal(
+            barrier, inc=1, device_id={"lev": lax.rem(lev + d, lev_n)}, device_id_type=MESH
+        )
+    for peer in (east, west, up, down):
+        pl.semaphore_signal(barrier, inc=1, device_id=peer, device_id_type=MESH)
+    pl.semaphore_wait(barrier, lev_n - 1 + 4)
+    scatter_start(lev_n, p_ref, pieces, sends, recvs)
+    for d in range(1, lev_n):
+        lev_copy(pc_ref, pc_slots.at[lev], pc_send.at[d - 1], pc_recv.at[lev], lax.rem(lev + d, lev_n)).start()
+    pc_slots[lev] = pc_ref[...]
+    scatter_finish_gather_start(lev_n, p_ref, pieces, reduced, sends, recvs, gsends, grecvs)
+    for d in range(1, lev_n):
+        sender = lax.rem(lev + lev_n - d, lev_n)
+        lev_copy(pc_ref, pc_slots.at[sender], pc_send.at[d - 1], pc_recv.at[sender], sender).wait_recv()
+        lev_copy(pc_ref, pc_slots.at[sender], pc_send.at[d - 1], pc_recv.at[sender], lax.rem(lev + d, lev_n)).wait_send()
+    pc_sum = pc_slots[0]
+    for s in range(1, lev_n):
+        pc_sum = pc_sum + pc_slots[s]
+    gather_finish(lev_n, cs_out, reduced, gsends, grecvs)
+    last_row = cs_out.shape[1] - 1
+    for e, r in ((0, last_row), (1, 0)):
+        cs_row = cs_out[:, r, :]
+        m = mr_ref[e]
+        rowbuf[e] = (1.0 - m) * ar_ref[e] + m * (cs_row[None] / tr_ref[e][None])
+        mc = mc_ref[e]
+        colbuf[e] = (1.0 - mc) * ac_ref[e] + mc * (pc_sum[e][None] / tc_ref[e][None])
+    plan = (
+        (colbuf.at[0], cols.at[0], col_sem.at[0], east),
+        (colbuf.at[1], cols.at[1], col_sem.at[1], west),
+        (rowbuf.at[0], rows.at[up_slot], row_sem.at[up_slot], up),
+        (rowbuf.at[1], rows.at[down_slot], row_sem.at[down_slot], down),
+    )
+    copies = []
+    for i, (src, dst, sem, peer) in enumerate(plan):
+        copy = pltpu.make_async_remote_copy(
+            src_ref=src, dst_ref=dst, send_sem=h_send.at[i], recv_sem=sem,
+            device_id=peer, device_id_type=MESH,
+        )
+        copy.start()
+        copies.append(copy)
+    for src, dst, sem in (
+        (colbuf.at[0], cols.at[0], col_sem.at[0]),
+        (colbuf.at[1], cols.at[1], col_sem.at[1]),
+        (rowbuf.at[0], rows.at[0], row_sem.at[0]),
+        (rowbuf.at[1], rows.at[1], row_sem.at[1]),
+    ):
+        pltpu.make_async_remote_copy(
+            src_ref=src, dst_ref=dst, send_sem=h_send.at[0], recv_sem=sem,
+            device_id=east, device_id_type=MESH,
+        ).wait_recv()
+    for copy in copies:
+        copy.wait_send()
+    west_out[...] = cols[0]
+    east_out[...] = cols[1]
+    north_out[...] = rows[0]
+    south_out[...] = rows[1]
+
+
+def mix_halo(p, pc, ar, ac, mr, mc, tr, tc, collective_id):
+    lev_n, lon_n, lat_n = lax.axis_size("lev"), lax.axis_size("lon"), lax.axis_size("lat")
+    vmem = pl.BlockSpec(memory_space=pltpu.VMEM)
+    col_shape, row_shape = ac.shape[1:], ar.shape[1:]
+    return pl.pallas_call(
+        functools.partial(mix_halo_body, lev_n, lon_n, lat_n),
+        out_shape=(
+            jax.ShapeDtypeStruct(p.shape, p.dtype),
+            jax.ShapeDtypeStruct(col_shape, p.dtype),
+            jax.ShapeDtypeStruct(col_shape, p.dtype),
+            jax.ShapeDtypeStruct(row_shape, p.dtype),
+            jax.ShapeDtypeStruct(row_shape, p.dtype),
+        ),
+        in_specs=[vmem] * 8,
+        out_specs=(vmem,) * 5,
+        scratch_shapes=lev_scratch(lev_n, p.shape, p.dtype) + [
+            pltpu.VMEM((lev_n,) + pc.shape, p.dtype),
+            pltpu.SemaphoreType.DMA((lev_n - 1,)),
+            pltpu.SemaphoreType.DMA((lev_n,)),
+            pltpu.VMEM(ac.shape, p.dtype),
+            pltpu.VMEM(ar.shape, p.dtype),
+            pltpu.VMEM(ac.shape, p.dtype),
+            pltpu.VMEM(ar.shape, p.dtype),
+            pltpu.SemaphoreType.DMA((4,)),
+            pltpu.SemaphoreType.DMA((2,)),
+            pltpu.SemaphoreType.DMA((2,)),
+        ],
+        compiler_params=pltpu.CompilerParams(
+            collective_id=collective_id, has_side_effects=True
+        ),
+    )(p, pc, ar, ac, mr, mc, tr, tc)
 
 
 def lev_sum(x, collective_id):
@@ -400,43 +512,59 @@
             total_detrain = early[tracers]
         else:
             partial_sum = jnp.sum(detrain_share[None] * adjoint, axis=1)
-            column_sum = lev_sum(partial_sum, 1)
+            edge_cols = jnp.stack([partial_sum[:, :, -1], partial_sum[:, :, 0]])
+            edge_a_rows = jnp.stack([adjoint[:, :, -1, :], adjoint[:, :, 0, :]]).transpose(0, 2, 1, 3)
+            edge_a_cols = jnp.stack([adjoint[:, :, :, -1], adjoint[:, :, :, 0]]).transpose(0, 2, 1, 3)
+            edge_m_rows = jnp.stack([mix_fraction[:, -1:, :], mix_fraction[:, :1, :]])
+            edge_m_cols = jnp.stack([mix_fraction[:, :, -1], mix_fraction[:, :, 0]])[:, :, None, :]
+            edge_t_rows = jnp.stack([total_detrain[-1:, :], total_detrain[:1, :]])
+            edge_t_cols = jnp.stack([total_detrain[:, -1], total_detrain[:, 0]])[:, None, :]
+            column_sum, west_k, east_k, north_k, south_k = mix_halo(
+                partial_sum, edge_cols, edge_a_rows, edge_a_cols,
+                edge_m_rows, edge_m_cols, edge_t_rows, edge_t_cols, 5,
+            )
         adjoint = (1.0 - mix_fraction)[None] * adjoint + mix_fraction[None] * (
             column_sum / total_detrain
         )[:, None]
+        if position == 1:
+            west_halo = jnp.swapaxes(west_k, 0, 1).reshape(tracers * lev_dev, lat_rows)
+            east_halo = jnp.swapaxes(east_k, 0, 1).reshape(tracers * lev_dev, lat_rows)
+            north_halo = jnp.swapaxes(north_k, 0, 1).reshape(tracers * lev_dev, lon_cols)
+            south_halo = jnp.swapaxes(south_k, 0, 1).reshape(tracers * lev_dev, lon_cols)
         planes = tracers * lev_dev
-        col_last = adjoint[:, :, :, -1].reshape(planes, lat_rows)
-        col_first = adjoint[:, :, :, 0].reshape(planes, lat_rows)
-        row_last = adjoint[:, :, -1, :].reshape(planes, lon_cols)
-        row_first = adjoint[:, :, 0, :].reshape(planes, lon_cols)
         if position == 0:
-            col_last = jnp.concatenate([col_last, east_courant[:, :, -1]], axis=0)
-            col_first = jnp.concatenate([col_first, east_courant[:, :, 0]], axis=0)
-            row_last = jnp.concatenate([row_last, north_courant[:, -1, :]], axis=0)
-            row_first = jnp.concatenate([row_first, pole_courant], axis=0)
-        west_halo, east_halo, north_halo, south_halo = halo_swap(
-            col_last, col_first, row_last, row_first, 2 + position
-        )
-        if position == 0:
-            west_wind = jnp.concatenate(
-                [west_halo[planes:, :, None], east_courant[:, :, :-1]], axis=2
+            col_last = adjoint[:, :, :, -1].reshape(planes, lat_rows)
+            col_first = adjoint[:, :, :, 0].reshape(planes, lat_rows)
+            row_last = adjoint[:, :, -1, :].reshape(planes, lon_cols)
+            row_first = adjoint[:, :, 0, :].reshape(planes, lon_cols)
+            if position == 0:
+                col_last = jnp.concatenate([col_last, east_courant[:, :, -1]], axis=0)
+                col_first = jnp.concatenate([col_first, east_courant[:, :, 0]], axis=0)
+                row_last = jnp.concatenate([row_last, north_courant[:, -1, :]], axis=0)
+                row_first = jnp.concatenate([row_first, pole_courant], axis=0)
+            west_halo, east_halo, north_halo, south_halo = halo_swap(
+                col_last, col_first, row_last, row_first, 2 + position
             )
-            partner_top = north_halo[planes:]
-            south_wind = jnp.concatenate(
-                [south_halo[planes:, None, :], north_courant[:, :-1, :]], axis=1
-            )
-            partner_pole = south_halo[planes:]
-            upwind_west = -jnp.minimum(west_wind, 0.0)
-            upwind_north = jnp.maximum(north_courant, 0.0) + jnp.where(
-                at_top, -jnp.minimum(partner_top, 0.0)[:, None, :], 0.0
-            )
-            upwind_south = jnp.where(
-                at_bottom,
-                (jnp.maximum(pole_courant, 0.0) - jnp.minimum(partner_pole, 0.0))[:, None, :],
-                -jnp.minimum(south_wind, 0.0),
-            )
-            west_halo, east_halo = west_halo[:planes], east_halo[:planes]
-            north_halo, south_halo = north_halo[:planes], south_halo[:planes]
+            if position == 0:
+                west_wind = jnp.concatenate(
+                    [west_halo[planes:, :, None], east_courant[:, :, :-1]], axis=2
+                )
+                partner_top = north_halo[planes:]
+                south_wind = jnp.concatenate(
+                    [south_halo[planes:, None, :], north_courant[:, :-1, :]], axis=1
+                )
+                partner_pole = south_halo[planes:]
+                upwind_west = -jnp.minimum(west_wind, 0.0)
+                upwind_north = jnp.maximum(north_courant, 0.0) + jnp.where(
+                    at_top, -jnp.minimum(partner_top, 0.0)[:, None, :], 0.0
+                )
+                upwind_south = jnp.where(
+                    at_bottom,
+                    (jnp.maximum(pole_courant, 0.0) - jnp.minimum(partner_pole, 0.0))[:, None, :],
+                    -jnp.minimum(south_wind, 0.0),
+                )
+                west_halo, east_halo = west_halo[:planes], east_halo[:planes]
+                north_halo, south_halo = north_halo[:planes], south_halo[:planes]
         east_side = jnp.concatenate(
             [adjoint[:, :, :, 1:], east_halo.reshape(tracers, lev_dev, lat_rows, 1)], axis=3
         )

time: 113 us -> 209 us (1.85)
  local copies, waits for them, and re-layouts: 17 us -> 80.8 us
  other arithmetic: 13.6 us -> 49.4 us
  Pallas kernels: 80.2 us -> 75.8 us
    slice x0 -> x8, local copies, waits for them, and re-layouts: none -> 12.7 us  [the longest x2 6.03 us: on_device(): adjoint[:, :, -1, :]]
    reduce_sum x1, other arithmetic: 1.37 us -> 12.2 us  [on_device(): partial_sum = jnp.sum(detrain_share[None] * adjoint, axis=1)]
    pallas_call x2 -> x1, Pallas kernels: 18.9 us -> 8.15 us  [halo_swap(): pl.pallas_call(functools.partial(halo_body, lon_n, lat_n), out_shape=(jax...]
    add x1, other arithmetic: 2.63 us -> 10.3 us  [on_device(): adjoint + upwind_east * (east_side - adjoint)]
    slice x1, local copies, waits for them, and re-layouts: 0.11 us -> 6.56 us  [on_device(): adjoint[:, :, :-1, :]]
    pallas_call x1, Pallas kernels: 14.1 us -> 20.5 us  [mix_halo(): pl.pallas_call(functools.partial(mix_halo_body, lev_n, lon_n, lat_n), out...]
    slice x2, local copies, waits for them, and re-layouts: 0.22 us -> 6.25 us  [on_device(): row_first = adjoint[:, :, 0, :].reshape(planes, lon_cols)]
    another operation x0 -> x9, local copies, waits for them, and re-layouts: none -> 5.2 us  [the longest x1 2.26 us: on_device(): south_halo.reshape(tracers, lev_dev, 1, lon_cols)]
where the time goes in v9:
time: 209 us; the launch traced here: 207 us
  local copies, waits for them, and re-layouts  80.8 us (39%)
  Pallas kernels  75.8 us (36%)
  other arithmetic  49.4 us (24%)
    pallas_call x1, Pallas kernels, exchange(): pl.pallas_call(functools.partial(exchange_body, lev_n, owners, lat_n), ou...  38.3 us
    pallas_call x1, Pallas kernels, mix_halo(): pl.pallas_call(functools.partial(mix_halo_body, lev_n, lon_n, lat_n), out...  20.5 us
    reduce_sum x1, other arithmetic, on_device(): partial_sum = jnp.sum(detrain_share[None] * adjoint, axis=1)  12.2 us
    add x1, other arithmetic, on_device(): adjoint + upwind_east * (east_side - adjoint)  10.3 us
    pallas_call x1, Pallas kernels, lev_direct(): pl.pallas_call(functools.partial(lev_direct_body, n), out_shape=jax.Shape...  8.92 us
    pallas_call x1, Pallas kernels, halo_swap(): pl.pallas_call(functools.partial(halo_body, lon_n, lat_n), out_shape=(jax...  8.15 us
    slice x1, local copies, waits for them, and re-layouts, on_device(): adjoint[:, :, :-1, :]  6.56 us
    slice x2, local copies, waits for them, and re-layouts, on_device(): row_first = adjoint[:, :, 0, :].reshape(planes, lon_cols)  6.25 us

profile of v9, /device:TPU:1, one launch (start us, length us, event | category | flops | bytes accessed | tf_op | source)
XLA Modules:
  0.0 206.9 jit_solution(14835030192564853100)
XLA Ops:
  7.8 2.1 %copy.186 = f32[12,3,32,128]{2,0,1,3:T(8,128)S(1)} copy(f32[12,3,32,128]{3,2,1,0:T(8,128)} %param.10) | data formatting | bytes 1179648 | tf_op args[0]
  10.0 1.8 multiply_reduce_fusion.1
  11.8 2.2 %copy.182 = f32[12,32,128]{2,1,0:T(8,128)} copy(f32[12,32,128]{1,0,2:T(8,128)} %multiply_reduce_fusion.1) | data formatting | bytes 393216 | tf_op jit(solution)/shard_map/reduce_sum | solution.py:486
  14.0 1.6 pad_maximum_fusion.part_ref
  15.7 38.3 %shard_map.100 = (f32[128,128]{1,0:T(8,128)}, f32[13,32,128]{2,1,0:T(8,128)}) custom-call(f32[128,128]{1,0:T(8,128)} %pad.4.rows_ref, f32[13,32,128]{2,1,0:T(8,128)} %pad_maximum_fusion.part_ref), custom_call_target="tpu_custom_call" | custom-call | tf_op jit(solution)/shard_map/pallas_call | solution.py:225
  58.2 8.9 %shard_map.101 = f32[1,32,128]{2,1,0:T(8,128)} custom-call(f32[1,32,128]{2,1,0:T(8,128)} %bitcast.119), custom_call_target="tpu_custom_call" | custom-call | tf_op jit(solution)/shard_map/pallas_call | solution.py:267
  71.3 3.0 %multiply_add_fusion.1 = f32[12,3,32,128]{2,0,1,3:T(8,128)S(1)} fusion(f32[12,3,32,128]{2,0,1,3:T(8,128)} %copy-done.1, f32[12,32,128]{1,0,2:T(8,128)} %copy.188, f32[3,32,128]{1,0,2:T(4,128)S(1)} %copy.187, f32[3,32,128]{1,0,2:T(4,128)} %copy.185, f32[3,32,128]{1,0,2:T(4,128)} %copy.173), kind=kLoop, calls=%fused_computation.27 | loop fusion | flops 589824 | bytes 1523712 | tf_op jit(solution)/shard_map/add | solution.py:526
  74.3 3.7 %fusion.35 = (f32[12,3,31,128]{2,0,1,3:T(8,128)}, f32[12,3,31,128]{2,0,1,3:T(8,128)}) fusion(f32[12,3,32,128]{2,0,1,3:T(8,128)S(1)} %multiply_add_fusion.1), kind=kLoop, calls=%fused_computation.110 | loop fusion | bytes 2285568 | tf_op jit(solution)/shard_map/slice | solution.py:575
  83.6 3.6 %fusion.36 = (f32[12,3,1,128]{2,0,1,3:T(8,128)}, f32[12,3,1,128]{2,0,1,3:T(8,128)}) fusion(f32[12,3,32,128]{2,0,1,3:T(8,128)S(1)} %multiply_add_fusion.1), kind=kLoop, calls=%fused_computation.111 | loop fusion | bytes 73728 | tf_op jit(solution)/shard_map/slice | solution.py:539
  87.1 2.7 %copy.192 = f32[12,3,1,128]{3,1,0,2:T(4,128)S(1)} copy(f32[12,3,1,128]{2,0,1,3:T(8,128)} %get-tuple-element.48) | data formatting | bytes 36864 | tf_op jit(solution)/shard_map/slice | solution.py:538
  90.5 2.7 %copy.194 = f32[12,3,1,128]{3,1,0,2:T(4,128)S(1)} copy(f32[12,3,1,128]{2,0,1,3:T(8,128)} %get-tuple-element.47) | data formatting | bytes 36864 | tf_op jit(solution)/shard_map/slice | solution.py:539
  95.1 8.1 %shard_map.102 = (f32[39,32]{1,0:T(8,128)}, f32[39,32]{1,0:T(8,128)}, f32[39,128]{1,0:T(8,128)}, f32[39,128]{1,0:T(8,128)}) custom-call(f32[39,32]{1,0:T(8,128)} %get-tuple-element.63.col_last, f32[39,32]{1,0:T(8,128)} %get-tuple-element.64.col_first, f32[39,128]{1,0:T(8,128)} %get-tuple-element.65.row_last, f32[39,128]{1,0:T(8,128)} %get-tuple-element.66.row_first), custom_call_target="tpu_custom_call" | custom-call | tf_op jit(solution)/shard_map/pallas_call | solution.py:79
  104.0 2.3 %copy.203 = f32[12,3,1,128]{2,0,1,3:T(8,128)} copy(f32[12,3,1,128]{3,1,0,2:T(4,128)S(1)} %reshape.190) | data formatting | bytes 36864 | tf_op jit(solution)/shard_map/reshape | solution.py:578
  108.5 1.6 copy.202
  110.9 2.3 %copy.200 = f32[12,3,1,128]{2,0,1,3:T(8,128)} copy(f32[12,3,1,128]{3,1,0,2:T(4,128)S(1)} %reshape.189) | data formatting | bytes 36864 | tf_op jit(solution)/shard_map/reshape | solution.py:575
  115.4 1.6 copy.199
  117.0 3.0 %fusion.34 = (f32[12,3,32,127]{2,0,1,3:T(8,128)}, f32[12,3,32,127]{2,0,1,3:T(8,128)}) fusion(f32[12,3,32,128]{2,0,1,3:T(8,128)S(1)} %multiply_add_fusion.1), kind=kLoop, calls=%fused_computation.109 | loop fusion | bytes 2340864 | tf_op jit(solution)/shard_map/slice | solution.py:569
  124.0 12.2 %multiply_reduce_fusion = (f32[12,32,128]{1,0,2:T(8,128)}, f32[12,3,32,128]{2,0,1,3:T(8,128)S(1)}) fusion(f32[3,32,128]{1,0,2:T(4,128)} %copy-done.2, f32[3,32,128]{1,0,2:T(4,128)} %copy.204, f32[12,3,31,128]{2,0,1,3:T(8,128)} %get-tuple-element.46, f32[12,3,1,128]{2,0,1,3:T(8,128)} %copy.203, f32[3,32,128]{1,0,2:T(4,128)} %copy.202, ...), kind=kLoop, calls=%fused_computation.26 | loop fusion | flops 3342336 | bytes 4374528 | tf_op jit(solution)/shard_map/reduce_sum | solution.py:514
  136.1 2.2 %copy.209.p_ref = f32[12,32,128]{2,1,0:T(8,128)} copy(f32[12,32,128]{1,0,2:T(8,128)} %get-tuple-element.33) | data formatting | bytes 393216 | tf_op jit(solution)/shard_map/reduce_sum | solution.py:514
  139.7 3.7 %fusion.33 = (f32[12,3,1,128]{2,0,1,3:T(8,128)}, f32[12,3,1,128]{2,0,1,3:T(8,128)}) fusion(f32[12,3,32,128]{2,0,1,3:T(8,128)S(1)} %get-tuple-element.34), kind=kLoop, calls=%fused_computation.108 | loop fusion | bytes 73728 | tf_op jit(solution)/shard_map/slice | solution.py:516
  143.3 2.4 %copy.206 = f32[12,3,1,128]{3,2,1,0:T(1,128)S(1)} copy(f32[12,3,1,128]{2,0,1,3:T(8,128)} %get-tuple-element.42) | data formatting | bytes 36864 | tf_op jit(solution)/shard_map/slice | solution.py:516
  145.7 2.4 %copy.205 = f32[12,3,1,128]{3,2,1,0:T(1,128)S(1)} copy(f32[12,3,1,128]{2,0,1,3:T(8,128)} %get-tuple-element.41) | data formatting | bytes 36864 | tf_op jit(solution)/shard_map/slice | solution.py:516
  152.8 20.5 %shard_map.103 = (f32[12,32,128]{2,1,0:T(8,128)}, f32[3,12,32]{2,1,0:T(8,128)}, f32[3,12,32]{2,1,0:T(8,128)}, f32[3,12,128]{2,1,0:T(8,128)}, f32[3,12,128]{2,1,0:T(8,128)}) custom-call(f32[12,32,128]{2,1,0:T(8,128)} %copy.209.p_ref, f32[2,12,32]{2,1,0:T(8,128)} %pad_maximum_fusion.6.pc_ref, f32[2,3,12,128]{3,2,1,0:T(8,128)} %maximum_bitcast_fusion.ar_ref, ...), custom_call_target="tpu_custom_call" | custom-call | tf_op jit(solution)/shard_map/pallas_call | solution.py:366
  173.3 1.6 broadcast_divide_fusion
  174.9 2.3 %copy.212 = f32[12,32,128]{1,0,2:T(8,128)} copy(f32[12,32,128]{2,1,0:T(8,128)} %broadcast_divide_fusion) | data formatting | bytes 393216 | tf_op jit(solution)/shard_map/div | solution.py:527
  177.2 1.8 multiply_add_fusion
  179.1 3.3 %fusion.32 = (f32[12,3,32,127]{2,0,1,3:T(8,128)}, f32[12,3,32,127]{2,0,1,3:T(8,128)}) fusion(f32[12,3,32,128]{2,0,1,3:T(8,128)S(1)} %multiply_add_fusion), kind=kLoop, calls=%fused_computation.107 | loop fusion | bytes 2340864 | tf_op jit(solution)/shard_map/slice | solution.py:572
  182.6 2.2 %copy.213 = f32[12,3,1,128]{2,0,1,3:T(8,128)} copy(f32[12,3,1,128]{3,0,2,1:T(8,128)S(1)} %bitcast.127) | data formatting | bytes 36864 | tf_op jit(solution)/shard_map/reshape;reshape | solution.py:575
  184.8 6.6 %fusion.31 = (f32[12,3,31,128]{2,0,1,3:T(8,128)}, f32[12,3,31,128]{2,0,1,3:T(8,128)}) fusion(f32[12,3,32,128]{2,0,1,3:T(8,128)} %copy-done), kind=kLoop, calls=%fused_computation.106 | loop fusion | bytes 2285568 | tf_op jit(solution)/shard_map/slice | solution.py:578
  191.3 2.3 %copy.214 = f32[12,3,1,128]{2,0,1,3:T(8,128)} copy(f32[12,3,1,128]{3,0,2,1:T(8,128)S(1)} %bitcast.126) | data formatting | bytes 36864 | tf_op jit(solution)/shard_map/reshape;reshape | solution.py:578
  193.6 10.3 %fusion.13 = f32[12,3,32,128]{2,0,1,3:T(8,128)} fusion(f32[12,3,32,1]{2,0,1,3:T(8,128)S(1)} %bitcast.129, f32[12,3,32,127]{2,0,1,3:T(8,128)} %get-tuple-element.38, f32[12,3,32,127]{2,0,1,3:T(8,128)} %get-tuple-element.37, f32[12,3,32,1]{2,0,1,3:T(8,128)S(1)} %bitcast.128, f32[12,3,1,128]{2,0,1,3:T(8,128)} %copy.213, ...), kind=kLoop, calls=%fused_computation.18 | loop fusion | flops 2801664 | bytes 4030464 | tf_op jit(solution)/shard_map/add | solution.py:581
  203.9 3.0 %copy.215 = f32[12,3,32,128]{3,2,1,0:T(8,128)} copy(f32[12,3,32,128]{2,0,1,3:T(8,128)} %fusion.13) | data formatting | bytes 1179648 | tf_op jit(solution)/shard_map/add | solution.py:581
  (111 shorter events, 40.3 us)
Async XLA Ops:
  1.0 10.9 %copy-start.2 = (f32[3,32,128]{1,0,2:T(4,128)}, f32[3,32,128]{1,0,2:T(4,128)S(1)}, u32[]{:S(2)}) copy-start(f32[3,32,128]{1,0,2:T(4,128)S(1)} %copy.180) | copy-start | bytes 147460
  10.0 44.0 %copy-start.1 = (f32[12,3,32,128]{2,0,1,3:T(8,128)}, f32[12,3,32,128]{2,0,1,3:T(8,128)S(1)}, u32[]{:S(2)}) copy-start(f32[12,3,32,128]{2,0,1,3:T(8,128)S(1)} %copy.186) | copy-start | bytes 1769476
  11.8 45.7 %copy-start.5 = (f32[3,32,128]{2,1,0:T(8,128)S(1)}, f32[3,32,128]{2,1,0:T(8,128)}, u32[]{:S(2)}) copy-start(f32[3,32,128]{2,1,0:T(8,128)} %param.15) | copy-start | bytes 147460
  11.8 57.6 %copy-start.3 = (f32[3,32,128]{2,1,0:T(8,128)S(1)}, f32[3,32,128]{2,1,0:T(8,128)}, u32[]{:S(2)}) copy-start(f32[3,32,128]{2,1,0:T(8,128)} %param.14) | copy-start | bytes 147460
  74.3 3.7 %copy-start.4 = (f32[3,32,128]{2,1,0:T(8,128)S(1)}, f32[3,32,128]{2,1,0:T(8,128)}, u32[]{:S(2)}) copy-start(f32[3,32,128]{2,1,0:T(8,128)} %param.11) | copy-start | bytes 147460
  87.1 6.6 %copy-start.11 = (f32[3,128]{1,0:T(4,128)S(1)}, f32[3,128]{1,0:T(4,128)}, u32[]{:S(2)}) copy-start(f32[3,128]{1,0:T(4,128)} %param.13) | copy-start | bytes 4612
  117.0 3.0 %copy-start.6 = (f32[39,32]{1,0:T(8,128)S(1)}, f32[39,32]{1,0:T(8,128)}, u32[]{:S(2)}) copy-start(f32[39,32]{1,0:T(8,128)} %get-tuple-element.19) | copy-start | bytes 14980
  179.0 3.5 %copy-start = (f32[12,3,32,128]{2,0,1,3:T(8,128)}, f32[12,3,32,128]{2,0,1,3:T(8,128)S(1)}, u32[]{:S(2)}) copy-start(f32[12,3,32,128]{2,0,1,3:T(8,128)S(1)} %multiply_add_fusion) | copy-start | bytes 1769476
  179.1 3.5 %copy-start.8 = (f32[3,12,128]{2,1,0:T(8,128)S(1)}, f32[3,12,128]{2,1,0:T(8,128)}, u32[]{:S(2)}) copy-start(f32[3,12,128]{2,1,0:T(8,128)} %get-tuple-element.25) | copy-start | bytes 55300
  184.8 6.6 %copy-start.7 = (f32[3,12,128]{2,1,0:T(8,128)S(1)}, f32[3,12,128]{2,1,0:T(8,128)}, u32[]{:S(2)}) copy-start(f32[3,12,128]{2,1,0:T(8,128)} %get-tuple-element.26) | copy-start | bytes 55300
  191.3 2.3 %copy-start.9 = (f32[3,12,32]{2,1,0:T(8,128)S(1)}, f32[3,12,32]{2,1,0:T(8,128)}, u32[]{:S(2)}) copy-start(f32[3,12,32]{2,1,0:T(8,128)} %get-tuple-element.24) | copy-start | bytes 13828
  191.3 2.3 %copy-start.10 = (f32[3,12,32]{2,1,0:T(8,128)S(1)}, f32[3,12,32]{2,1,0:T(8,128)}, u32[]{:S(2)}) copy-start(f32[3,12,32]{2,1,0:T(8,128)} %get-tuple-element.23) | copy-start | bytes 13828

commit v10 on v9

--- a/solution.py
+++ b/solution.py
@@ -293,10 +293,9 @@
     return east, west, up, down, 1 - top, 1 - inner
 
 
-def mix_halo_body(lev_n, lon_n, lat_n, p_ref, pc_ref, ar_ref, ac_ref, mr_ref, mc_ref, tr_ref, tc_ref,
-                  cs_out, west_out, east_out, north_out, south_out,
+def mix_halo_body(lev_n, lon_n, lat_n, p_ref, pe_ref, ae_ref, me_ref, te_ref, cs_out, halo_out,
                   pieces, reduced, sends, recvs, gsends, grecvs,
-                  pc_slots, pc_send, pc_recv, colbuf, rowbuf, cols, rows, h_send, col_sem, row_sem):
+                  pe_slots, pe_send, pe_recv, mixed, got, h_send, h_recv):
     lev = lax.axis_index("lev")
     east, west, up, down, up_slot, down_slot = halo_places(lon_n, lat_n)
     barrier = pltpu.get_barrier_semaphore()
@@ -309,29 +308,23 @@
     pl.semaphore_wait(barrier, lev_n - 1 + 4)
     scatter_start(lev_n, p_ref, pieces, sends, recvs)
     for d in range(1, lev_n):
-        lev_copy(pc_ref, pc_slots.at[lev], pc_send.at[d - 1], pc_recv.at[lev], lax.rem(lev + d, lev_n)).start()
-    pc_slots[lev] = pc_ref[...]
+        lev_copy(pe_ref, pe_slots.at[lev], pe_send.at[d - 1], pe_recv.at[lev], lax.rem(lev + d, lev_n)).start()
+    pe_slots[lev] = pe_ref[...]
     scatter_finish_gather_start(lev_n, p_ref, pieces, reduced, sends, recvs, gsends, grecvs)
     for d in range(1, lev_n):
         sender = lax.rem(lev + lev_n - d, lev_n)
-        lev_copy(pc_ref, pc_slots.at[sender], pc_send.at[d - 1], pc_recv.at[sender], sender).wait_recv()
-        lev_copy(pc_ref, pc_slots.at[sender], pc_send.at[d - 1], pc_recv.at[sender], lax.rem(lev + d, lev_n)).wait_send()
-    pc_sum = pc_slots[0]
+        lev_copy(pe_ref, pe_slots.at[sender], pe_send.at[d - 1], pe_recv.at[sender], sender).wait_recv()
+        lev_copy(pe_ref, pe_slots.at[sender], pe_send.at[d - 1], pe_recv.at[sender], lax.rem(lev + d, lev_n)).wait_send()
+    pe_sum = pe_slots[0]
     for s in range(1, lev_n):
-        pc_sum = pc_sum + pc_slots[s]
-    gather_finish(lev_n, cs_out, reduced, gsends, grecvs)
-    last_row = cs_out.shape[1] - 1
-    for e, r in ((0, last_row), (1, 0)):
-        cs_row = cs_out[:, r, :]
-        m = mr_ref[e]
-        rowbuf[e] = (1.0 - m) * ar_ref[e] + m * (cs_row[None] / tr_ref[e][None])
-        mc = mc_ref[e]
-        colbuf[e] = (1.0 - mc) * ac_ref[e] + mc * (pc_sum[e][None] / tc_ref[e][None])
+        pe_sum = pe_sum + pe_slots[s]
+    share = me_ref[...]
+    mixed[...] = (1.0 - share) * ae_ref[...] + share * (pe_sum / te_ref[...])
     plan = (
-        (colbuf.at[0], cols.at[0], col_sem.at[0], east),
-        (colbuf.at[1], cols.at[1], col_sem.at[1], west),
-        (rowbuf.at[0], rows.at[up_slot], row_sem.at[up_slot], up),
-        (rowbuf.at[1], rows.at[down_slot], row_sem.at[down_slot], down),
+        (mixed.at[0], got.at[0], h_recv.at[0], east),
+        (mixed.at[1], got.at[1], h_recv.at[1], west),
+        (mixed.at[2], got.at[2 + up_slot], h_recv.at[2 + up_slot], up),
+        (mixed.at[3], got.at[2 + down_slot], h_recv.at[2 + down_slot], down),
     )
     copies = []
     for i, (src, dst, sem, peer) in enumerate(plan):
@@ -341,55 +334,41 @@
         )
         copy.start()
         copies.append(copy)
-    for src, dst, sem in (
-        (colbuf.at[0], cols.at[0], col_sem.at[0]),
-        (colbuf.at[1], cols.at[1], col_sem.at[1]),
-        (rowbuf.at[0], rows.at[0], row_sem.at[0]),
-        (rowbuf.at[1], rows.at[1], row_sem.at[1]),
-    ):
+    gather_finish(lev_n, cs_out, reduced, gsends, grecvs)
+    for i in range(4):
         pltpu.make_async_remote_copy(
-            src_ref=src, dst_ref=dst, send_sem=h_send.at[0], recv_sem=sem,
+            src_ref=mixed.at[i], dst_ref=got.at[i], send_sem=h_send.at[i], recv_sem=h_recv.at[i],
             device_id=east, device_id_type=MESH,
         ).wait_recv()
     for copy in copies:
         copy.wait_send()
-    west_out[...] = cols[0]
-    east_out[...] = cols[1]
-    north_out[...] = rows[0]
-    south_out[...] = rows[1]
-
-
-def mix_halo(p, pc, ar, ac, mr, mc, tr, tc, collective_id):
+    halo_out[...] = got[...]
+
+
+def mix_halo(p, pe, ae, me, te, collective_id):
     lev_n, lon_n, lat_n = lax.axis_size("lev"), lax.axis_size("lon"), lax.axis_size("lat")
     vmem = pl.BlockSpec(memory_space=pltpu.VMEM)
-    col_shape, row_shape = ac.shape[1:], ar.shape[1:]
     return pl.pallas_call(
         functools.partial(mix_halo_body, lev_n, lon_n, lat_n),
         out_shape=(
             jax.ShapeDtypeStruct(p.shape, p.dtype),
-            jax.ShapeDtypeStruct(col_shape, p.dtype),
-            jax.ShapeDtypeStruct(col_shape, p.dtype),
-            jax.ShapeDtypeStruct(row_shape, p.dtype),
-            jax.ShapeDtypeStruct(row_shape, p.dtype),
-        ),
-        in_specs=[vmem] * 8,
-        out_specs=(vmem,) * 5,
+            jax.ShapeDtypeStruct(pe.shape, p.dtype),
+        ),
+        in_specs=[vmem] * 5,
+        out_specs=(vmem, vmem),
         scratch_shapes=lev_scratch(lev_n, p.shape, p.dtype) + [
-            pltpu.VMEM((lev_n,) + pc.shape, p.dtype),
+            pltpu.VMEM((lev_n,) + pe.shape, p.dtype),
             pltpu.SemaphoreType.DMA((lev_n - 1,)),
             pltpu.SemaphoreType.DMA((lev_n,)),
-            pltpu.VMEM(ac.shape, p.dtype),
-            pltpu.VMEM(ar.shape, p.dtype),
-            pltpu.VMEM(ac.shape, p.dtype),
-            pltpu.VMEM(ar.shape, p.dtype),
+            pltpu.VMEM(pe.shape, p.dtype),
+            pltpu.VMEM(pe.shape, p.dtype),
             pltpu.SemaphoreType.DMA((4,)),
-            pltpu.SemaphoreType.DMA((2,)),
-            pltpu.SemaphoreType.DMA((2,)),
+            pltpu.SemaphoreType.DMA((4,)),
         ],
         compiler_params=pltpu.CompilerParams(
             collective_id=collective_id, has_side_effects=True
         ),
-    )(p, pc, ar, ac, mr, mc, tr, tc)
+    )(p, pe, ae, me, te)
 
 
 def lev_sum(x, collective_id):
@@ -512,25 +491,34 @@
             total_detrain = early[tracers]
         else:
             partial_sum = jnp.sum(detrain_share[None] * adjoint, axis=1)
-            edge_cols = jnp.stack([partial_sum[:, :, -1], partial_sum[:, :, 0]])
-            edge_a_rows = jnp.stack([adjoint[:, :, -1, :], adjoint[:, :, 0, :]]).transpose(0, 2, 1, 3)
-            edge_a_cols = jnp.stack([adjoint[:, :, :, -1], adjoint[:, :, :, 0]]).transpose(0, 2, 1, 3)
-            edge_m_rows = jnp.stack([mix_fraction[:, -1:, :], mix_fraction[:, :1, :]])
-            edge_m_cols = jnp.stack([mix_fraction[:, :, -1], mix_fraction[:, :, 0]])[:, :, None, :]
-            edge_t_rows = jnp.stack([total_detrain[-1:, :], total_detrain[:1, :]])
-            edge_t_cols = jnp.stack([total_detrain[:, -1], total_detrain[:, 0]])[:, None, :]
-            column_sum, west_k, east_k, north_k, south_k = mix_halo(
-                partial_sum, edge_cols, edge_a_rows, edge_a_cols,
-                edge_m_rows, edge_m_cols, edge_t_rows, edge_t_cols, 5,
+            planes = tracers * lev_dev
+
+            def spread(x, width, fill=0.0):
+                x = jnp.broadcast_to(x, (tracers, lev_dev, width)).reshape(planes, width)
+                return jnp.pad(x, ((0, 0), (0, lon_cols - width)), constant_values=fill)
+
+            def edges(x, fill=0.0):
+                return jnp.stack([
+                    spread(x[..., :, -1], lat_rows, fill), spread(x[..., :, 0], lat_rows, fill),
+                    spread(x[..., -1, :], lon_cols), spread(x[..., 0, :], lon_cols),
+                ])
+
+            column_sum, halos = mix_halo(
+                partial_sum,
+                edges(partial_sum[:, None]),
+                edges(adjoint),
+                edges(mix_fraction[None]),
+                edges(total_detrain[None, None], 1.0),
+                5,
             )
         adjoint = (1.0 - mix_fraction)[None] * adjoint + mix_fraction[None] * (
             column_sum / total_detrain
         )[:, None]
         if position == 1:
-            west_halo = jnp.swapaxes(west_k, 0, 1).reshape(tracers * lev_dev, lat_rows)
-            east_halo = jnp.swapaxes(east_k, 0, 1).reshape(tracers * lev_dev, lat_rows)
-            north_halo = jnp.swapaxes(north_k, 0, 1).reshape(tracers * lev_dev, lon_cols)
-            south_halo = jnp.swapaxes(south_k, 0, 1).reshape(tracers * lev_dev, lon_cols)
+            west_halo = halos[0, :, :lat_rows]
+            east_halo = halos[1, :, :lat_rows]
+            north_halo = halos[2]
+            south_halo = halos[3]
         planes = tracers * lev_dev
         if position == 0:
             col_last = adjoint[:, :, :, -1].reshape(planes, lat_rows)

time: 209 us -> 105 us (0.50)
  local copies, waits for them, and re-layouts: 80.8 us -> 12 us
  other arithmetic: 49.4 us -> 13.9 us
    reduce_sum x1, other arithmetic: 12.2 us -> 0.7 us  [on_device(): partial_sum = jnp.sum(detrain_share[None] * adjoint, axis=1)]
    slice x8 -> x9, local copies, waits for them, and re-layouts: 12.7 us -> 2.03 us  [the longest x4 1.23 us: edges(): x[..., :, -1]]
    add x1, other arithmetic: 10.3 us -> 2.66 us  [on_device(): adjoint + upwind_east * (east_side - adjoint)]
    slice x1, local copies, waits for them, and re-layouts: 6.56 us -> 0.11 us  [on_device(): adjoint[:, :, :-1, :]]
    slice x2 -> x1, local copies, waits for them, and re-layouts: 6.25 us -> 0.11 us  [on_device(): row_first = adjoint[:, :, 0, :].reshape(planes, lon_cols)]
    add x2 -> x0, local copies, waits for them, and re-layouts: 4.65 us -> none  [the longest x1 3.01 us: on_device(): adjoint + upwind_east * (east_side - adjoint)]
    add x2, other arithmetic: 4.79 us -> 0.19 us  [on_device(): (1.0 - mix_fraction)[None] * adjoint]
    div x3 -> x0, local copies, waits for them, and re-layouts: 4.44 us -> none  [on_device(): column_sum / total_detrain]
where the time goes in v10:
time: 105 us; the launch traced here: 103 us
  Pallas kernels  75.9 us (72%)
  other arithmetic  13.9 us (13%)
  local copies, waits for them, and re-layouts  12 us (11%)
    pallas_call x1, Pallas kernels, exchange(): pl.pallas_call(functools.partial(exchange_body, lev_n, owners, lat_n), ou...  38.2 us
    pallas_call x1, Pallas kernels, mix_halo(): pl.pallas_call(functools.partial(mix_halo_body, lev_n, lon_n, lat_n), out...  20.6 us
    pallas_call x1, Pallas kernels, lev_direct(): pl.pallas_call(functools.partial(lev_direct_body, n), out_shape=jax.Shape...  8.92 us
    pallas_call x1, Pallas kernels, halo_swap(): pl.pallas_call(functools.partial(halo_body, lon_n, lat_n), out_shape=(jax...  8.14 us
    add x1, other arithmetic, on_device(): adjoint + upwind_east * (east_side - adjoint)  2.66 us
    another operation x4, other arithmetic, edges(): jnp.stack([spread(x[..., :, -1], lat_rows, fill), spread(x[..., :, 0], la...  2.58 us

profile of v10, /device:TPU:1, one launch (start us, length us, event | category | flops | bytes accessed | tf_op | source)
XLA Modules:
  0.0 103.1 jit_solution(14631548723146257321)
XLA Ops:
  0.0 0.7 copy.112
  0.9 0.7 fusion.28
  1.8 0.7 iota_compare_fusion.4
  2.5 0.7 broadcast_select_fusion
  3.6 0.4 reshape.230
  4.8 0.6 pad.29.rows_ref
  5.5 0.7 pad_maximum_fusion.part_ref
  6.2 38.2 %shard_map.100 = (f32[128,128]{1,0:T(8,128)}, f32[13,32,128]{2,1,0:T(8,128)}) custom-call(f32[128,128]{1,0:T(8,128)} %pad.29.rows_ref, f32[13,32,128]{2,1,0:T(8,128)} %pad_maximum_fusion.part_ref), custom_call_target="tpu_custom_call" | custom-call | tf_op jit(solution)/shard_map/pallas_call | solution.py:225
  44.5 0.9 copy.62
  46.0 0.5 fusion.18
  46.5 0.6 multiply_reduce_fusion.2
  47.1 8.9 %shard_map.101 = f32[1,32,128]{2,1,0:T(8,128)} custom-call(f32[1,32,128]{2,1,0:T(8,128)} %bitcast.110), custom_call_target="tpu_custom_call" | custom-call | tf_op jit(solution)/shard_map/pallas_call | solution.py:267
  56.0 0.7 add_divide_fusion
  57.0 0.6 slice_reduce_fusion.2
  57.9 0.6 pad_maximum_fusion.5
  58.7 0.6 pad_maximum_fusion.7
  59.3 8.1 %shard_map.102 = (f32[39,32]{1,0:T(8,128)}, f32[39,32]{1,0:T(8,128)}, f32[39,128]{1,0:T(8,128)}, f32[39,128]{1,0:T(8,128)}) custom-call(f32[39,32]{1,0:T(8,128)} %get-tuple-element.65.col_last, f32[39,32]{1,0:T(8,128)} %get-tuple-element.66.col_first, f32[39,128]{1,0:T(8,128)} %get-tuple-element.67.row_last, f32[39,128]{1,0:T(8,128)} %get-tuple-element.68.row_first), custom_call_target="tpu_custom_call" | custom-call | tf_op jit(solution)/shard_map/pallas_call | solution.py:79
  67.5 1.3 %reshape.231 = f32[12,3,32,1]{3,2,1,0:T(8,128)S(1)} reshape(f32[36,32]{1,0:T(8,128)} %bitcast.119) | data formatting | bytes 9216 | tf_op jit(solution)/shard_map/reshape | solution.py:557
  68.9 0.6 reshape.232
  70.3 0.7 multiply_reduce_fusion
  71.0 0.6 slice_reduce_fusion.1
  71.8 0.6 pad_maximum_fusion.2.ae_ref
  72.9 0.6 pad_maximum_fusion.1.pe_ref
  73.8 0.6 pad_maximum_fusion.4.te_ref
  74.8 0.7 pad_maximum_fusion.3.me_ref
  75.4 20.6 %shard_map.103 = (f32[12,32,128]{2,1,0:T(8,128)}, f32[4,36,128]{2,1,0:T(8,128)}) custom-call(f32[12,32,128]{2,1,0:T(8,128)} %copy-done.1, f32[4,36,128]{2,1,0:T(8,128)} %pad_maximum_fusion.1.pe_ref, f32[4,36,128]{2,1,0:T(8,128)} %pad_maximum_fusion.2.ae_ref, f32[4,36,128]{2,1,0:T(8,128)} %pad_maximum_fusion.3.me_ref, f32[4,36,128]{2,1,0:T(8,128)} %pad_maximum_fusion.4.te_ref), custom_call_target="tpu_custom_call" | custom-call | tf_op jit(solution)/shard_map/pallas_call | solution.py:351
  96.0 0.9 broadcast_divide_fusion
  97.2 1.2 %fusion.32 = (f32[12,3,32,127]{3,2,1,0:T(8,128)}, f32[12,3,32,127]{3,2,1,0:T(8,128)}) fusion(f32[12,3,32,128]{3,2,1,0:T(8,128)S(1)} %multiply_add_fusion), kind=kLoop, calls=%fused_computation.119 | loop fusion | bytes 2340864 | tf_op jit(solution)/shard_map/slice | solution.py:560
  98.4 0.6 reshape_squeeze.42
  99.0 0.6 reshape_squeeze.43
  99.6 0.8 fusion.37
  100.4 2.7 %fusion.13 = f32[12,3,32,128]{3,2,1,0:T(8,128)} fusion(f32[12,3,32,1]{3,2,1,0:T(8,128)S(1)} %reshape_squeeze.42, f32[12,3,32,127]{3,2,1,0:T(8,128)} %get-tuple-element.40, f32[12,3,32,127]{3,2,1,0:T(8,128)} %get-tuple-element.39, f32[12,3,32,1]{3,2,1,0:T(8,128)S(1)} %reshape_squeeze.43, f32[12,3,1,128]{3,2,1,0:T(1,128)S(1)} %reshape_squeeze.40, ...), kind=kLoop, calls=%fused_computation.25 | loop fusion | flops 2801664 | bytes 4030464 | tf_op jit(solution)/shard_map/add | solution.py:569
  (119 shorter events, 4.7 us)
Async XLA Ops:
  1.8 2.4 %copy-start.12 = (s32[2,256]{1,0:T(2,128)S(1)}, s32[2,256]{1,0:T(2,128)}, u32[]{:S(2)}) copy-start(s32[2,256]{1,0:T(2,128)} %param.17) | copy-start | bytes 6148
  3.6 1.8 %copy-start = (f32[12,3,32,128]{3,2,1,0:T(8,128)S(1)}, f32[12,3,32,128]{3,2,1,0:T(8,128)}, u32[]{:S(2)}) copy-start(f32[12,3,32,128]{3,2,1,0:T(8,128)} %param.10) | copy-start | bytes 1769476
  3.6 1.8 %copy-start.3 = (f32[3,32,128]{2,1,0:T(8,128)S(1)}, f32[3,32,128]{2,1,0:T(8,128)}, u32[]{:S(2)}) copy-start(f32[3,32,128]{2,1,0:T(8,128)} %param.15) | copy-start | bytes 147460
  45.6 10.4 %copy-start.5 = (f32[13,32,128]{2,1,0:T(8,128)S(1)}, f32[13,32,128]{2,1,0:T(8,128)}, u32[]{:S(2)}) copy-start(f32[13,32,128]{2,1,0:T(8,128)} %get-tuple-element.14) | copy-start | bytes 638980
  46.0 10.8 %copy-start.2 = (f32[3,32,128]{2,1,0:T(8,128)S(1)}, f32[3,32,128]{2,1,0:T(8,128)}, u32[]{:S(2)}) copy-start(f32[3,32,128]{2,1,0:T(8,128)} %param.14) | copy-start | bytes 147460
  56.9 0.8 copy-start.4
  56.9 1.7 %copy-start.6 = (f32[3,32,128]{2,1,0:T(8,128)S(1)}, f32[3,32,128]{2,1,0:T(8,128)}, u32[]{:S(2)}) copy-start(f32[3,32,128]{2,1,0:T(8,128)} %param.12) | copy-start | bytes 147460
  57.0 1.7 %copy-start.11 = (f32[3,128]{1,0:T(4,128)S(1)}, f32[3,128]{1,0:T(4,128)}, u32[]{:S(2)}) copy-start(f32[3,128]{1,0:T(4,128)} %param.13) | copy-start | bytes 4612
  67.5 1.4 %copy-start.8 = (f32[39,32]{1,0:T(8,128)S(1)}, f32[39,32]{1,0:T(8,128)}, u32[]{:S(2)}) copy-start(f32[39,32]{1,0:T(8,128)} %get-tuple-element.16) | copy-start | bytes 14980
  67.5 2.2 %copy-start.9 = (f32[39,128]{1,0:T(8,128)S(1)}, f32[39,128]{1,0:T(8,128)}, u32[]{:S(2)}) copy-start(f32[39,128]{1,0:T(8,128)} %get-tuple-element.18) | copy-start | bytes 59908
  68.8 1.0 copy-start.10
  71.0 1.8 %copy-start.1 = (f32[12,32,128]{2,1,0:T(8,128)}, f32[12,32,128]{2,1,0:T(8,128)S(1)}, u32[]{:S(2)}) copy-start(f32[12,32,128]{2,1,0:T(8,128)S(1)} %get-tuple-element.35.p_ref) | copy-start | bytes 589828
  97.2 1.2 %copy-start.7 = (f32[4,36,128]{2,1,0:T(8,128)S(1)}, f32[4,36,128]{2,1,0:T(8,128)}, u32[]{:S(2)}) copy-start(f32[4,36,128]{2,1,0:T(8,128)} %get-tuple-element.20) | copy-start | bytes 221188

commit v11 on v10

--- a/solution.py
+++ b/solution.py
@@ -293,7 +293,7 @@
     return east, west, up, down, 1 - top, 1 - inner
 
 
-def mix_halo_body(lev_n, lon_n, lat_n, p_ref, pe_ref, ae_ref, me_ref, te_ref, cs_out, halo_out,
+def mix_halo_body(lev_n, lon_n, lat_n, with_base, p_ref, pe_ref, ae_ref, me_ref, te_ref, be_ref, cs_out, halo_out,
                   pieces, reduced, sends, recvs, gsends, grecvs,
                   pe_slots, pe_send, pe_recv, mixed, got, h_send, h_recv):
     lev = lax.axis_index("lev")
@@ -319,6 +319,8 @@
     for s in range(1, lev_n):
         pe_sum = pe_sum + pe_slots[s]
     share = me_ref[...]
+    if with_base:
+        pe_sum = be_ref[...] + pe_sum
     mixed[...] = (1.0 - share) * ae_ref[...] + share * (pe_sum / te_ref[...])
     plan = (
         (mixed.at[0], got.at[0], h_recv.at[0], east),
@@ -345,16 +347,16 @@
     halo_out[...] = got[...]
 
 
-def mix_halo(p, pe, ae, me, te, collective_id):
+def mix_halo(p, pe, ae, me, te, be, collective_id):
     lev_n, lon_n, lat_n = lax.axis_size("lev"), lax.axis_size("lon"), lax.axis_size("lat")
     vmem = pl.BlockSpec(memory_space=pltpu.VMEM)
     return pl.pallas_call(
-        functools.partial(mix_halo_body, lev_n, lon_n, lat_n),
+        functools.partial(mix_halo_body, lev_n, lon_n, lat_n, be is not None),
         out_shape=(
             jax.ShapeDtypeStruct(p.shape, p.dtype),
             jax.ShapeDtypeStruct(pe.shape, p.dtype),
         ),
-        in_specs=[vmem] * 5,
+        in_specs=[vmem] * 6,
         out_specs=(vmem, vmem),
         scratch_shapes=lev_scratch(lev_n, p.shape, p.dtype) + [
             pltpu.VMEM((lev_n,) + pe.shape, p.dtype),
@@ -368,7 +370,7 @@
         compiler_params=pltpu.CompilerParams(
             collective_id=collective_id, has_side_effects=True
         ),
-    )(p, pe, ae, me, te)
+    )(p, pe, ae, me, te, pe if be is None else be)
 
 
 def lev_sum(x, collective_id):
@@ -480,79 +482,79 @@
     at_top = jnp.logical_and(lat_place == lat_count - 1, row_index == lat_rows - 1)
     at_bottom = jnp.logical_and(lat_place == 0, row_index == 0)
     upwind_east = jnp.maximum(east_courant, 0.0)
-    forcing_part = jnp.sum(detrain_share * forcing_grid[step_count - 1], axis=0)
-    forcing_sum = lev_direct(forcing_part[None], 4)[0]
+    total_detrain = early[tracers]
+    planes = tracers * lev_dev
+
+    def spread(x, width, fill=0.0):
+        x = jnp.broadcast_to(x, (tracers, lev_dev, width)).reshape(planes, width)
+        return jnp.pad(x, ((0, 0), (0, lon_cols - width)), constant_values=fill)
+
+    def edges(x, fill=0.0):
+        return jnp.stack([
+            spread(x[..., :, -1], lat_rows, fill), spread(x[..., :, 0], lat_rows, fill),
+            spread(x[..., -1, :], lon_cols), spread(x[..., 0, :], lon_cols),
+        ])
+
+    def widen(x):
+        return jnp.pad(x, ((0, 0), (0, lon_cols - x.shape[1])))
+
+    extra_winds = jnp.stack([
+        widen(east_courant[:, :, -1]), widen(east_courant[:, :, 0]),
+        north_courant[:, -1, :], pole_courant,
+    ])
+    no_extra = jnp.zeros_like(extra_winds)
     adjoint = adjoint_field
     for position in range(step_count):
         step_now = step_count - 1 - position
         adjoint = adjoint + forcing_grid[step_now][None]
         if position == 0:
-            column_sum = early[:tracers] + forcing_sum[None]
-            total_detrain = early[tracers]
+            forcing_part = jnp.sum(detrain_share * forcing_grid[step_now], axis=0)
+            fsum, halos = mix_halo(
+                forcing_part[None],
+                jnp.concatenate([edges(forcing_part[None, None]), no_extra], axis=1),
+                jnp.concatenate([edges(adjoint), extra_winds], axis=1),
+                jnp.concatenate([edges(mix_fraction[None]), no_extra], axis=1),
+                jnp.concatenate([edges(total_detrain[None, None], 1.0), no_extra + 1.0], axis=1),
+                jnp.concatenate([edges(early[:tracers][:, None]), no_extra], axis=1),
+                6,
+            )
+            column_sum = early[:tracers] + fsum
         else:
             partial_sum = jnp.sum(detrain_share[None] * adjoint, axis=1)
-            planes = tracers * lev_dev
-
-            def spread(x, width, fill=0.0):
-                x = jnp.broadcast_to(x, (tracers, lev_dev, width)).reshape(planes, width)
-                return jnp.pad(x, ((0, 0), (0, lon_cols - width)), constant_values=fill)
-
-            def edges(x, fill=0.0):
-                return jnp.stack([
-                    spread(x[..., :, -1], lat_rows, fill), spread(x[..., :, 0], lat_rows, fill),
-                    spread(x[..., -1, :], lon_cols), spread(x[..., 0, :], lon_cols),
-                ])
-
             column_sum, halos = mix_halo(
                 partial_sum,
                 edges(partial_sum[:, None]),
                 edges(adjoint),
                 edges(mix_fraction[None]),
                 edges(total_detrain[None, None], 1.0),
+                None,
                 5,
             )
         adjoint = (1.0 - mix_fraction)[None] * adjoint + mix_fraction[None] * (
             column_sum / total_detrain
         )[:, None]
-        if position == 1:
-            west_halo = halos[0, :, :lat_rows]
-            east_halo = halos[1, :, :lat_rows]
-            north_halo = halos[2]
-            south_halo = halos[3]
-        planes = tracers * lev_dev
+        west_halo = halos[0, :planes, :lat_rows]
+        east_halo = halos[1, :planes, :lat_rows]
+        north_halo = halos[2, :planes]
+        south_halo = halos[3, :planes]
         if position == 0:
-            col_last = adjoint[:, :, :, -1].reshape(planes, lat_rows)
-            col_first = adjoint[:, :, :, 0].reshape(planes, lat_rows)
-            row_last = adjoint[:, :, -1, :].reshape(planes, lon_cols)
-            row_first = adjoint[:, :, 0, :].reshape(planes, lon_cols)
-            if position == 0:
-                col_last = jnp.concatenate([col_last, east_courant[:, :, -1]], axis=0)
-                col_first = jnp.concatenate([col_first, east_courant[:, :, 0]], axis=0)
-                row_last = jnp.concatenate([row_last, north_courant[:, -1, :]], axis=0)
-                row_first = jnp.concatenate([row_first, pole_courant], axis=0)
-            west_halo, east_halo, north_halo, south_halo = halo_swap(
-                col_last, col_first, row_last, row_first, 2 + position
+            west_wind = jnp.concatenate(
+                [halos[0, planes:, :lat_rows, None], east_courant[:, :, :-1]], axis=2
             )
-            if position == 0:
-                west_wind = jnp.concatenate(
-                    [west_halo[planes:, :, None], east_courant[:, :, :-1]], axis=2
-                )
-                partner_top = north_halo[planes:]
-                south_wind = jnp.concatenate(
-                    [south_halo[planes:, None, :], north_courant[:, :-1, :]], axis=1
-                )
-                partner_pole = south_halo[planes:]
-                upwind_west = -jnp.minimum(west_wind, 0.0)
-                upwind_north = jnp.maximum(north_courant, 0.0) + jnp.where(
-                    at_top, -jnp.minimum(partner_top, 0.0)[:, None, :], 0.0
-                )
-                upwind_south = jnp.where(
-                    at_bottom,
-                    (jnp.maximum(pole_courant, 0.0) - jnp.minimum(partner_pole, 0.0))[:, None, :],
-                    -jnp.minimum(south_wind, 0.0),
-                )
-                west_halo, east_halo = west_halo[:planes], east_halo[:planes]
-                north_halo, south_halo = north_halo[:planes], south_halo[:planes]
+            partner_top = halos[2, planes:]
+            south_wind = jnp.concatenate(
+                [halos[3, planes:, None, :], north_courant[:, :-1, :]], axis=1
+            )
+            partner_pole = halos[3, planes:]
+            upwind_west = -jnp.minimum(west_wind, 0.0)
+            upwind_north = jnp.maximum(north_courant, 0.0) + jnp.where(
+                at_top, -jnp.minimum(partner_top, 0.0)[:, None, :], 0.0
+            )
+            upwind_south = jnp.where(
+                at_bottom,
+                (jnp.maximum(pole_courant, 0.0) - jnp.minimum(partner_pole, 0.0))[:, None, :],
+                -jnp.minimum(south_wind, 0.0),
+            )
         east_side = jnp.concatenate(
             [adjoint[:, :, :, 1:], east_halo.reshape(tracers, lev_dev, lat_rows, 1)], axis=3
         )

time: 105 us -> 112 us (1.067); the launches traced: 103 us -> 111 us
  local copies, waits for them, and re-layouts: 12 us -> 16.6 us
  other arithmetic: 13.9 us -> 16.8 us
    reshape x4 -> x0, local copies, waits for them, and re-layouts: 1.97 us -> none  [the longest x1 1.33 us: on_device(): east_halo.reshape(tracers, lev_dev, lat_rows, 1)]
    reduce_sum x1, other arithmetic: 0.7 us -> 2.17 us  [on_device(): partial_sum = jnp.sum(detrain_share[None] * adjoint, axis=1)]
    concatenate x3 -> x4, local copies, waits for them, and re-layouts: 0.11 us -> 1.39 us  [the longest x1 0.66 us: on_device(): jnp.concatenate([edges(mix_fraction[None]), no_extra], axis=1)]
    slice x4 -> x7, local copies, waits for them, and re-layouts: 1.23 us -> 2.3 us  [edges(): x[..., :, -1]]
    pallas_call x3 -> x2, Pallas kernels: 37.7 us -> 38.2 us  [mix_halo(): pl.pallas_call(functools.partial(mix_halo_body, lev_n, lon_n, lat_n, be i...]
    another operation x4 -> x6, other arithmetic: 2.58 us -> 2.59 us  [edges(): jnp.stack([spread(x[..., :, -1], lat_rows, fill), spread(x[..., :, 0], la...]
where the time goes in v11:
time: 112 us; the launch traced here: 111 us
  Pallas kernels  76.4 us (68%)
  other arithmetic  16.8 us (15%)
  local copies, waits for them, and re-layouts  16.6 us (15%)
    pallas_call x1, Pallas kernels, exchange(): pl.pallas_call(functools.partial(exchange_body, lev_n, owners, lat_n), ou...  38.2 us
    pallas_call x2, Pallas kernels, mix_halo(): pl.pallas_call(functools.partial(mix_halo_body, lev_n, lon_n, lat_n, be i...  38.2 us
    add x1, other arithmetic, on_device(): adjoint + upwind_east * (east_side - adjoint)  2.66 us
    another operation x6, other arithmetic, edges(): jnp.stack([spread(x[..., :, -1], lat_rows, fill), spread(x[..., :, 0], la...  2.59 us
    slice x7, local copies, waits for them, and re-layouts, edges(): x[..., :, -1]  2.3 us

profile of v11, /device:TPU:1, one launch (start us, length us, event | category | flops | bytes accessed | tf_op | source)
XLA Modules:
  0.0 111.3 jit_solution(13172076079016866122)
XLA Ops:
  0.0 0.7 copy.114
  0.9 0.7 fusion.28
  1.8 0.7 iota_compare_fusion.5
  2.5 0.7 broadcast_select_fusion
  4.8 0.6 pad.62.rows_ref
  5.5 0.7 pad_maximum_fusion.part_ref
  6.2 38.2 %shard_map.100 = (f32[128,128]{1,0:T(8,128)}, f32[13,32,128]{2,1,0:T(8,128)}) custom-call(f32[128,128]{1,0:T(8,128)} %pad.62.rows_ref, f32[13,32,128]{2,1,0:T(8,128)} %pad_maximum_fusion.part_ref), custom_call_target="tpu_custom_call" | custom-call | tf_op jit(solution)/shard_map/pallas_call | solution.py:225
  44.5 0.9 copy.62
  46.5 0.6 slice_bitcast_fusion.2
  47.2 0.6 slice_reduce_fusion.3
  48.2 0.6 maximum_maximum_fusion.ae_ref
  49.1 0.6 select_maximum_fusion.3.pe_ref
  50.2 0.6 select_maximum_fusion.be_ref
  51.2 0.7 concatenate.72.te_ref
  52.2 0.7 concatenate.71.me_ref
  52.8 16.3 %shard_map.101 = (f32[1,32,128]{2,1,0:T(8,128)}, f32[4,39,128]{2,1,0:T(8,128)}) custom-call(f32[1,32,128]{2,1,0:T(8,128)} %bitcast.130, f32[4,39,128]{2,1,0:T(8,128)} %select_maximum_fusion.3.pe_ref, f32[4,39,128]{2,1,0:T(8,128)} %maximum_maximum_fusion.ae_ref, f32[4,39,128]{2,1,0:T(8,128)} %concatenate.71.me_ref, f32[4,39,128]{2,1,0:T(8,128)} %concatenate.72.te_ref, ...), custom_call_target="tpu_custom_call" | custom-call | tf_op jit(solution)/shard_map/pallas_call | solution.py:353
  69.1 0.7 negate_bitcast_fusion
  69.8 0.7 bitcast_subtract_fusion
  70.5 0.7 fusion.27
  71.2 0.7 add_divide_fusion
  72.1 1.0 fusion.34
  73.0 1.1 fusion.35
  75.5 0.7 fusion.25
  76.2 0.6 reshape_squeeze.44
  77.5 2.2 %multiply_reduce_fusion = (f32[12,32,128]{2,1,0:T(8,128)S(1)}, f32[12,3,32,128]{3,2,1,0:T(8,128)S(1)}) fusion(f32[3,32,128]{2,1,0:T(8,128)S(1)} %copy-done.4, f32[3,32,128]{2,1,0:T(8,128)} %get-tuple-element.54, f32[12,3,31,128]{3,2,1,0:T(8,128)} %get-tuple-element.44, f32[12,3,1,128]{3,2,1,0:T(1,128)} %reshape_squeeze.45, f32[3,32,128]{2,1,0:T(8,128)} %fusion.27, ...), kind=kLoop, calls=%fused_computation.33 | loop fusion | flops 3342336 | bytes 4374528 | tf_op jit(solution)/shard_map/reduce_sum | solution.py:523
  80.5 0.6 pad_maximum_fusion.4.ae_ref
  81.6 0.6 pad_maximum_fusion.3.pe_ref.be_ref
  82.3 21.9 %shard_map.102 = (f32[12,32,128]{2,1,0:T(8,128)}, f32[4,36,128]{2,1,0:T(8,128)}) custom-call(f32[12,32,128]{2,1,0:T(8,128)} %copy-done.1, f32[4,36,128]{2,1,0:T(8,128)} %pad_maximum_fusion.3.pe_ref.be_ref, f32[4,36,128]{2,1,0:T(8,128)} %pad_maximum_fusion.4.ae_ref, f32[4,36,128]{2,1,0:T(8,128)} %copy-done.8, f32[4,36,128]{2,1,0:T(8,128)} %copy-done.7, ...), custom_call_target="tpu_custom_call" | custom-call | tf_op jit(solution)/shard_map/pallas_call | solution.py:353
  104.2 0.9 broadcast_divide_fusion
  105.4 1.2 %fusion.32 = (f32[12,3,32,127]{3,2,1,0:T(8,128)}, f32[12,3,32,127]{3,2,1,0:T(8,128)}) fusion(f32[12,3,32,128]{3,2,1,0:T(8,128)S(1)} %multiply_add_fusion), kind=kLoop, calls=%fused_computation.136 | loop fusion | bytes 2340864 | tf_op jit(solution)/shard_map/slice | solution.py:562
  107.8 0.8 fusion.39
  108.6 2.7 %fusion.13 = f32[12,3,32,128]{3,2,1,0:T(8,128)} fusion(f32[12,3,32,1]{3,2,1,0:T(8,128)S(1)} %reshape_squeeze.54, f32[12,3,32,127]{3,2,1,0:T(8,128)} %get-tuple-element.38, f32[12,3,32,127]{3,2,1,0:T(8,128)} %get-tuple-element.37, f32[12,3,32,1]{3,2,1,0:T(8,128)S(1)} %reshape_squeeze.55, f32[12,3,1,128]{3,2,1,0:T(1,128)S(1)} %reshape_squeeze.50, ...), kind=kLoop, calls=%fused_computation.25 | loop fusion | flops 2801664 | bytes 4030464 | tf_op jit(solution)/shard_map/add | solution.py:571
  (165 shorter events, 9.1 us)
Async XLA Ops:
  1.8 2.4 %copy-start.21 = (s32[2,256]{1,0:T(2,128)S(1)}, s32[2,256]{1,0:T(2,128)}, u32[]{:S(2)}) copy-start(s32[2,256]{1,0:T(2,128)} %param.17) | copy-start | bytes 6148
  3.6 1.8 %copy-start = (f32[12,3,32,128]{3,2,1,0:T(8,128)S(1)}, f32[12,3,32,128]{3,2,1,0:T(8,128)}, u32[]{:S(2)}) copy-start(f32[12,3,32,128]{3,2,1,0:T(8,128)} %param.10) | copy-start | bytes 1769476
  3.6 1.8 %copy-start.4 = (f32[3,32,128]{2,1,0:T(8,128)S(1)}, f32[3,32,128]{2,1,0:T(8,128)}, u32[]{:S(2)}) copy-start(f32[3,32,128]{2,1,0:T(8,128)} %param.15) | copy-start | bytes 147460
  47.1 0.8 copy-start.5
  47.1 1.0 copy-start.16
  47.2 1.0 copy-start.20
  47.8 1.9 %copy-start.3 = (f32[13,32,128]{2,1,0:T(8,128)S(1)}, f32[13,32,128]{2,1,0:T(8,128)}, u32[]{:S(2)}) copy-start(f32[13,32,128]{2,1,0:T(8,128)} %get-tuple-element.12) | copy-start | bytes 638980
  48.8 1.3 %copy-start.15 = (f32[32,128]{1,0:T(8,128)}, f32[32,128]{1,0:T(8,128)S(1)}, u32[]{:S(2)}) copy-start(f32[32,128]{1,0:T(8,128)S(1)} %multiply_reduce_fusion.2) | copy-start | bytes 49156
  50.0 1.8 %copy-start.2 = (f32[3,32,128]{2,1,0:T(8,128)S(1)}, f32[3,32,128]{2,1,0:T(8,128)}, u32[]{:S(2)}) copy-start(f32[3,32,128]{2,1,0:T(8,128)} %param.14) | copy-start | bytes 147460
  51.2 18.0 %copy-start.7 = (f32[4,36,128]{2,1,0:T(8,128)}, f32[4,36,128]{2,1,0:T(8,128)S(1)}, u32[]{:S(2)}) copy-start(f32[4,36,128]{2,1,0:T(8,128)S(1)} %pad_maximum_fusion.2.te_ref) | copy-start | bytes 221188
  52.2 19.8 %copy-start.8 = (f32[4,36,128]{2,1,0:T(8,128)}, f32[4,36,128]{2,1,0:T(8,128)S(1)}, u32[]{:S(2)}) copy-start(f32[4,36,128]{2,1,0:T(8,128)S(1)} %pad_maximum_fusion.1.me_ref) | copy-start | bytes 221188
  73.0 1.1 copy-start.18
  74.2 1.3 %copy-start.6 = (f32[3,32,128]{2,1,0:T(8,128)S(1)}, f32[3,32,128]{2,1,0:T(8,128)}, u32[]{:S(2)}) copy-start(f32[3,32,128]{2,1,0:T(8,128)} %param.11) | copy-start | bytes 147460
  74.8 2.7 %copy-start.17 = (f32[3,32,128]{2,1,0:T(8,128)S(1)}, f32[3,32,128]{2,1,0:T(8,128)}, u32[]{:S(2)}) copy-start(f32[3,32,128]{2,1,0:T(8,128)} %param.12) | copy-start | bytes 147460
  77.5 2.2 %copy-start.10 = (f32[3,32,128]{2,1,0:T(8,128)}, f32[3,32,128]{2,1,0:T(8,128)S(1)}, u32[]{:S(2)}) copy-start(f32[3,32,128]{2,1,0:T(8,128)S(1)} %select_add_fusion) | copy-start | bytes 147460
  77.5 2.2 %copy-start.12 = (f32[3,32,128]{2,1,0:T(8,128)}, f32[3,32,128]{2,1,0:T(8,128)S(1)}, u32[]{:S(2)}) copy-start(f32[3,32,128]{2,1,0:T(8,128)S(1)} %broadcast_maximum_fusion) | copy-start | bytes 147460
  79.7 1.8 %copy-start.1 = (f32[12,32,128]{2,1,0:T(8,128)}, f32[12,32,128]{2,1,0:T(8,128)S(1)}, u32[]{:S(2)}) copy-start(f32[12,32,128]{2,1,0:T(8,128)S(1)} %get-tuple-element.33.p_ref) | copy-start | bytes 589828
  105.4 1.2 %copy-start.19 = (f32[4,36,128]{2,1,0:T(8,128)S(1)}, f32[4,36,128]{2,1,0:T(8,128)}, u32[]{:S(2)}) copy-start(f32[4,36,128]{2,1,0:T(8,128)} %get-tuple-element.16) | copy-start | bytes 221188
  106.6 2.1 %copy-start.9 = (f32[3,32,128]{2,1,0:T(8,128)S(1)}, f32[3,32,128]{2,1,0:T(8,128)}, u32[]{:S(2)}) copy-start(f32[3,32,128]{2,1,0:T(8,128)} %fusion.27) | copy-start | bytes 147460
  106.6 2.1 %copy-start.11 = (f32[3,32,128]{2,1,0:T(8,128)S(1)}, f32[3,32,128]{2,1,0:T(8,128)}, u32[]{:S(2)}) copy-start(f32[3,32,128]{2,1,0:T(8,128)} %copy-done.10) | copy-start | bytes 147460
  106.6 2.1 %copy-start.13 = (f32[3,32,128]{2,1,0:T(8,128)S(1)}, f32[3,32,128]{2,1,0:T(8,128)}, u32[]{:S(2)}) copy-start(f32[3,32,128]{2,1,0:T(8,128)} %copy-done.12) | copy-start | bytes 147460
  106.6 2.1 %copy-start.14 = (f32[3,32,128]{2,1,0:T(8,128)S(1)}, f32[3,32,128]{2,1,0:T(8,128)}, u32[]{:S(2)}) copy-start(f32[3,32,128]{2,1,0:T(8,128)} %fusion.25) | copy-start | bytes 147460

commit v12 on v11

--- a/solution.py
+++ b/solution.py
@@ -293,10 +293,11 @@
     return east, west, up, down, 1 - top, 1 - inner
 
 
-def mix_halo_body(lev_n, lon_n, lat_n, with_base, p_ref, pe_ref, ae_ref, me_ref, te_ref, be_ref, cs_out, halo_out,
+def mix_halo_body(lev_n, lon_n, lat_n, with_base, p_ref, st_ref, cs_out, halo_out,
                   pieces, reduced, sends, recvs, gsends, grecvs,
                   pe_slots, pe_send, pe_recv, mixed, got, h_send, h_recv):
     lev = lax.axis_index("lev")
+    pe_ref = st_ref.at[0]
     east, west, up, down, up_slot, down_slot = halo_places(lon_n, lat_n)
     barrier = pltpu.get_barrier_semaphore()
     for d in range(1, lev_n):
@@ -318,10 +319,10 @@
     pe_sum = pe_slots[0]
     for s in range(1, lev_n):
         pe_sum = pe_sum + pe_slots[s]
-    share = me_ref[...]
     if with_base:
-        pe_sum = be_ref[...] + pe_sum
-    mixed[...] = (1.0 - share) * ae_ref[...] + share * (pe_sum / te_ref[...])
+        pe_sum = st_ref[4] + pe_sum
+    share = st_ref[2]
+    mixed[...] = (1.0 - share) * st_ref[1] + share * (pe_sum / st_ref[3])
     plan = (
         (mixed.at[0], got.at[0], h_recv.at[0], east),
         (mixed.at[1], got.at[1], h_recv.at[1], west),
@@ -347,30 +348,30 @@
     halo_out[...] = got[...]
 
 
-def mix_halo(p, pe, ae, me, te, be, collective_id):
+def mix_halo(p, st, with_base, collective_id):
     lev_n, lon_n, lat_n = lax.axis_size("lev"), lax.axis_size("lon"), lax.axis_size("lat")
     vmem = pl.BlockSpec(memory_space=pltpu.VMEM)
     return pl.pallas_call(
-        functools.partial(mix_halo_body, lev_n, lon_n, lat_n, be is not None),
+        functools.partial(mix_halo_body, lev_n, lon_n, lat_n, with_base),
         out_shape=(
             jax.ShapeDtypeStruct(p.shape, p.dtype),
-            jax.ShapeDtypeStruct(pe.shape, p.dtype),
-        ),
-        in_specs=[vmem] * 6,
+            jax.ShapeDtypeStruct(st.shape[1:], p.dtype),
+        ),
+        in_specs=[vmem] * 2,
         out_specs=(vmem, vmem),
         scratch_shapes=lev_scratch(lev_n, p.shape, p.dtype) + [
-            pltpu.VMEM((lev_n,) + pe.shape, p.dtype),
+            pltpu.VMEM((lev_n,) + st.shape[1:], p.dtype),
             pltpu.SemaphoreType.DMA((lev_n - 1,)),
             pltpu.SemaphoreType.DMA((lev_n,)),
-            pltpu.VMEM(pe.shape, p.dtype),
-            pltpu.VMEM(pe.shape, p.dtype),
+            pltpu.VMEM(st.shape[1:], p.dtype),
+            pltpu.VMEM(st.shape[1:], p.dtype),
             pltpu.SemaphoreType.DMA((4,)),
             pltpu.SemaphoreType.DMA((4,)),
         ],
         compiler_params=pltpu.CompilerParams(
             collective_id=collective_id, has_side_effects=True
         ),
-    )(p, pe, ae, me, te, pe if be is None else be)
+    )(p, st)
 
 
 def lev_sum(x, collective_id):
@@ -511,11 +512,14 @@
             forcing_part = jnp.sum(detrain_share * forcing_grid[step_now], axis=0)
             fsum, halos = mix_halo(
                 forcing_part[None],
-                jnp.concatenate([edges(forcing_part[None, None]), no_extra], axis=1),
-                jnp.concatenate([edges(adjoint), extra_winds], axis=1),
-                jnp.concatenate([edges(mix_fraction[None]), no_extra], axis=1),
-                jnp.concatenate([edges(total_detrain[None, None], 1.0), no_extra + 1.0], axis=1),
-                jnp.concatenate([edges(early[:tracers][:, None]), no_extra], axis=1),
+                jnp.stack([
+                    jnp.concatenate([edges(forcing_part[None, None]), no_extra], axis=1),
+                    jnp.concatenate([edges(adjoint), extra_winds], axis=1),
+                    jnp.concatenate([edges(mix_fraction[None]), no_extra], axis=1),
+                    jnp.concatenate([edges(total_detrain[None, None], 1.0), no_extra + 1.0], axis=1),
+                    jnp.concatenate([edges(early[:tracers][:, None]), no_extra], axis=1),
+                ]),
+                True,
                 6,
             )
             column_sum = early[:tracers] + fsum
@@ -523,11 +527,13 @@
             partial_sum = jnp.sum(detrain_share[None] * adjoint, axis=1)
             column_sum, halos = mix_halo(
                 partial_sum,
-                edges(partial_sum[:, None]),
-                edges(adjoint),
-                edges(mix_fraction[None]),
-                edges(total_detrain[None, None], 1.0),
-                None,
+                jnp.stack([
+                    edges(partial_sum[:, None]),
+                    edges(adjoint),
+                    edges(mix_fraction[None]),
+                    edges(total_detrain[None, None], 1.0),
+                ]),
+                False,
                 5,
             )
         adjoint = (1.0 - mix_fraction)[None] * adjoint + mix_fraction[None] * (

time: 112 us -> 111 us (level)
    concatenate x2 -> x0, local copies, waits for them, and re-layouts: 1.31 us -> none  [the longest x1 0.66 us: on_device(): jnp.concatenate([edges(mix_fraction[None]), no_extra], axis=1)]
    unnamed x50, local copies, waits for them, and re-layouts: 0.84 us -> 2.14 us
where the time goes in v12:
time: 111 us; the launch traced here: 110 us
  Pallas kernels  76.3 us (69%)
  local copies, waits for them, and re-layouts  16.6 us (15%)
  other arithmetic  15.7 us (14%)
    pallas_call x1, Pallas kernels, exchange(): pl.pallas_call(functools.partial(exchange_body, lev_n, owners, lat_n), ou...  38.2 us
    pallas_call x2, Pallas kernels, mix_halo(): pl.pallas_call(functools.partial(mix_halo_body, lev_n, lon_n, lat_n, with...  38.1 us
    add x1, other arithmetic, on_device(): adjoint + upwind_east * (east_side - adjoint)  2.66 us
    slice x7, local copies, waits for them, and re-layouts, edges(): x[..., :, -1]  2.3 us

profile of v12, /device:TPU:1, one launch (start us, length us, event | category | flops | bytes accessed | tf_op | source)
XLA Modules:
  0.0 110.1 jit_solution(15405052452782725109)
XLA Ops:
  0.0 0.7 copy.114
  0.9 0.7 fusion.34
  1.8 0.7 iota_compare_fusion.5
  2.5 0.7 broadcast_select_fusion
  4.8 0.6 pad.62.rows_ref
  5.5 0.7 pad_maximum_fusion.1.part_ref
  6.2 38.2 %shard_map.100 = (f32[128,128]{1,0:T(8,128)}, f32[13,32,128]{2,1,0:T(8,128)}) custom-call(f32[128,128]{1,0:T(8,128)} %pad.62.rows_ref, f32[13,32,128]{2,1,0:T(8,128)} %pad_maximum_fusion.1.part_ref), custom_call_target="tpu_custom_call" | custom-call | tf_op jit(solution)/shard_map/pallas_call | solution.py:225
  44.5 0.9 copy.62
  46.8 0.6 slice_bitcast_fusion.2
  47.5 0.6 slice_reduce_fusion.3
  49.3 0.6 fusion.36
  50.2 0.6 fusion.33
  51.4 0.7 copy-done.6
  52.1 16.2 %shard_map.101 = (f32[1,32,128]{2,1,0:T(8,128)}, f32[4,39,128]{2,1,0:T(8,128)}) custom-call(f32[1,32,128]{2,1,0:T(8,128)} %bitcast.154, f32[5,4,39,128]{3,2,1,0:T(8,128)} %copy-done.6), custom_call_target="tpu_custom_call" | custom-call | tf_op jit(solution)/shard_map/pallas_call | solution.py:354
  68.3 0.7 negate_bitcast_fusion
  69.0 0.7 bitcast_subtract_fusion
  69.7 0.7 fusion.32
  70.4 0.7 add_divide_fusion
  71.2 1.0 fusion.41
  72.2 1.1 fusion.42
  73.9 0.6 reshape_squeeze.53
  74.6 0.7 fusion.30
  75.3 0.6 reshape_squeeze.44
  76.0 0.6 reshape_squeeze.45
  76.7 2.2 %multiply_reduce_fusion = (f32[12,32,128]{2,1,0:T(8,128)S(1)}, f32[12,3,32,128]{3,2,1,0:T(8,128)S(1)}) fusion(f32[3,32,128]{2,1,0:T(8,128)S(1)} %copy-done.4, f32[3,32,128]{2,1,0:T(8,128)} %get-tuple-element.54, f32[12,3,31,128]{3,2,1,0:T(8,128)} %get-tuple-element.44, f32[12,3,1,128]{3,2,1,0:T(1,128)} %reshape_squeeze.45, f32[3,32,128]{2,1,0:T(8,128)} %fusion.32, ...), kind=kLoop, calls=%fused_computation.33 | loop fusion | flops 3342336 | bytes 4374528 | tf_op jit(solution)/shard_map/reduce_sum | solution.py:527
  79.4 0.6 slice_reduce_fusion.1
  80.3 0.7 pad_maximum_fusion.st_ref
  81.1 21.9 %shard_map.102 = (f32[12,32,128]{2,1,0:T(8,128)}, f32[4,36,128]{2,1,0:T(8,128)}) custom-call(f32[12,32,128]{2,1,0:T(8,128)} %copy-done.1, f32[4,4,36,128]{3,2,1,0:T(8,128)} %pad_maximum_fusion.st_ref), custom_call_target="tpu_custom_call" | custom-call | tf_op jit(solution)/shard_map/pallas_call | solution.py:354
  103.0 0.9 broadcast_divide_fusion
  104.1 1.2 %fusion.39 = (f32[12,3,32,127]{3,2,1,0:T(8,128)}, f32[12,3,32,127]{3,2,1,0:T(8,128)}) fusion(f32[12,3,32,128]{3,2,1,0:T(8,128)S(1)} %multiply_add_fusion), kind=kLoop, calls=%fused_computation.146 | loop fusion | bytes 2340864 | tf_op jit(solution)/shard_map/slice | solution.py:568
  106.6 0.8 fusion.46
  107.4 2.7 %fusion.13 = f32[12,3,32,128]{3,2,1,0:T(8,128)} fusion(f32[12,3,32,1]{3,2,1,0:T(8,128)S(1)} %reshape_squeeze.54, f32[12,3,32,127]{3,2,1,0:T(8,128)} %get-tuple-element.38, f32[12,3,32,127]{3,2,1,0:T(8,128)} %get-tuple-element.37, f32[12,3,32,1]{3,2,1,0:T(8,128)S(1)} %reshape_squeeze.55, f32[12,3,1,128]{3,2,1,0:T(1,128)S(1)} %reshape_squeeze.50, ...), kind=kLoop, calls=%fused_computation.25 | loop fusion | flops 2801664 | bytes 4030464 | tf_op jit(solution)/shard_map/add | solution.py:577
  (164 shorter events, 7.9 us)
Async XLA Ops:
  1.8 2.4 %copy-start.20 = (s32[2,256]{1,0:T(2,128)S(1)}, s32[2,256]{1,0:T(2,128)}, u32[]{:S(2)}) copy-start(s32[2,256]{1,0:T(2,128)} %param.17) | copy-start | bytes 6148
  3.6 1.8 %copy-start = (f32[12,3,32,128]{3,2,1,0:T(8,128)S(1)}, f32[12,3,32,128]{3,2,1,0:T(8,128)}, u32[]{:S(2)}) copy-start(f32[12,3,32,128]{3,2,1,0:T(8,128)} %param.10) | copy-start | bytes 1769476
  3.6 1.8 %copy-start.4 = (f32[3,32,128]{2,1,0:T(8,128)S(1)}, f32[3,32,128]{2,1,0:T(8,128)}, u32[]{:S(2)}) copy-start(f32[3,32,128]{2,1,0:T(8,128)} %param.15) | copy-start | bytes 147460
  46.5 1.0 copy-start.15
  47.5 0.8 copy-start.5
  47.5 1.0 copy-start.16
  47.5 1.0 copy-start.19
  48.1 0.8 copy-start.2
  48.3 1.7 %copy-start.3 = (f32[13,32,128]{2,1,0:T(8,128)S(1)}, f32[13,32,128]{2,1,0:T(8,128)}, u32[]{:S(2)}) copy-start(f32[13,32,128]{2,1,0:T(8,128)} %get-tuple-element.12) | copy-start | bytes 638980
  51.3 0.8 copy-start.6
  72.2 1.1 %copy-start.17 = (f32[4,39,128]{2,1,0:T(8,128)S(1)}, f32[4,39,128]{2,1,0:T(8,128)}, u32[]{:S(2)}) copy-start(f32[4,39,128]{2,1,0:T(8,128)} %get-tuple-element.14) | copy-start | bytes 239620
  76.7 2.2 %copy-start.8 = (f32[3,32,128]{2,1,0:T(8,128)}, f32[3,32,128]{2,1,0:T(8,128)S(1)}, u32[]{:S(2)}) copy-start(f32[3,32,128]{2,1,0:T(8,128)S(1)} %select_add_fusion) | copy-start | bytes 147460
  76.7 2.2 %copy-start.10 = (f32[3,32,128]{2,1,0:T(8,128)}, f32[3,32,128]{2,1,0:T(8,128)S(1)}, u32[]{:S(2)}) copy-start(f32[3,32,128]{2,1,0:T(8,128)S(1)} %broadcast_maximum_fusion) | copy-start | bytes 147460
  78.9 1.2 %copy-start.1 = (f32[12,32,128]{2,1,0:T(8,128)}, f32[12,32,128]{2,1,0:T(8,128)S(1)}, u32[]{:S(2)}) copy-start(f32[12,32,128]{2,1,0:T(8,128)S(1)} %get-tuple-element.33.p_ref) | copy-start | bytes 589828
  79.4 0.9 copy-start.13
  79.4 0.9 copy-start.14
  104.1 1.2 %copy-start.18 = (f32[4,36,128]{2,1,0:T(8,128)S(1)}, f32[4,36,128]{2,1,0:T(8,128)}, u32[]{:S(2)}) copy-start(f32[4,36,128]{2,1,0:T(8,128)} %get-tuple-element.16) | copy-start | bytes 221188
  105.3 2.1 %copy-start.7 = (f32[3,32,128]{2,1,0:T(8,128)S(1)}, f32[3,32,128]{2,1,0:T(8,128)}, u32[]{:S(2)}) copy-start(f32[3,32,128]{2,1,0:T(8,128)} %fusion.32) | copy-start | bytes 147460
  105.3 2.1 %copy-start.9 = (f32[3,32,128]{2,1,0:T(8,128)S(1)}, f32[3,32,128]{2,1,0:T(8,128)}, u32[]{:S(2)}) copy-start(f32[3,32,128]{2,1,0:T(8,128)} %copy-done.8) | copy-start | bytes 147460
  105.3 2.1 %copy-start.11 = (f32[3,32,128]{2,1,0:T(8,128)S(1)}, f32[3,32,128]{2,1,0:T(8,128)}, u32[]{:S(2)}) copy-start(f32[3,32,128]{2,1,0:T(8,128)} %copy-done.10) | copy-start | bytes 147460
  105.3 2.1 %copy-start.12 = (f32[3,32,128]{2,1,0:T(8,128)S(1)}, f32[3,32,128]{2,1,0:T(8,128)}, u32[]{:S(2)}) copy-start(f32[3,32,128]{2,1,0:T(8,128)} %fusion.30) | copy-start | bytes 147460

commit v13 on v10

--- a/solution.py
+++ b/solution.py
@@ -293,10 +293,11 @@
     return east, west, up, down, 1 - top, 1 - inner
 
 
-def mix_halo_body(lev_n, lon_n, lat_n, p_ref, pe_ref, ae_ref, me_ref, te_ref, cs_out, halo_out,
+def mix_halo_body(lev_n, lon_n, lat_n, p_ref, st_ref, cs_out, halo_out,
                   pieces, reduced, sends, recvs, gsends, grecvs,
                   pe_slots, pe_send, pe_recv, mixed, got, h_send, h_recv):
     lev = lax.axis_index("lev")
+    pe_ref = st_ref.at[0]
     east, west, up, down, up_slot, down_slot = halo_places(lon_n, lat_n)
     barrier = pltpu.get_barrier_semaphore()
     for d in range(1, lev_n):
@@ -318,8 +319,8 @@
     pe_sum = pe_slots[0]
     for s in range(1, lev_n):
         pe_sum = pe_sum + pe_slots[s]
-    share = me_ref[...]
-    mixed[...] = (1.0 - share) * ae_ref[...] + share * (pe_sum / te_ref[...])
+    share = st_ref[2]
+    mixed[...] = (1.0 - share) * st_ref[1] + share * (pe_sum / st_ref[3])
     plan = (
         (mixed.at[0], got.at[0], h_recv.at[0], east),
         (mixed.at[1], got.at[1], h_recv.at[1], west),
@@ -345,30 +346,30 @@
     halo_out[...] = got[...]
 
 
-def mix_halo(p, pe, ae, me, te, collective_id):
+def mix_halo(p, st, collective_id):
     lev_n, lon_n, lat_n = lax.axis_size("lev"), lax.axis_size("lon"), lax.axis_size("lat")
     vmem = pl.BlockSpec(memory_space=pltpu.VMEM)
     return pl.pallas_call(
         functools.partial(mix_halo_body, lev_n, lon_n, lat_n),
         out_shape=(
             jax.ShapeDtypeStruct(p.shape, p.dtype),
-            jax.ShapeDtypeStruct(pe.shape, p.dtype),
-        ),
-        in_specs=[vmem] * 5,
+            jax.ShapeDtypeStruct(st.shape[1:], p.dtype),
+        ),
+        in_specs=[vmem] * 2,
         out_specs=(vmem, vmem),
         scratch_shapes=lev_scratch(lev_n, p.shape, p.dtype) + [
-            pltpu.VMEM((lev_n,) + pe.shape, p.dtype),
+            pltpu.VMEM((lev_n,) + st.shape[1:], p.dtype),
             pltpu.SemaphoreType.DMA((lev_n - 1,)),
             pltpu.SemaphoreType.DMA((lev_n,)),
-            pltpu.VMEM(pe.shape, p.dtype),
-            pltpu.VMEM(pe.shape, p.dtype),
+            pltpu.VMEM(st.shape[1:], p.dtype),
+            pltpu.VMEM(st.shape[1:], p.dtype),
             pltpu.SemaphoreType.DMA((4,)),
             pltpu.SemaphoreType.DMA((4,)),
         ],
         compiler_params=pltpu.CompilerParams(
             collective_id=collective_id, has_side_effects=True
         ),
-    )(p, pe, ae, me, te)
+    )(p, st)
 
 
 def lev_sum(x, collective_id):
@@ -505,10 +506,12 @@
 
             column_sum, halos = mix_halo(
                 partial_sum,
-                edges(partial_sum[:, None]),
-                edges(adjoint),
-                edges(mix_fraction[None]),
-                edges(total_detrain[None, None], 1.0),
+                jnp.stack([
+                    edges(partial_sum[:, None]),
+                    edges(adjoint),
+                    edges(mix_fraction[None]),
+                    edges(total_detrain[None, None], 1.0),
+                ]),
                 5,
             )
         adjoint = (1.0 - mix_fraction)[None] * adjoint + mix_fraction[None] * (

time: 105 us -> 103 us (0.981)
  other arithmetic: 13.9 us -> 12.1 us
    another operation x4 -> x5, other arithmetic: 2.58 us -> 0.79 us  [on_device(): jnp.stack([edges(partial_sum[:, None]), edges(adjoint), edges(mix_fractio...]
where the time goes in v13:
time: 103 us; the launch traced here: 101 us
  Pallas kernels  75.9 us (74%)
  other arithmetic  12.1 us (12%)
  local copies, waits for them, and re-layouts  12 us (12%)
    pallas_call x1, Pallas kernels, exchange(): pl.pallas_call(functools.partial(exchange_body, lev_n, owners, lat_n), ou...  38.2 us
    pallas_call x1, Pallas kernels, mix_halo(): pl.pallas_call(functools.partial(mix_halo_body, lev_n, lon_n, lat_n), out...  20.6 us
    pallas_call x1, Pallas kernels, lev_direct(): pl.pallas_call(functools.partial(lev_direct_body, n), out_shape=jax.Shape...  8.92 us
    pallas_call x1, Pallas kernels, halo_swap(): pl.pallas_call(functools.partial(halo_body, lon_n, lat_n), out_shape=(jax...  8.14 us
    add x1, other arithmetic, on_device(): adjoint + upwind_east * (east_side - adjoint)  2.66 us

profile of v13, /device:TPU:1, one launch (start us, length us, event | category | flops | bytes accessed | tf_op | source)
XLA Modules:
  0.0 101.3 jit_solution(12334608052607100812)
XLA Ops:
  0.0 0.7 copy.112
  0.9 0.7 fusion.28
  1.8 0.7 iota_compare_fusion.4
  2.5 0.7 broadcast_select_fusion
  3.2 0.4 select_reduce_fusion
  3.6 0.4 reshape.230
  4.8 0.6 pad.29.rows_ref
  5.5 0.7 pad_maximum_fusion.1.part_ref
  6.2 38.2 %shard_map.100 = (f32[128,128]{1,0:T(8,128)}, f32[13,32,128]{2,1,0:T(8,128)}) custom-call(f32[128,128]{1,0:T(8,128)} %pad.29.rows_ref, f32[13,32,128]{2,1,0:T(8,128)} %pad_maximum_fusion.1.part_ref), custom_call_target="tpu_custom_call" | custom-call | tf_op jit(solution)/shard_map/pallas_call | solution.py:225
  44.5 0.9 copy.62
  45.6 0.3 reshape.220
  46.0 0.5 fusion.18
  46.5 0.6 multiply_reduce_fusion.2
  47.1 8.9 %shard_map.101 = f32[1,32,128]{2,1,0:T(8,128)} custom-call(f32[1,32,128]{2,1,0:T(8,128)} %bitcast.118), custom_call_target="tpu_custom_call" | custom-call | tf_op jit(solution)/shard_map/pallas_call | solution.py:267
  56.0 0.7 add_divide_fusion
  57.0 0.6 slice_reduce_fusion.2
  57.9 0.6 pad_maximum_fusion.2
  58.7 0.6 pad_maximum_fusion.4
  59.3 8.1 %shard_map.102 = (f32[39,32]{1,0:T(8,128)}, f32[39,32]{1,0:T(8,128)}, f32[39,128]{1,0:T(8,128)}, f32[39,128]{1,0:T(8,128)}) custom-call(f32[39,32]{1,0:T(8,128)} %get-tuple-element.65.col_last, f32[39,32]{1,0:T(8,128)} %get-tuple-element.66.col_first, f32[39,128]{1,0:T(8,128)} %get-tuple-element.67.row_last, f32[39,128]{1,0:T(8,128)} %get-tuple-element.68.row_first), custom_call_target="tpu_custom_call" | custom-call | tf_op jit(solution)/shard_map/pallas_call | solution.py:79
  67.5 1.3 %reshape.231 = f32[12,3,32,1]{3,2,1,0:T(8,128)S(1)} reshape(f32[36,32]{1,0:T(8,128)} %bitcast.127) | data formatting | bytes 9216 | tf_op jit(solution)/shard_map/reshape | solution.py:560
  68.9 0.6 reshape.232
  70.3 0.7 multiply_reduce_fusion
  71.0 0.3 slice_reduce_fusion.5
  71.5 0.6 slice_reduce_fusion.1
  72.9 0.7 pad_maximum_fusion.st_ref
  73.7 20.6 %shard_map.103 = (f32[12,32,128]{2,1,0:T(8,128)}, f32[4,36,128]{2,1,0:T(8,128)}) custom-call(f32[12,32,128]{2,1,0:T(8,128)} %copy-done.1, f32[4,4,36,128]{3,2,1,0:T(8,128)} %pad_maximum_fusion.st_ref), custom_call_target="tpu_custom_call" | custom-call | tf_op jit(solution)/shard_map/pallas_call | solution.py:352
  94.3 0.9 broadcast_divide_fusion
  95.4 1.2 %fusion.32 = (f32[12,3,32,127]{3,2,1,0:T(8,128)}, f32[12,3,32,127]{3,2,1,0:T(8,128)}) fusion(f32[12,3,32,128]{3,2,1,0:T(8,128)S(1)} %multiply_add_fusion), kind=kLoop, calls=%fused_computation.120 | loop fusion | bytes 2340864 | tf_op jit(solution)/shard_map/slice | solution.py:563
  96.6 0.6 reshape_squeeze.42
  97.2 0.6 reshape_squeeze.43
  97.8 0.8 fusion.37
  98.6 2.7 %fusion.13 = f32[12,3,32,128]{3,2,1,0:T(8,128)} fusion(f32[12,3,32,1]{3,2,1,0:T(8,128)S(1)} %reshape_squeeze.42, f32[12,3,32,127]{3,2,1,0:T(8,128)} %get-tuple-element.40, f32[12,3,32,127]{3,2,1,0:T(8,128)} %get-tuple-element.39, f32[12,3,32,1]{3,2,1,0:T(8,128)S(1)} %reshape_squeeze.43, f32[12,3,1,128]{3,2,1,0:T(1,128)S(1)} %reshape_squeeze.40, ...), kind=kLoop, calls=%fused_computation.25 | loop fusion | flops 2801664 | bytes 4030464 | tf_op jit(solution)/shard_map/add | solution.py:572
  (120 shorter events, 3.8 us)
Async XLA Ops:
  1.8 2.4 %copy-start.12 = (s32[2,256]{1,0:T(2,128)S(1)}, s32[2,256]{1,0:T(2,128)}, u32[]{:S(2)}) copy-start(s32[2,256]{1,0:T(2,128)} %param.17) | copy-start | bytes 6148
  3.6 1.8 %copy-start = (f32[12,3,32,128]{3,2,1,0:T(8,128)S(1)}, f32[12,3,32,128]{3,2,1,0:T(8,128)}, u32[]{:S(2)}) copy-start(f32[12,3,32,128]{3,2,1,0:T(8,128)} %param.10) | copy-start | bytes 1769476
  3.6 1.8 %copy-start.3 = (f32[3,32,128]{2,1,0:T(8,128)S(1)}, f32[3,32,128]{2,1,0:T(8,128)}, u32[]{:S(2)}) copy-start(f32[3,32,128]{2,1,0:T(8,128)} %param.15) | copy-start | bytes 147460
  45.6 10.4 %copy-start.5 = (f32[13,32,128]{2,1,0:T(8,128)S(1)}, f32[13,32,128]{2,1,0:T(8,128)}, u32[]{:S(2)}) copy-start(f32[13,32,128]{2,1,0:T(8,128)} %get-tuple-element.14) | copy-start | bytes 638980
  46.0 10.8 %copy-start.2 = (f32[3,32,128]{2,1,0:T(8,128)S(1)}, f32[3,32,128]{2,1,0:T(8,128)}, u32[]{:S(2)}) copy-start(f32[3,32,128]{2,1,0:T(8,128)} %param.14) | copy-start | bytes 147460
  56.9 0.8 copy-start.4
  56.9 1.7 %copy-start.6 = (f32[3,32,128]{2,1,0:T(8,128)S(1)}, f32[3,32,128]{2,1,0:T(8,128)}, u32[]{:S(2)}) copy-start(f32[3,32,128]{2,1,0:T(8,128)} %param.12) | copy-start | bytes 147460
  57.0 1.7 %copy-start.11 = (f32[3,128]{1,0:T(4,128)S(1)}, f32[3,128]{1,0:T(4,128)}, u32[]{:S(2)}) copy-start(f32[3,128]{1,0:T(4,128)} %param.13) | copy-start | bytes 4612
  67.5 1.4 %copy-start.8 = (f32[39,32]{1,0:T(8,128)S(1)}, f32[39,32]{1,0:T(8,128)}, u32[]{:S(2)}) copy-start(f32[39,32]{1,0:T(8,128)} %get-tuple-element.16) | copy-start | bytes 14980
  67.5 2.2 %copy-start.9 = (f32[39,128]{1,0:T(8,128)S(1)}, f32[39,128]{1,0:T(8,128)}, u32[]{:S(2)}) copy-start(f32[39,128]{1,0:T(8,128)} %get-tuple-element.18) | copy-start | bytes 59908
  68.8 1.0 copy-start.10
  71.0 1.1 %copy-start.1 = (f32[12,32,128]{2,1,0:T(8,128)}, f32[12,32,128]{2,1,0:T(8,128)S(1)}, u32[]{:S(2)}) copy-start(f32[12,32,128]{2,1,0:T(8,128)S(1)} %get-tuple-element.35.p_ref) | copy-start | bytes 589828
  95.4 1.2 %copy-start.7 = (f32[4,36,128]{2,1,0:T(8,128)S(1)}, f32[4,36,128]{2,1,0:T(8,128)}, u32[]{:S(2)}) copy-start(f32[4,36,128]{2,1,0:T(8,128)} %get-tuple-element.20) | copy-start | bytes 221188

commit v14 on v13

--- a/solution.py
+++ b/solution.py
@@ -370,6 +370,55 @@
             collective_id=collective_id, has_side_effects=True
         ),
     )(p, st)
+
+
+def halo_pack_body(lon_n, lat_n, st_ref, out_ref, got, h_send, h_recv):
+    east, west, up, down, up_slot, down_slot = halo_places(lon_n, lat_n)
+    barrier = pltpu.get_barrier_semaphore()
+    for peer in (east, west, up, down):
+        pl.semaphore_signal(barrier, inc=1, device_id=peer, device_id_type=MESH)
+    pl.semaphore_wait(barrier, 4)
+    plan = (
+        (st_ref.at[0], got.at[0], h_recv.at[0], east),
+        (st_ref.at[1], got.at[1], h_recv.at[1], west),
+        (st_ref.at[2], got.at[2 + up_slot], h_recv.at[2 + up_slot], up),
+        (st_ref.at[3], got.at[2 + down_slot], h_recv.at[2 + down_slot], down),
+    )
+    copies = []
+    for i, (src, dst, sem, peer) in enumerate(plan):
+        copy = pltpu.make_async_remote_copy(
+            src_ref=src, dst_ref=dst, send_sem=h_send.at[i], recv_sem=sem,
+            device_id=peer, device_id_type=MESH,
+        )
+        copy.start()
+        copies.append(copy)
+    for i in range(4):
+        pltpu.make_async_remote_copy(
+            src_ref=st_ref.at[i], dst_ref=got.at[i], send_sem=h_send.at[i], recv_sem=h_recv.at[i],
+            device_id=east, device_id_type=MESH,
+        ).wait_recv()
+    for copy in copies:
+        copy.wait_send()
+    out_ref[...] = got[...]
+
+
+def halo_pack(st, collective_id):
+    lon_n, lat_n = lax.axis_size("lon"), lax.axis_size("lat")
+    vmem = pl.BlockSpec(memory_space=pltpu.VMEM)
+    return pl.pallas_call(
+        functools.partial(halo_pack_body, lon_n, lat_n),
+        out_shape=jax.ShapeDtypeStruct(st.shape, st.dtype),
+        in_specs=[vmem],
+        out_specs=vmem,
+        scratch_shapes=[
+            pltpu.VMEM(st.shape, st.dtype),
+            pltpu.SemaphoreType.DMA((4,)),
+            pltpu.SemaphoreType.DMA((4,)),
+        ],
+        compiler_params=pltpu.CompilerParams(
+            collective_id=collective_id, has_side_effects=True
+        ),
+    )(st)
 
 
 def lev_sum(x, collective_id):
@@ -533,9 +582,16 @@
                 col_first = jnp.concatenate([col_first, east_courant[:, :, 0]], axis=0)
                 row_last = jnp.concatenate([row_last, north_courant[:, -1, :]], axis=0)
                 row_first = jnp.concatenate([row_first, pole_courant], axis=0)
-            west_halo, east_halo, north_halo, south_halo = halo_swap(
-                col_last, col_first, row_last, row_first, 2 + position
+            pad_lanes = ((0, 0), (0, lon_cols - lat_rows))
+            got = halo_pack(
+                jnp.stack([
+                    jnp.pad(col_last, pad_lanes), jnp.pad(col_first, pad_lanes),
+                    row_last, row_first,
+                ]),
+                2,
             )
+            west_halo, east_halo = got[0, :, :lat_rows], got[1, :, :lat_rows]
+            north_halo, south_halo = got[2], got[3]
             if position == 0:
                 west_wind = jnp.concatenate(
                     [west_halo[planes:, :, None], east_courant[:, :, :-1]], axis=2

time: 103 us -> 102 us (level)
    concatenate x2 -> x0, other arithmetic: 1.24 us -> none  [the longest x1 0.63 us: on_device(): col_last = jnp.concatenate([col_last, east_courant[:, :, -1]], axis=0)]
where the time goes in v14:
time: 102 us; the launch traced here: 101 us
  Pallas kernels  76 us (75%)
  local copies, waits for them, and re-layouts  12 us (12%)
  other arithmetic  11.6 us (11%)
    pallas_call x1, Pallas kernels, exchange(): pl.pallas_call(functools.partial(exchange_body, lev_n, owners, lat_n), ou...  38.2 us
    pallas_call x1, Pallas kernels, mix_halo(): pl.pallas_call(functools.partial(mix_halo_body, lev_n, lon_n, lat_n), out...  20.6 us
    pallas_call x1, Pallas kernels, lev_direct(): pl.pallas_call(functools.partial(lev_direct_body, n), out_shape=jax.Shape...  8.92 us
    pallas_call x1, Pallas kernels, halo_pack(): pl.pallas_call(functools.partial(halo_pack_body, lon_n, lat_n), out_shape...  8.23 us
    add x1, other arithmetic, on_device(): adjoint + upwind_east * (east_side - adjoint)  2.66 us

profile of v14, /device:TPU:1, one launch (start us, length us, event | category | flops | bytes accessed | tf_op | source)
XLA Modules:
  0.0 100.8 jit_solution(6035870012911833241)
XLA Ops:
  0.0 0.7 copy.106
  0.9 0.7 fusion.30
  1.8 0.7 iota_compare_fusion.5
  2.5 0.7 broadcast_select_fusion
  3.2 0.4 select_reduce_fusion
  3.6 0.4 reshape.253
  4.8 0.6 pad.36.rows_ref
  5.5 0.7 pad_maximum_fusion.1.part_ref
  6.2 38.2 %shard_map.100 = (f32[128,128]{1,0:T(8,128)}, f32[13,32,128]{2,1,0:T(8,128)}) custom-call(f32[128,128]{1,0:T(8,128)} %pad.36.rows_ref, f32[13,32,128]{2,1,0:T(8,128)} %pad_maximum_fusion.1.part_ref), custom_call_target="tpu_custom_call" | custom-call | tf_op jit(solution)/shard_map/pallas_call | solution.py:225
  44.5 0.9 copy.58
  45.6 0.3 reshape.243
  46.0 0.5 fusion.18
  46.5 0.6 multiply_reduce_fusion.2
  47.1 8.9 %shard_map.101 = f32[1,32,128]{2,1,0:T(8,128)} custom-call(f32[1,32,128]{2,1,0:T(8,128)} %bitcast.124), custom_call_target="tpu_custom_call" | custom-call | tf_op jit(solution)/shard_map/pallas_call | solution.py:267
  56.0 0.7 add_divide_fusion
  57.0 0.6 slice_reduce_fusion.3
  58.1 0.6 pad_maximum_fusion.2.st_ref
  58.8 8.2 %shard_map.102 = f32[4,39,128]{2,1,0:T(8,128)} custom-call(f32[4,39,128]{2,1,0:T(8,128)} %pad_maximum_fusion.2.st_ref), custom_call_target="tpu_custom_call" | custom-call | tf_op jit(solution)/shard_map/pallas_call | solution.py:408
  67.0 0.8 fusion.41
  67.8 0.6 reshape.254
  68.4 0.6 reshape.255
  69.8 0.7 multiply_reduce_fusion
  70.5 0.3 slice_reduce_fusion.5
  71.0 0.6 slice_reduce_fusion.1
  72.4 0.7 pad_maximum_fusion.st_ref
  73.2 20.6 %shard_map.103 = (f32[12,32,128]{2,1,0:T(8,128)}, f32[4,36,128]{2,1,0:T(8,128)}) custom-call(f32[12,32,128]{2,1,0:T(8,128)} %copy-done.1, f32[4,4,36,128]{3,2,1,0:T(8,128)} %pad_maximum_fusion.st_ref), custom_call_target="tpu_custom_call" | custom-call | tf_op jit(solution)/shard_map/pallas_call | solution.py:352
  93.8 0.9 broadcast_divide_fusion
  94.9 1.2 %fusion.34 = (f32[12,3,32,127]{3,2,1,0:T(8,128)}, f32[12,3,32,127]{3,2,1,0:T(8,128)}) fusion(f32[12,3,32,128]{3,2,1,0:T(8,128)S(1)} %multiply_add_fusion), kind=kLoop, calls=%fused_computation.123 | loop fusion | bytes 2340864 | tf_op jit(solution)/shard_map/slice | solution.py:619
  96.1 0.6 reshape_squeeze.42
  96.7 0.6 reshape_squeeze.43
  97.3 0.8 fusion.39
  98.2 2.7 %fusion.13 = f32[12,3,32,128]{3,2,1,0:T(8,128)} fusion(f32[12,3,32,1]{3,2,1,0:T(8,128)S(1)} %reshape_squeeze.42, f32[12,3,32,127]{3,2,1,0:T(8,128)} %get-tuple-element.32, f32[12,3,32,127]{3,2,1,0:T(8,128)} %get-tuple-element.31, f32[12,3,32,1]{3,2,1,0:T(8,128)S(1)} %reshape_squeeze.43, f32[12,3,1,128]{3,2,1,0:T(1,128)S(1)} %reshape_squeeze.40, ...), kind=kLoop, calls=%fused_computation.25 | loop fusion | flops 2801664 | bytes 4030464 | tf_op jit(solution)/shard_map/add | solution.py:628
  (119 shorter events, 3.8 us)
Async XLA Ops:
  1.8 2.4 %copy-start.10 = (s32[2,256]{1,0:T(2,128)S(1)}, s32[2,256]{1,0:T(2,128)}, u32[]{:S(2)}) copy-start(s32[2,256]{1,0:T(2,128)} %param.17) | copy-start | bytes 6148
  3.6 1.8 %copy-start = (f32[12,3,32,128]{3,2,1,0:T(8,128)S(1)}, f32[12,3,32,128]{3,2,1,0:T(8,128)}, u32[]{:S(2)}) copy-start(f32[12,3,32,128]{3,2,1,0:T(8,128)} %param.10) | copy-start | bytes 1769476
  3.6 1.8 %copy-start.3 = (f32[3,32,128]{2,1,0:T(8,128)S(1)}, f32[3,32,128]{2,1,0:T(8,128)}, u32[]{:S(2)}) copy-start(f32[3,32,128]{2,1,0:T(8,128)} %param.15) | copy-start | bytes 147460
  45.6 10.4 %copy-start.6 = (f32[13,32,128]{2,1,0:T(8,128)S(1)}, f32[13,32,128]{2,1,0:T(8,128)}, u32[]{:S(2)}) copy-start(f32[13,32,128]{2,1,0:T(8,128)} %get-tuple-element.10) | copy-start | bytes 638980
  46.0 10.8 %copy-start.2 = (f32[3,32,128]{2,1,0:T(8,128)S(1)}, f32[3,32,128]{2,1,0:T(8,128)}, u32[]{:S(2)}) copy-start(f32[3,32,128]{2,1,0:T(8,128)} %param.14) | copy-start | bytes 147460
  56.9 0.8 copy-start.4
  56.9 1.1 %copy-start.7 = (f32[3,32,128]{2,1,0:T(8,128)S(1)}, f32[3,32,128]{2,1,0:T(8,128)}, u32[]{:S(2)}) copy-start(f32[3,32,128]{2,1,0:T(8,128)} %param.12) | copy-start | bytes 147460
  57.0 1.1 %copy-start.9 = (f32[3,128]{1,0:T(4,128)S(1)}, f32[3,128]{1,0:T(4,128)}, u32[]{:S(2)}) copy-start(f32[3,128]{1,0:T(4,128)} %param.13) | copy-start | bytes 4612
  67.8 1.2 %copy-start.5 = (f32[4,39,128]{2,1,0:T(8,128)S(1)}, f32[4,39,128]{2,1,0:T(8,128)}, u32[]{:S(2)}) copy-start(f32[4,39,128]{2,1,0:T(8,128)} %shard_map.102) | copy-start | bytes 239620
  70.5 1.1 %copy-start.1 = (f32[12,32,128]{2,1,0:T(8,128)}, f32[12,32,128]{2,1,0:T(8,128)S(1)}, u32[]{:S(2)}) copy-start(f32[12,32,128]{2,1,0:T(8,128)S(1)} %get-tuple-element.27.p_ref) | copy-start | bytes 589828
  94.9 1.2 %copy-start.8 = (f32[4,36,128]{2,1,0:T(8,128)S(1)}, f32[4,36,128]{2,1,0:T(8,128)}, u32[]{:S(2)}) copy-start(f32[4,36,128]{2,1,0:T(8,128)} %get-tuple-element.12) | copy-start | bytes 221188

commit v15 on v10

--- a/solution.py
+++ b/solution.py
@@ -293,9 +293,9 @@
     return east, west, up, down, 1 - top, 1 - inner
 
 
-def mix_halo_body(lev_n, lon_n, lat_n, p_ref, pe_ref, ae_ref, me_ref, te_ref, cs_out, halo_out,
+def mix_halo_body(lev_n, lon_n, lat_n, p_ref, pe_ref, st_ref, cs_out, halo_out,
                   pieces, reduced, sends, recvs, gsends, grecvs,
-                  pe_slots, pe_send, pe_recv, mixed, got, h_send, h_recv):
+                  pe_slots, pe_send, pe_recv, spread, mixed, got, h_send, h_recv):
     lev = lax.axis_index("lev")
     east, west, up, down, up_slot, down_slot = halo_places(lon_n, lat_n)
     barrier = pltpu.get_barrier_semaphore()
@@ -318,13 +318,17 @@
     pe_sum = pe_slots[0]
     for s in range(1, lev_n):
         pe_sum = pe_sum + pe_slots[s]
-    share = me_ref[...]
-    mixed[...] = (1.0 - share) * ae_ref[...] + share * (pe_sum / te_ref[...])
+    tracers = pe_ref.shape[1]
+    copies_k = spread.shape[1] // tracers
+    for k in range(copies_k):
+        spread[:, pl.ds(k, tracers, stride=copies_k), :] = pe_sum
+    share = st_ref[1]
+    mixed[...] = (1.0 - share) * st_ref[0] + share * (spread[...] / st_ref[2])
     plan = (
         (mixed.at[0], got.at[0], h_recv.at[0], east),
-        (mixed.at[1], got.at[1], h_recv.at[1], west),
-        (mixed.at[2], got.at[2 + up_slot], h_recv.at[2 + up_slot], up),
-        (mixed.at[3], got.at[2 + down_slot], h_recv.at[2 + down_slot], down),
+        (mixed.at[0], got.at[1], h_recv.at[1], west),
+        (mixed.at[1], got.at[2 + up_slot], h_recv.at[2 + up_slot], up),
+        (mixed.at[2], got.at[2 + down_slot], h_recv.at[2 + down_slot], down),
     )
     copies = []
     for i, (src, dst, sem, peer) in enumerate(plan):
@@ -337,7 +341,7 @@
     gather_finish(lev_n, cs_out, reduced, gsends, grecvs)
     for i in range(4):
         pltpu.make_async_remote_copy(
-            src_ref=mixed.at[i], dst_ref=got.at[i], send_sem=h_send.at[i], recv_sem=h_recv.at[i],
+            src_ref=mixed.at[0], dst_ref=got.at[i], send_sem=h_send.at[i], recv_sem=h_recv.at[i],
             device_id=east, device_id_type=MESH,
         ).wait_recv()
     for copy in copies:
@@ -345,30 +349,33 @@
     halo_out[...] = got[...]
 
 
-def mix_halo(p, pe, ae, me, te, collective_id):
+def mix_halo(p, pe, st, collective_id):
     lev_n, lon_n, lat_n = lax.axis_size("lev"), lax.axis_size("lon"), lax.axis_size("lat")
     vmem = pl.BlockSpec(memory_space=pltpu.VMEM)
+    edge_shape = st.shape[1:]
+    halo_shape = (4,) + edge_shape[1:]
     return pl.pallas_call(
         functools.partial(mix_halo_body, lev_n, lon_n, lat_n),
         out_shape=(
             jax.ShapeDtypeStruct(p.shape, p.dtype),
-            jax.ShapeDtypeStruct(pe.shape, p.dtype),
-        ),
-        in_specs=[vmem] * 5,
+            jax.ShapeDtypeStruct(halo_shape, p.dtype),
+        ),
+        in_specs=[vmem] * 3,
         out_specs=(vmem, vmem),
         scratch_shapes=lev_scratch(lev_n, p.shape, p.dtype) + [
             pltpu.VMEM((lev_n,) + pe.shape, p.dtype),
             pltpu.SemaphoreType.DMA((lev_n - 1,)),
             pltpu.SemaphoreType.DMA((lev_n,)),
-            pltpu.VMEM(pe.shape, p.dtype),
-            pltpu.VMEM(pe.shape, p.dtype),
+            pltpu.VMEM(edge_shape, p.dtype),
+            pltpu.VMEM(edge_shape, p.dtype),
+            pltpu.VMEM(halo_shape, p.dtype),
             pltpu.SemaphoreType.DMA((4,)),
             pltpu.SemaphoreType.DMA((4,)),
         ],
         compiler_params=pltpu.CompilerParams(
             collective_id=collective_id, has_side_effects=True
         ),
-    )(p, pe, ae, me, te)
+    )(p, pe, st)
 
 
 def lev_sum(x, collective_id):
@@ -493,22 +500,33 @@
             partial_sum = jnp.sum(detrain_share[None] * adjoint, axis=1)
             planes = tracers * lev_dev
 
-            def spread(x, width, fill=0.0):
-                x = jnp.broadcast_to(x, (tracers, lev_dev, width)).reshape(planes, width)
-                return jnp.pad(x, ((0, 0), (0, lon_cols - width)), constant_values=fill)
-
-            def edges(x, fill=0.0):
-                return jnp.stack([
-                    spread(x[..., :, -1], lat_rows, fill), spread(x[..., :, 0], lat_rows, fill),
-                    spread(x[..., -1, :], lon_cols), spread(x[..., 0, :], lon_cols),
-                ])
-
+            def packed(x, fill=0.0):
+                x = jnp.broadcast_to(x, (tracers, lev_dev) + x.shape[2:]).reshape(
+                    (planes,) + x.shape[2:]
+                )
+                return x
+
+            def edge_set(x, fill=0.0):
+                rest = jnp.full((planes, lon_cols - 2 * lat_rows), fill, jnp.float32)
+                cols = jnp.concatenate(
+                    [packed(x[..., :, -1]), packed(x[..., :, 0]), rest], axis=1
+                )
+                return jnp.stack([cols, packed(x[..., -1, :]), packed(x[..., 0, :])])
+
+            part_rest = jnp.zeros((tracers, lon_cols - 2 * lat_rows), jnp.float32)
+            part_edges = jnp.stack([
+                jnp.concatenate([partial_sum[:, :, -1], partial_sum[:, :, 0], part_rest], axis=1),
+                partial_sum[:, -1, :],
+                partial_sum[:, 0, :],
+            ])
             column_sum, halos = mix_halo(
                 partial_sum,
-                edges(partial_sum[:, None]),
-                edges(adjoint),
-                edges(mix_fraction[None]),
-                edges(total_detrain[None, None], 1.0),
+                part_edges,
+                jnp.stack([
+                    edge_set(adjoint),
+                    edge_set(mix_fraction[None]),
+                    edge_set(total_detrain[None, None], 1.0),
+                ]),
                 5,
             )
         adjoint = (1.0 - mix_fraction)[None] * adjoint + mix_fraction[None] * (
@@ -516,7 +534,7 @@
         )[:, None]
         if position == 1:
             west_halo = halos[0, :, :lat_rows]
-            east_halo = halos[1, :, :lat_rows]
+            east_halo = halos[1, :, lat_rows:2 * lat_rows]
             north_halo = halos[2]
             south_halo = halos[3]
         planes = tracers * lev_dev

time: 105 us -> 100 us (0.952); the launches traced: 103 us -> 99.4 us
  Pallas kernels: 75.9 us -> 73.4 us
    pallas_call x1, Pallas kernels: 20.6 us -> 18.1 us  [mix_halo(): pl.pallas_call(functools.partial(mix_halo_body, lev_n, lon_n, lat_n), out...]
    another operation x4 -> x7, other arithmetic: 2.58 us -> 1.48 us  [the longest x4 0.72 us: on_device(): jnp.stack([edge_set(adjoint), edge_set(mix_fraction[None]), edge_set(tota...]
where the time goes in v15:
time: 100 us; the launch traced here: 99.4 us
  Pallas kernels  73.4 us (73%)
  other arithmetic  12.9 us (13%)
  local copies, waits for them, and re-layouts  12 us (12%)
    pallas_call x1, Pallas kernels, exchange(): pl.pallas_call(functools.partial(exchange_body, lev_n, owners, lat_n), ou...  38.2 us
    pallas_call x1, Pallas kernels, mix_halo(): pl.pallas_call(functools.partial(mix_halo_body, lev_n, lon_n, lat_n), out...  18.1 us
    pallas_call x1, Pallas kernels, lev_direct(): pl.pallas_call(functools.partial(lev_direct_body, n), out_shape=jax.Shape...  8.92 us
    pallas_call x1, Pallas kernels, halo_swap(): pl.pallas_call(functools.partial(halo_body, lon_n, lat_n), out_shape=(jax...  8.14 us
    add x1, other arithmetic, on_device(): adjoint + upwind_east * (east_side - adjoint)  2.66 us

profile of v15, /device:TPU:1, one launch (start us, length us, event | category | flops | bytes accessed | tf_op | source)
XLA Modules:
  0.0 99.4 jit_solution(15987382187533405285)
XLA Ops:
  0.0 0.7 copy.122
  0.9 0.7 fusion.28
  1.8 0.7 iota_compare_fusion.4
  2.5 0.7 broadcast_select_fusion
  3.2 0.4 select_reduce_fusion
  3.6 0.4 reshape.212
  4.8 0.6 pad.4.rows_ref
  5.5 0.7 pad_maximum_fusion.part_ref
  6.2 38.2 %shard_map.100 = (f32[128,128]{1,0:T(8,128)}, f32[13,32,128]{2,1,0:T(8,128)}) custom-call(f32[128,128]{1,0:T(8,128)} %pad.4.rows_ref, f32[13,32,128]{2,1,0:T(8,128)} %pad_maximum_fusion.part_ref), custom_call_target="tpu_custom_call" | custom-call | tf_op jit(solution)/shard_map/pallas_call | solution.py:225
  44.5 0.9 copy.70
  45.6 0.3 reshape.202
  46.0 0.5 fusion.18
  46.5 0.6 multiply_reduce_fusion.2
  47.1 8.9 %shard_map.101 = f32[1,32,128]{2,1,0:T(8,128)} custom-call(f32[1,32,128]{2,1,0:T(8,128)} %bitcast.109), custom_call_target="tpu_custom_call" | custom-call | tf_op jit(solution)/shard_map/pallas_call | solution.py:267
  56.0 0.7 add_divide_fusion
  57.0 0.6 slice_reduce_fusion.2
  57.9 0.6 pad_maximum_fusion.3
  58.7 0.6 pad_maximum_fusion.5
  59.3 8.1 %shard_map.102 = (f32[39,32]{1,0:T(8,128)}, f32[39,32]{1,0:T(8,128)}, f32[39,128]{1,0:T(8,128)}, f32[39,128]{1,0:T(8,128)}) custom-call(f32[39,32]{1,0:T(8,128)} %get-tuple-element.67.col_last, f32[39,32]{1,0:T(8,128)} %get-tuple-element.68.col_first, f32[39,128]{1,0:T(8,128)} %get-tuple-element.69.row_last, f32[39,128]{1,0:T(8,128)} %get-tuple-element.70.row_first), custom_call_target="tpu_custom_call" | custom-call | tf_op jit(solution)/shard_map/pallas_call | solution.py:79
  67.5 1.3 %reshape.213 = f32[12,3,32,1]{3,2,1,0:T(8,128)S(1)} reshape(f32[36,32]{1,0:T(8,128)} %bitcast.118) | data formatting | bytes 9216 | tf_op jit(solution)/shard_map/reshape | solution.py:575
  68.9 0.6 reshape.214
  70.3 0.7 multiply_reduce_fusion
  71.0 0.6 slice_reduce_fusion.1
  72.6 0.7 pad_maximum_fusion.1.st_ref
  73.7 0.6 pad_maximum_fusion.2.pe_ref
  74.3 18.1 %shard_map.103 = (f32[12,32,128]{2,1,0:T(8,128)}, f32[4,36,128]{2,1,0:T(8,128)}) custom-call(f32[12,32,128]{2,1,0:T(8,128)} %copy-done.1, f32[3,12,128]{2,1,0:T(8,128)} %pad_maximum_fusion.2.pe_ref, f32[3,3,36,128]{3,2,1,0:T(8,128)} %pad_maximum_fusion.1.st_ref), custom_call_target="tpu_custom_call" | custom-call | tf_op jit(solution)/shard_map/pallas_call | solution.py:357
  92.3 0.9 broadcast_divide_fusion
  93.5 1.2 %fusion.32 = (f32[12,3,32,127]{3,2,1,0:T(8,128)}, f32[12,3,32,127]{3,2,1,0:T(8,128)}) fusion(f32[12,3,32,128]{3,2,1,0:T(8,128)S(1)} %multiply_add_fusion), kind=kLoop, calls=%fused_computation.119 | loop fusion | bytes 2340864 | tf_op jit(solution)/shard_map/slice | solution.py:578
  94.8 0.6 reshape_squeeze.40
  95.4 0.6 reshape_squeeze.41
  96.0 0.8 fusion.37
  96.8 2.7 %fusion.13 = f32[12,3,32,128]{3,2,1,0:T(8,128)} fusion(f32[12,3,32,1]{3,2,1,0:T(8,128)S(1)} %reshape_squeeze.40, f32[12,3,32,127]{3,2,1,0:T(8,128)} %get-tuple-element.40, f32[12,3,32,127]{3,2,1,0:T(8,128)} %get-tuple-element.39, f32[12,3,32,1]{3,2,1,0:T(8,128)S(1)} %reshape_squeeze.41, f32[12,3,1,128]{3,2,1,0:T(1,128)S(1)} %reshape_squeeze.38, ...), kind=kLoop, calls=%fused_computation.25 | loop fusion | flops 2801664 | bytes 4030464 | tf_op jit(solution)/shard_map/add | solution.py:587
  (110 shorter events, 4.3 us)
Async XLA Ops:
  1.8 2.4 %copy-start.12 = (s32[2,256]{1,0:T(2,128)S(1)}, s32[2,256]{1,0:T(2,128)}, u32[]{:S(2)}) copy-start(s32[2,256]{1,0:T(2,128)} %param.17) | copy-start | bytes 6148
  3.6 1.8 %copy-start = (f32[12,3,32,128]{3,2,1,0:T(8,128)S(1)}, f32[12,3,32,128]{3,2,1,0:T(8,128)}, u32[]{:S(2)}) copy-start(f32[12,3,32,128]{3,2,1,0:T(8,128)} %param.10) | copy-start | bytes 1769476
  3.6 1.8 %copy-start.3 = (f32[3,32,128]{2,1,0:T(8,128)S(1)}, f32[3,32,128]{2,1,0:T(8,128)}, u32[]{:S(2)}) copy-start(f32[3,32,128]{2,1,0:T(8,128)} %param.15) | copy-start | bytes 147460
  45.6 10.4 %copy-start.5 = (f32[13,32,128]{2,1,0:T(8,128)S(1)}, f32[13,32,128]{2,1,0:T(8,128)}, u32[]{:S(2)}) copy-start(f32[13,32,128]{2,1,0:T(8,128)} %get-tuple-element.14) | copy-start | bytes 638980
  46.0 10.8 %copy-start.2 = (f32[3,32,128]{2,1,0:T(8,128)S(1)}, f32[3,32,128]{2,1,0:T(8,128)}, u32[]{:S(2)}) copy-start(f32[3,32,128]{2,1,0:T(8,128)} %param.14) | copy-start | bytes 147460
  56.9 0.8 copy-start.4
  56.9 1.7 %copy-start.6 = (f32[3,32,128]{2,1,0:T(8,128)S(1)}, f32[3,32,128]{2,1,0:T(8,128)}, u32[]{:S(2)}) copy-start(f32[3,32,128]{2,1,0:T(8,128)} %param.12) | copy-start | bytes 147460
  57.0 1.7 %copy-start.11 = (f32[3,128]{1,0:T(4,128)S(1)}, f32[3,128]{1,0:T(4,128)}, u32[]{:S(2)}) copy-start(f32[3,128]{1,0:T(4,128)} %param.13) | copy-start | bytes 4612
  67.5 1.4 %copy-start.8 = (f32[39,32]{1,0:T(8,128)S(1)}, f32[39,32]{1,0:T(8,128)}, u32[]{:S(2)}) copy-start(f32[39,32]{1,0:T(8,128)} %get-tuple-element.16) | copy-start | bytes 14980
  67.5 2.2 %copy-start.9 = (f32[39,128]{1,0:T(8,128)S(1)}, f32[39,128]{1,0:T(8,128)}, u32[]{:S(2)}) copy-start(f32[39,128]{1,0:T(8,128)} %get-tuple-element.18) | copy-start | bytes 59908
  68.8 1.0 copy-start.10
  71.0 2.6 %copy-start.1 = (f32[12,32,128]{2,1,0:T(8,128)}, f32[12,32,128]{2,1,0:T(8,128)S(1)}, u32[]{:S(2)}) copy-start(f32[12,32,128]{2,1,0:T(8,128)S(1)} %get-tuple-element.35.p_ref) | copy-start | bytes 589828
  93.5 1.2 %copy-start.7 = (f32[4,36,128]{2,1,0:T(8,128)S(1)}, f32[4,36,128]{2,1,0:T(8,128)}, u32[]{:S(2)}) copy-start(f32[4,36,128]{2,1,0:T(8,128)} %get-tuple-element.20) | copy-start | bytes 221188

commit v16 on v15

--- a/solution.py
+++ b/solution.py
@@ -467,12 +467,12 @@
     packed = packed.reshape(step_count, lev_dev + 1, owner_count, cap)
     packed = jnp.transpose(packed, (2, 0, 1, 3))
     row_width = step_count * (lev_dev + 1) * cap
-    rows = jnp.pad(packed.reshape(owner_count, row_width), ((0, 0), (0, 128 - row_width)))
+    rows = packed.reshape(owner_count, row_width)
     early_part = jnp.concatenate(
         [jnp.sum(detrain_share[None] * adjoint_field, axis=1), detrain_part[None]], axis=0
     )
     arrived, early = exchange(rows, early_part, 0)
-    arrived = arrived[:, :row_width].reshape(owner_count, step_count, lev_dev + 1, cap)
+    arrived = arrived.reshape(owner_count, step_count, lev_dev + 1, cap)
     arrived = jnp.transpose(arrived, (1, 2, 0, 3)).reshape(
         step_count, lev_dev + 1, owner_count * cap
     )

time: 100 us -> 100 us (level)
  no operation moved by 1% of the time
where the time goes in v16:
time: 100 us; the launch traced here: 99.4 us
  Pallas kernels  73.3 us (73%)
  other arithmetic  12.9 us (13%)
  local copies, waits for them, and re-layouts  12 us (12%)
    pallas_call x1, Pallas kernels, exchange(): pl.pallas_call(functools.partial(exchange_body, lev_n, owners, lat_n), ou...  38.2 us
    pallas_call x1, Pallas kernels, mix_halo(): pl.pallas_call(functools.partial(mix_halo_body, lev_n, lon_n, lat_n), out...  18.1 us
    pallas_call x1, Pallas kernels, lev_direct(): pl.pallas_call(functools.partial(lev_direct_body, n), out_shape=jax.Shape...  8.92 us
    pallas_call x1, Pallas kernels, halo_swap(): pl.pallas_call(functools.partial(halo_body, lon_n, lat_n), out_shape=(jax...  8.14 us
    add x1, other arithmetic, on_device(): adjoint + upwind_east * (east_side - adjoint)  2.66 us

profile of v16, /device:TPU:1, one launch (start us, length us, event | category | flops | bytes accessed | tf_op | source)
XLA Modules:
  0.0 99.4 jit_solution(8852833147729479463)
XLA Ops:
  0.0 0.7 copy.122
  0.9 0.7 fusion.28
  1.8 0.7 iota_compare_fusion.4
  2.5 0.7 broadcast_select_fusion
  3.2 0.4 select_reduce_fusion
  3.6 0.4 reshape.212
  4.7 0.7 copy.69.rows_ref
  5.5 0.7 pad_maximum_fusion.part_ref
  6.2 38.2 %shard_map.100 = (f32[128,32]{1,0:T(8,128)}, f32[13,32,128]{2,1,0:T(8,128)}) custom-call(f32[128,32]{1,0:T(8,128)} %copy.69.rows_ref, f32[13,32,128]{2,1,0:T(8,128)} %pad_maximum_fusion.part_ref), custom_call_target="tpu_custom_call" | custom-call | tf_op jit(solution)/shard_map/pallas_call | solution.py:225
  44.5 0.9 copy.70
  45.6 0.3 reshape.202
  46.0 0.5 fusion.18
  46.5 0.6 multiply_reduce_fusion.2
  47.1 8.9 %shard_map.101 = f32[1,32,128]{2,1,0:T(8,128)} custom-call(f32[1,32,128]{2,1,0:T(8,128)} %bitcast.107), custom_call_target="tpu_custom_call" | custom-call | tf_op jit(solution)/shard_map/pallas_call | solution.py:267
  56.0 0.7 add_divide_fusion
  57.0 0.6 slice_reduce_fusion.2
  57.9 0.6 pad_maximum_fusion.3
  58.7 0.6 pad_maximum_fusion.5
  59.3 8.1 %shard_map.102 = (f32[39,32]{1,0:T(8,128)}, f32[39,32]{1,0:T(8,128)}, f32[39,128]{1,0:T(8,128)}, f32[39,128]{1,0:T(8,128)}) custom-call(f32[39,32]{1,0:T(8,128)} %get-tuple-element.67.col_last, f32[39,32]{1,0:T(8,128)} %get-tuple-element.68.col_first, f32[39,128]{1,0:T(8,128)} %get-tuple-element.69.row_last, f32[39,128]{1,0:T(8,128)} %get-tuple-element.70.row_first), custom_call_target="tpu_custom_call" | custom-call | tf_op jit(solution)/shard_map/pallas_call | solution.py:79
  67.5 1.3 %reshape.213 = f32[12,3,32,1]{3,2,1,0:T(8,128)S(1)} reshape(f32[36,32]{1,0:T(8,128)} %bitcast.116) | data formatting | bytes 9216 | tf_op jit(solution)/shard_map/reshape | solution.py:575
  68.8 0.6 reshape.214
  70.3 0.7 multiply_reduce_fusion
  71.0 0.6 slice_reduce_fusion.1
  72.5 0.7 pad_maximum_fusion.1.st_ref
  73.6 0.6 pad_maximum_fusion.2.pe_ref
  74.2 18.1 %shard_map.103 = (f32[12,32,128]{2,1,0:T(8,128)}, f32[4,36,128]{2,1,0:T(8,128)}) custom-call(f32[12,32,128]{2,1,0:T(8,128)} %copy-done.1, f32[3,12,128]{2,1,0:T(8,128)} %pad_maximum_fusion.2.pe_ref, f32[3,3,36,128]{3,2,1,0:T(8,128)} %pad_maximum_fusion.1.st_ref), custom_call_target="tpu_custom_call" | custom-call | tf_op jit(solution)/shard_map/pallas_call | solution.py:357
  92.3 0.9 broadcast_divide_fusion
  93.5 1.2 %fusion.32 = (f32[12,3,32,127]{3,2,1,0:T(8,128)}, f32[12,3,32,127]{3,2,1,0:T(8,128)}) fusion(f32[12,3,32,128]{3,2,1,0:T(8,128)S(1)} %multiply_add_fusion), kind=kLoop, calls=%fused_computation.119 | loop fusion | bytes 2340864 | tf_op jit(solution)/shard_map/slice | solution.py:578
  94.7 0.6 reshape_squeeze.40
  95.4 0.6 reshape_squeeze.41
  96.0 0.8 fusion.37
  96.8 2.7 %fusion.13 = f32[12,3,32,128]{3,2,1,0:T(8,128)} fusion(f32[12,3,32,1]{3,2,1,0:T(8,128)S(1)} %reshape_squeeze.40, f32[12,3,32,127]{3,2,1,0:T(8,128)} %get-tuple-element.40, f32[12,3,32,127]{3,2,1,0:T(8,128)} %get-tuple-element.39, f32[12,3,32,1]{3,2,1,0:T(8,128)S(1)} %reshape_squeeze.41, f32[12,3,1,128]{3,2,1,0:T(1,128)S(1)} %reshape_squeeze.38, ...), kind=kLoop, calls=%fused_computation.25 | loop fusion | flops 2801664 | bytes 4030464 | tf_op jit(solution)/shard_map/add | solution.py:587
  (109 shorter events, 4.2 us)
Async XLA Ops:
  1.8 2.4 %copy-start.12 = (s32[2,256]{1,0:T(2,128)S(1)}, s32[2,256]{1,0:T(2,128)}, u32[]{:S(2)}) copy-start(s32[2,256]{1,0:T(2,128)} %param.17) | copy-start | bytes 6148
  3.6 1.8 %copy-start = (f32[12,3,32,128]{3,2,1,0:T(8,128)S(1)}, f32[12,3,32,128]{3,2,1,0:T(8,128)}, u32[]{:S(2)}) copy-start(f32[12,3,32,128]{3,2,1,0:T(8,128)} %param.10) | copy-start | bytes 1769476
  3.6 1.8 %copy-start.3 = (f32[3,32,128]{2,1,0:T(8,128)S(1)}, f32[3,32,128]{2,1,0:T(8,128)}, u32[]{:S(2)}) copy-start(f32[3,32,128]{2,1,0:T(8,128)} %param.15) | copy-start | bytes 147460
  45.6 10.4 %copy-start.5 = (f32[13,32,128]{2,1,0:T(8,128)S(1)}, f32[13,32,128]{2,1,0:T(8,128)}, u32[]{:S(2)}) copy-start(f32[13,32,128]{2,1,0:T(8,128)} %get-tuple-element.14) | copy-start | bytes 638980
  46.0 10.8 %copy-start.2 = (f32[3,32,128]{2,1,0:T(8,128)S(1)}, f32[3,32,128]{2,1,0:T(8,128)}, u32[]{:S(2)}) copy-start(f32[3,32,128]{2,1,0:T(8,128)} %param.14) | copy-start | bytes 147460
  56.9 0.8 copy-start.4
  56.9 1.7 %copy-start.6 = (f32[3,32,128]{2,1,0:T(8,128)S(1)}, f32[3,32,128]{2,1,0:T(8,128)}, u32[]{:S(2)}) copy-start(f32[3,32,128]{2,1,0:T(8,128)} %param.12) | copy-start | bytes 147460
  56.9 1.7 %copy-start.11 = (f32[3,128]{1,0:T(4,128)S(1)}, f32[3,128]{1,0:T(4,128)}, u32[]{:S(2)}) copy-start(f32[3,128]{1,0:T(4,128)} %param.13) | copy-start | bytes 4612
  67.5 1.4 %copy-start.8 = (f32[39,32]{1,0:T(8,128)S(1)}, f32[39,32]{1,0:T(8,128)}, u32[]{:S(2)}) copy-start(f32[39,32]{1,0:T(8,128)} %get-tuple-element.16) | copy-start | bytes 14980
  67.5 2.2 %copy-start.9 = (f32[39,128]{1,0:T(8,128)S(1)}, f32[39,128]{1,0:T(8,128)}, u32[]{:S(2)}) copy-start(f32[39,128]{1,0:T(8,128)} %get-tuple-element.18) | copy-start | bytes 59908
  68.8 1.0 copy-start.10
  71.0 2.6 %copy-start.1 = (f32[12,32,128]{2,1,0:T(8,128)}, f32[12,32,128]{2,1,0:T(8,128)S(1)}, u32[]{:S(2)}) copy-start(f32[12,32,128]{2,1,0:T(8,128)S(1)} %get-tuple-element.35.p_ref) | copy-start | bytes 589828
  93.5 1.2 %copy-start.7 = (f32[4,36,128]{2,1,0:T(8,128)S(1)}, f32[4,36,128]{2,1,0:T(8,128)}, u32[]{:S(2)}) copy-start(f32[4,36,128]{2,1,0:T(8,128)} %get-tuple-element.20) | copy-start | bytes 221188
